TPU v7x, 32 devices: a whole 2x2x4 slice. The times are simulated.
32 devices in a mesh: groups: 2 (over y), gy: 16 (over z, x, core).
Axes of the slice: x: 2, y: 2, z: 4, core: 2. Of those that a mesh axis runs over, the one named last changes fastest.
Arguments:
- levels: bfloat16 [32, 75, 512], P(('groups', 'gy')), parts along dimension 0, may hold values from -6 to 6
- ocean: int32 [32, 512], P(('groups', 'gy')), parts along dimension 0, may hold values 0 or 1
- stem: bfloat16 [75, 128], replicated, may hold values from -0.75 to 0.75
- dw_kernel: float32 [2, 49, 128], replicated, may hold values from -0.875 to 0.875
- ln_gain: float32 [2, 128], replicated, may hold values from 0.25 to 1.75
- w_in: bfloat16 [2, 128, 512], replicated, may hold values from -0.5 to 0.5
- w_out: bfloat16 [2, 512, 128], replicated, may hold values from -0.25 to 0.25
- layer_scale: float32 [2, 128], replicated, may hold values from 0.3 to 1
- upstream: bfloat16 [32, 512, 128], P(('groups', 'gy')), parts along dimension 0, may hold values from -6 to 6
Outputs:
- result: bfloat16 [32, 512, 128], P(('groups', 'gy')), parts along dimension 0
- stem_gradient: float32 [150, 128], P('groups'), parts along dimension 0
- grad_kernel: float32 [4, 49, 128], P('groups'), parts along dimension 0
- grad_gain: float32 [4, 128], P('groups'), parts along dimension 0
- grad_w_in: float32 [4, 128, 512], P('groups'), parts along dimension 0
- grad_w_out: float32 [4, 512, 128], P('groups'), parts along dimension 0
- grad_scale: float32 [4, 128], P('groups'), parts along dimension 0
There are 2 independent parts, one for each index of `groups`. A program takes and returns all parts, laid end to end along the dimension named above; an argument that names none is the same for every part. Nothing has to cross between parts.
Inputs may be any that keep to these rules, and one draw needn't show every extreme that they name: 1 marks an ocean cell, 0 a land cell.
All inputs are finite; a program needn't handle non-finite values. No bound on the sum of `ocean` on one device may be relied on, other than what follows from the above.
Results may differ from a plain program's by a relative error of at most 0.0088.
Values may be sent and summed in bfloat16 or wider, within the bound.
No kernel may reach another device: no remote copies, remote signals or barrier semaphores. Data moves between devices by JAX's collectives and lax.ppermute only.
A program may use at most 64 MiB of HBM per device.

v0:
```python
import math

import jax
import jax.numpy as jnp
from jax import lax
from jax.sharding import PartitionSpec as P

LAYERS = 2
TH = 16
TW = 32
TX = 8


SQRT_TWO_PI = 0.7978845608028654
CUBIC_COEF = 0.044715
NORM_STABILIZER = 1e-06


def passed_along(value, axis, steps):
    count = lax.axis_size(axis)
    initial, last = (max(0, -steps), min(count, count - steps))
    return lax.ppermute(value, axis, [(source, source + steps) for source in range(initial, last)])


def gelu_tanh(values):
    inner_arg = SQRT_TWO_PI * (values + CUBIC_COEF * values * values * values)
    return 0.5 * values * (1.0 + jnp.tanh(inner_arg))


def gelu_slope(values):
    tangent = jnp.tanh(SQRT_TWO_PI * (values + CUBIC_COEF * values * values * values))
    return 0.5 * (1.0 + tangent) + 0.5 * values * (1.0 - tangent * tangent) * SQRT_TWO_PI * (
        1.0 + 3.0 * CUBIC_COEF * values * values
    )


def normalize(conv_out, gain_row):
    average = jnp.mean(conv_out, axis=-1, keepdims=True)
    centered = conv_out - average
    inverse_result = lax.rsqrt(
        jnp.mean(centered * centered, axis=-1, keepdims=True) + NORM_STABILIZER
    )
    scaled = centered * inverse_result
    return (scaled, inverse_result, (scaled * gain_row).astype(jnp.bfloat16))


def contract_rows(left_side, right_side):
    return lax.dot_general(
        left_side, right_side, (((0,), (0,)), ((), ())), preferred_element_type=jnp.float32
    )


def contract_cols(left_side, right_side):
    return lax.dot_general(
        left_side, right_side, (((1,), (1,)), ((), ())), preferred_element_type=jnp.float32
    )


def tile_move(strip_rows, offset):
    return passed_along(strip_rows, "gy", offset)


def mirror_partner(fold_rows, column):
    partner = jnp.zeros_like(fold_rows)
    for col_index in range(TX):
        moved = tile_move(fold_rows, 2 * col_index - (TX - 1))
        partner = jnp.where(column == col_index, moved, partner)
    return partner


def extend_tile(tile_field, column, is_top):
    west_cols = jnp.where(
        column == 0, tile_move(tile_field[:, -3:], 1 - TX), tile_move(tile_field[:, -3:], 1)
    )
    east_cols = jnp.where(
        column == TX - 1, tile_move(tile_field[:, :3], TX - 1), tile_move(tile_field[:, :3], -1)
    )
    widened = jnp.concatenate([west_cols, tile_field, east_cols], axis=1)
    south_rows = tile_move(widened[-3:], TX)
    upper_rows = tile_move(widened[:3], -TX)
    mirrored = mirror_partner(widened[-3:], column)[::-1, ::-1]
    north_rows = jnp.where(is_top, mirrored, upper_rows)
    return jnp.concatenate([south_rows, widened, north_rows], axis=0)


def depthwise(extended, kernel):
    total = jnp.zeros((TH, TW, kernel.shape[1]), jnp.float32)
    for row_tap in range(7):
        for col_tap in range(7):
            window = extended[row_tap : row_tap + TH, col_tap : col_tap + TW].astype(jnp.float32)
            total = total + kernel[row_tap * 7 + col_tap] * window
    return total


def kernel_grads(extended, grad_conv):
    kernel_rows = []
    for row_tap in range(7):
        for col_tap in range(7):
            window = extended[row_tap : row_tap + TH, col_tap : col_tap + TW].astype(jnp.float32)
            kernel_rows.append(jnp.sum(grad_conv * window, axis=(0, 1)))
    return jnp.stack(kernel_rows)


def flipped_transpose(grad_ext, kernel, is_top):
    ghost_rows = grad_ext[TH + 3 :]
    direct_result = jnp.concatenate(
        [grad_ext[: TH + 3], jnp.where(is_top, jnp.zeros_like(ghost_rows), ghost_rows)], axis=0
    )
    total = jnp.zeros((TH, TW, kernel.shape[1]), jnp.float32)
    for row_tap in range(7):
        for col_tap in range(7):
            window = direct_result[row_tap : row_tap + TH, col_tap : col_tap + TW].astype(
                jnp.float32
            )
            total = total + kernel[48 - (row_tap * 7 + col_tap)] * window
    fold_rows = jnp.where(is_top, ghost_rows, jnp.zeros_like(ghost_rows)).astype(jnp.float32)
    fold_block = jnp.concatenate(
        [jnp.zeros((6,) + fold_rows.shape[1:], jnp.float32), fold_rows], axis=0
    )
    folded_sum = jnp.zeros((3, TW, kernel.shape[1]), jnp.float32)
    for row_tap in range(7):
        for col_tap in range(7):
            folded_sum = (
                folded_sum
                + kernel[row_tap * 7 + col_tap]
                * fold_block[row_tap : row_tap + 3, col_tap : col_tap + TW]
            )
    return total.at[TH - 3 :].add(folded_sum)


def shards(levels, ocean, stem, dw_kernel, ln_gain, w_in, w_out, layer_scale, upstream):
    position = lax.axis_index("gy")
    column = position % TX
    is_top = position // TX == lax.axis_size("gy") // TX - 1
    cell_count = levels.shape[2]
    channels = stem.shape[1]
    land_mask = ocean[0].astype(jnp.float32)[:, None]
    embedded = contract_rows(levels[0], stem)
    stream_field = (land_mask * embedded).astype(jnp.bfloat16)
    saved = []
    for layer_index in range(LAYERS):
        extended = extend_tile(stream_field.reshape(TH, TW, channels), column, is_top)
        conv_out = depthwise(extended, dw_kernel[layer_index]).reshape(cell_count, channels)
        scaled, inverse_result, normed = normalize(conv_out, ln_gain[layer_index])
        hidden_pre = jnp.dot(normed, w_in[layer_index], preferred_element_type=jnp.float32)
        activated = gelu_tanh(hidden_pre).astype(jnp.bfloat16)
        branch = jnp.dot(activated, w_out[layer_index], preferred_element_type=jnp.float32)
        saved.append((extended, scaled, inverse_result, normed, hidden_pre, activated, branch))
        stream_field = (
            land_mask * (stream_field.astype(jnp.float32) + layer_scale[layer_index] * branch)
        ).astype(jnp.bfloat16)
    rescale = 1.0 / math.sqrt(lax.axis_size("gy") * cell_count)
    carried = upstream[0].astype(jnp.float32) * rescale
    layer_grads = [None] * LAYERS
    for layer_index in reversed(range(LAYERS)):
        extended, scaled, inverse_result, normed, hidden_pre, activated, branch = saved[layer_index]
        masked = land_mask * carried
        grad_scale = jnp.sum(masked * branch, axis=0)
        grad_branch = (masked * layer_scale[layer_index]).astype(jnp.bfloat16)
        grad_wout = contract_rows(activated, grad_branch)
        grad_pre = (contract_cols(grad_branch, w_out[layer_index]) * gelu_slope(hidden_pre)).astype(
            jnp.bfloat16
        )
        grad_win = contract_rows(normed, grad_pre)
        grad_normed = contract_cols(grad_pre, w_in[layer_index])
        grad_gain = jnp.sum(grad_normed * scaled, axis=0)
        grad_scaled = grad_normed * ln_gain[layer_index]
        grad_conv = inverse_result * (
            grad_scaled
            - jnp.mean(grad_scaled, axis=-1, keepdims=True)
            - scaled * jnp.mean(grad_scaled * scaled, axis=-1, keepdims=True)
        )
        rounded_half = lax.optimization_barrier(grad_conv.astype(jnp.bfloat16))
        rounded = rounded_half.astype(jnp.float32).reshape(TH, TW, channels)
        grad_kernel = kernel_grads(extended, rounded)
        grad_ext = extend_tile(rounded_half.reshape(TH, TW, channels), column, is_top)
        grad_input = flipped_transpose(grad_ext, dw_kernel[layer_index], is_top).reshape(
            cell_count, channels
        )
        carried = masked + grad_input
        terms = (grad_kernel, grad_gain, grad_win, grad_wout, grad_scale)
        layer_grads[layer_index] = terms
    stem_contribution = (land_mask * carried).astype(jnp.bfloat16)
    stem_gradient = jnp.dot(levels[0], stem_contribution, preferred_element_type=jnp.float32)
    kernel_stack = jnp.stack([layer_grads[layer_index][0] for layer_index in range(LAYERS)])
    gain_stack = jnp.stack([layer_grads[layer_index][1] for layer_index in range(LAYERS)])
    win_stack = jnp.stack([layer_grads[layer_index][2] for layer_index in range(LAYERS)])
    wout_stack = jnp.stack([layer_grads[layer_index][3] for layer_index in range(LAYERS)])
    scale_stack = jnp.stack([layer_grads[layer_index][4] for layer_index in range(LAYERS)])
    stem_gradient, kernel_stack, gain_stack, win_stack, wout_stack, scale_stack = lax.psum(
        (stem_gradient, kernel_stack, gain_stack, win_stack, wout_stack, scale_stack), "gy"
    )
    return (
        stream_field[None],
        stem_gradient,
        kernel_stack,
        gain_stack,
        win_stack,
        wout_stack,
        scale_stack,
    )


def solution(mesh):
    in_specs = (
        P(("groups", "gy"), None, None),
        P(("groups", "gy"), None),
        P(),
        P(),
        P(),
        P(),
        P(),
        P(),
        P(("groups", "gy"), None, None),
    )
    out_specs = (
        P(("groups", "gy"), None, None),
        P("groups", None),
        P("groups", None, None),
        P("groups", None),
        P("groups", None, None),
        P("groups", None, None),
        P("groups", None),
    )
    return jax.shard_map(shards, mesh=mesh, in_specs=in_specs, out_specs=out_specs, check_vma=False)
```

profile of v0, /device:TPU:0, one launch (start us, length us, event | category | flops | bytes accessed | tf_op | source)
XLA Modules:
  0.0 432.7 jit_solution(554958904832869838)
XLA Ops:
  9.0 1.3 collective-permute-start
  10.3 2.4 collective-permute-start.1
  12.7 7.3 %collective-permute-start.2 = (bf16[16,3,128]{2,1,0:T(4,128)(2,1)S(1)}, bf16[16,3,128]{2,1,0:T(4,128)(2,1)S(1)}, u32[]{:S(2)}, u32[]{:S(2)}) collective-permute-start(bf16[16,3,128]{2,1,0:T(4,128)(2,1)S(1)} %get-tuple-element.208), channel_id=1, source_target_pairs={{0,7},{1,8},{2,9},{3,10},{4,11},{5,12},{6,13},{7,14},{8,15},{16,23... | collective-permute-start | bytes 36872 | tf_op jit(solution)/shard_map/ppermute | solution.py:22
  20.0 1.3 collective-permute-start.3
  25.6 1.3 collective-permute-start.10
  26.9 1.3 collective-permute-start.11
  28.2 1.3 collective-permute-start.12
  30.1 7.6 %collective-permute-start.5 = (bf16[3,38,128]{2,1,0:T(8,128)(2,1)S(1)}, bf16[3,38,128]{2,1,0:T(8,128)(2,1)S(1)}, u32[]{:S(2)}, u32[]{:S(2)}) collective-permute-start(bf16[3,38,128]{2,1,0:T(8,128)(2,1)S(1)} %get-tuple-element.199), channel_id=1, source_target_pairs={{0,7},{1,8},{2,9},{3,10},{4,11},{5,12},{6,13},{7,14},{8,15},{16,23... | collective-permute-start | bytes 87560 | tf_op jit(solution)/shard_map/ppermute | solution.py:22
  37.7 4.5 %collective-permute-start.6 = (bf16[3,38,128]{2,1,0:T(8,128)(2,1)S(1)}, bf16[3,38,128]{2,1,0:T(8,128)(2,1)S(1)}, u32[]{:S(2)}, u32[]{:S(2)}) collective-permute-start(bf16[3,38,128]{2,1,0:T(8,128)(2,1)S(1)} %get-tuple-element.199), channel_id=1, source_target_pairs={{0,5},{1,6},{2,7},{3,8},{4,9},{5,10},{6,11},{7,12},{8,13},{9,14},{... | collective-permute-start | bytes 87560 | tf_op jit(solution)/shard_map/ppermute | solution.py:22
  42.2 3.7 collective-permute-start.7
  47.2 1.3 collective-permute-start.9
  49.1 4.6 %collective-permute-start.4 = (bf16[3,38,128]{2,1,0:T(8,128)(2,1)S(1)}, bf16[3,38,128]{2,1,0:T(8,128)(2,1)S(1)}, u32[]{:S(2)}, u32[]{:S(2)}) collective-permute-start(bf16[3,38,128]{2,1,0:T(8,128)(2,1)S(1)} %get-tuple-element.199), channel_id=1, source_target_pairs={{0,8},{1,9},{2,10},{3,11},{4,12},{5,13},{6,14},{7,15},{16,24},{17,... | collective-permute-start | bytes 87560 | tf_op jit(solution)/shard_map/ppermute | solution.py:22
  53.7 1.3 collective-permute-start.13
  55.1 5.3 %collective-permute-done.13 = bf16[3,38,128]{2,1,0:T(8,128)(2,1)S(1)} collective-permute-done((bf16[3,38,128]{2,1,0:T(8,128)(2,1)S(1)}, bf16[3,38,128]{2,1,0:T(8,128)(2,1)S(1)}, u32[]{:S(2)}, u32[]{:S(2)}) %collective-permute-start.13) | collective-permute-done | bytes 29216 | tf_op jit(solution)/shard_map/ppermute | solution.py:22
  60.7 2.7 fusion.337
  65.6 1.8 fusion.14
  67.5 1.3 collective-permute-start.14
  70.1 5.8 %collective-permute-start.16 = (bf16[16,3,128]{2,1,0:T(4,128)(2,1)S(1)}, bf16[16,3,128]{2,1,0:T(4,128)(2,1)S(1)}, u32[]{:S(2)}, u32[]{:S(2)}) collective-permute-start(bf16[16,3,128]{2,1,0:T(4,128)(2,1)S(1)} %get-tuple-element.206), channel_id=1, source_target_pairs={{0,7},{1,8},{2,9},{3,10},{4,11},{5,12},{6,13},{7,14},{8,15},{16,23... | collective-permute-start | bytes 36872 | tf_op jit(solution)/shard_map/ppermute | solution.py:22
  75.9 1.3 collective-permute-start.17
  77.3 1.7 collective-permute-done.17
  79.0 4.8 %collective-permute-start.19 = (bf16[3,38,128]{2,1,0:T(8,128)(2,1)S(1)}, bf16[3,38,128]{2,1,0:T(8,128)(2,1)S(1)}, u32[]{:S(2)}, u32[]{:S(2)}) collective-permute-start(bf16[3,38,128]{2,1,0:T(8,128)(2,1)S(1)} %get-tuple-element.195), channel_id=1, source_target_pairs={{0,7},{1,8},{2,9},{3,10},{4,11},{5,12},{6,13},{7,14},{8,15},{16,23... | collective-permute-start | bytes 87560 | tf_op jit(solution)/shard_map/ppermute | solution.py:22
  85.1 2.6 collective-permute-start.21
  89.6 1.3 collective-permute-start.23
  90.9 1.3 collective-permute-start.24
  92.2 1.3 collective-permute-start.25
  93.5 1.3 collective-permute-start.26
  95.6 9.1 %collective-permute-start.18 = (bf16[3,38,128]{2,1,0:T(8,128)(2,1)S(1)}, bf16[3,38,128]{2,1,0:T(8,128)(2,1)S(1)}, u32[]{:S(2)}, u32[]{:S(2)}) collective-permute-start(bf16[3,38,128]{2,1,0:T(8,128)(2,1)S(1)} %get-tuple-element.195), channel_id=1, source_target_pairs={{0,8},{1,9},{2,10},{3,11},{4,12},{5,13},{6,14},{7,15},{16,24},{17,... | collective-permute-start | bytes 87560 | tf_op jit(solution)/shard_map/ppermute | solution.py:22
  104.7 1.3 collective-permute-start.27
  106.1 5.3 %collective-permute-done.27 = bf16[3,38,128]{2,1,0:T(8,128)(2,1)S(1)} collective-permute-done((bf16[3,38,128]{2,1,0:T(8,128)(2,1)S(1)}, bf16[3,38,128]{2,1,0:T(8,128)(2,1)S(1)}, u32[]{:S(2)}, u32[]{:S(2)}) %collective-permute-start.27) | collective-permute-done | bytes 29216 | tf_op jit(solution)/shard_map/ppermute | solution.py:22
  111.7 2.7 fusion.335
  116.1 1.5 fusion
  118.9 1.3 collective-permute-start.28
  121.5 5.8 %collective-permute-start.30 = (bf16[16,3,128]{2,1,0:T(4,128)(2,1)S(1)}, bf16[16,3,128]{2,1,0:T(4,128)(2,1)S(1)}, u32[]{:S(2)}, u32[]{:S(2)}) collective-permute-start(bf16[16,3,128]{2,1,0:T(4,128)(2,1)S(1)} %get-tuple-element.204), channel_id=1, source_target_pairs={{0,7},{1,8},{2,9},{3,10},{4,11},{5,12},{6,13},{7,14},{8,15},{16,23... | collective-permute-start | bytes 36872 | tf_op jit(solution)/shard_map/ppermute | solution.py:22
  127.3 1.5 collective-permute-start.31
  132.2 6.7 %collective-permute-start.33 = (bf16[3,38,128]{2,1,0:T(8,128)(2,1)S(1)}, bf16[3,38,128]{2,1,0:T(8,128)(2,1)S(1)}, u32[]{:S(2)}, u32[]{:S(2)}) collective-permute-start(bf16[3,38,128]{2,1,0:T(8,128)(2,1)S(1)} %get-tuple-element.191), channel_id=1, source_target_pairs={{0,7},{1,8},{2,9},{3,10},{4,11},{5,12},{6,13},{7,14},{8,15},{16,23... | collective-permute-start | bytes 87560 | tf_op jit(solution)/shard_map/ppermute | solution.py:22
  140.2 2.2 collective-permute-start.35
  142.5 1.9 convolution_bitcast_fusion
  144.4 1.7 collective-permute-start.36
  146.1 1.3 collective-permute-start.37
  147.4 1.3 collective-permute-start.38
  148.7 1.3 collective-permute-start.39
  150.0 1.3 collective-permute-start.40
  151.5 9.1 %collective-permute-start.32 = (bf16[3,38,128]{2,1,0:T(8,128)(2,1)S(1)}, bf16[3,38,128]{2,1,0:T(8,128)(2,1)S(1)}, u32[]{:S(2)}, u32[]{:S(2)}) collective-permute-start(bf16[3,38,128]{2,1,0:T(8,128)(2,1)S(1)} %get-tuple-element.191), channel_id=1, source_target_pairs={{0,8},{1,9},{2,10},{3,11},{4,12},{5,13},{6,14},{7,15},{16,24},{17,... | collective-permute-start | bytes 87560 | tf_op jit(solution)/shard_map/ppermute | solution.py:22
  160.7 1.3 collective-permute-start.41
  162.1 5.3 %collective-permute-done.41 = bf16[3,38,128]{2,1,0:T(8,128)(2,1)S(1)} collective-permute-done((bf16[3,38,128]{2,1,0:T(8,128)(2,1)S(1)}, bf16[3,38,128]{2,1,0:T(8,128)(2,1)S(1)}, u32[]{:S(2)}, u32[]{:S(2)}) %collective-permute-start.41) | collective-permute-done | bytes 29216 | tf_op jit(solution)/shard_map/ppermute | solution.py:22
  168.3 2.5 multiply_add_fusion.3
  173.9 1.6 multiply_reduce_fusion.3
  178.2 1.3 collective-permute-start.42
  180.8 5.8 %collective-permute-start.44 = (bf16[16,3,128]{2,1,0:T(4,128)(2,1)S(1)}, bf16[16,3,128]{2,1,0:T(4,128)(2,1)S(1)}, u32[]{:S(2)}, u32[]{:S(2)}) collective-permute-start(bf16[16,3,128]{2,1,0:T(4,128)(2,1)S(1)} %get-tuple-element.202), channel_id=1, source_target_pairs={{0,7},{1,8},{2,9},{3,10},{4,11},{5,12},{6,13},{7,14},{8,15},{16,23... | collective-permute-start | bytes 36872 | tf_op jit(solution)/shard_map/ppermute | solution.py:22
  186.6 1.3 collective-permute-start.45
  187.9 1.9 multiply_reduce_fusion.1
  193.3 2.1 stack.445
  196.2 6.7 %collective-permute-start.47 = (bf16[3,38,128]{2,1,0:T(8,128)(2,1)S(1)}, bf16[3,38,128]{2,1,0:T(8,128)(2,1)S(1)}, u32[]{:S(2)}, u32[]{:S(2)}) collective-permute-start(bf16[3,38,128]{2,1,0:T(8,128)(2,1)S(1)} %get-tuple-element.187), channel_id=1, source_target_pairs={{0,7},{1,8},{2,9},{3,10},{4,11},{5,12},{6,13},{7,14},{8,15},{16,23... | collective-permute-start | bytes 87560 | tf_op jit(solution)/shard_map/ppermute | solution.py:22
  204.2 2.2 collective-permute-start.49
  207.0 1.6 collective-permute-start.50
  211.2 1.3 collective-permute-start.53
  215.1 9.1 %collective-permute-start.46 = (bf16[3,38,128]{2,1,0:T(8,128)(2,1)S(1)}, bf16[3,38,128]{2,1,0:T(8,128)(2,1)S(1)}, u32[]{:S(2)}, u32[]{:S(2)}) collective-permute-start(bf16[3,38,128]{2,1,0:T(8,128)(2,1)S(1)} %get-tuple-element.187), channel_id=1, source_target_pairs={{0,8},{1,9},{2,10},{3,11},{4,12},{5,13},{6,14},{7,15},{16,24},{17,... | collective-permute-start | bytes 87560 | tf_op jit(solution)/shard_map/ppermute | solution.py:22
  224.2 1.5 collective-permute-start.55
  225.8 5.0 %collective-permute-done.55 = bf16[3,38,128]{2,1,0:T(8,128)(2,1)S(1)} collective-permute-done((bf16[3,38,128]{2,1,0:T(8,128)(2,1)S(1)}, bf16[3,38,128]{2,1,0:T(8,128)(2,1)S(1)}, u32[]{:S(2)}, u32[]{:S(2)}) %collective-permute-start.55) | collective-permute-done | bytes 29216 | tf_op jit(solution)/shard_map/ppermute | solution.py:22
  231.8 2.5 multiply_add_fusion.2
  237.0 84.7 %all-reduce.7.cloned.1.call-done = (f32[75,128]{1,0:T(8,128)}, f32[2,49,128]{2,1,0:T(8,128)}, f32[2,128]{1,0:T(2,128)}, f32[2,128]{1,0:T(2,128)}) async-done(((f32[75,128]{1,0:T(8,128)}, f32[2,49,128]{2,1,0:T(8,128)}, f32[2,128]{1,0:T(2,128)}, f32[2,128]{1,0:T(2,128)}), (f32[75,128]{1,0:T(8,128)}, f32[2,49,128]{2,1,0:T(8,128)}, f32[2,128]{1,0:T(2,128)}, f32[2,128]{1,0:T(2,128)})) %all-reduce.7.cloned.1.call-update) | async-done | bytes 90640 | tf_op jit(solution)/shard_map/psum | solution.py:190
  321.7 1.5 copy.20
  323.1 98.2 %all-reduce.9.cloned.1.call-done = (f32[2,128,512]{2,1,0:T(8,128)}, f32[2,512,128]{2,1,0:T(8,128)}) async-done(((f32[2,128,512]{2,1,0:T(8,128)}, f32[2,512,128]{2,1,0:T(8,128)}), (f32[2,128,512]{2,1,0:T(8,128)}, f32[2,512,128]{2,1,0:T(8,128)})) %all-reduce.9.cloned.1.call-update) | async-done | bytes 1048592 | tf_op jit(solution)/shard_map/psum | solution.py:190
  422.6 1.9 copy.33
  (444 shorter events, 50.1 us)
Async XLA Ops:
  7.2 314.5 %all-reduce.7.cloned.1.call-start = ((), (), s32[]{:S(2)}) async-start(), calls=%async_computation | async-start | bytes 200704 | tf_op jit(solution)/shard_map/psum | solution.py:190
  9.0 16.5 %collective-permute-start = (bf16[16,3,128]{2,1,0:T(4,128)(2,1)S(1)}, bf16[16,3,128]{2,1,0:T(4,128)(2,1)S(1)}, u32[]{:S(2)}, u32[]{:S(2)}) collective-permute-start(bf16[16,3,128]{2,1,0:T(4,128)(2,1)S(1)} %get-tuple-element.207), channel_id=1, source_target_pairs={{7,0},{8,1},{9,2},{10,3},{11,4},{12,5},{13,6},{14,7},{15,8},{23,16... | collective-permute-start | bytes 36872 | tf_op jit(solution)/shard_map/ppermute | solution.py:22
  10.3 15.2 %collective-permute-start.1 = (bf16[16,3,128]{2,1,0:T(4,128)(2,1)S(1)}, bf16[16,3,128]{2,1,0:T(4,128)(2,1)S(1)}, u32[]{:S(2)}, u32[]{:S(2)}) collective-permute-start(bf16[16,3,128]{2,1,0:T(4,128)(2,1)S(1)} %get-tuple-element.207), channel_id=1, source_target_pairs={{0,1},{1,2},{2,3},{3,4},{4,5},{5,6},{6,7},{7,8},{8,9},{9,10},{10,1... | collective-permute-start | bytes 36872 | tf_op jit(solution)/shard_map/ppermute | solution.py:22
  12.7 12.8 %collective-permute-start.2 = (bf16[16,3,128]{2,1,0:T(4,128)(2,1)S(1)}, bf16[16,3,128]{2,1,0:T(4,128)(2,1)S(1)}, u32[]{:S(2)}, u32[]{:S(2)}) collective-permute-start(bf16[16,3,128]{2,1,0:T(4,128)(2,1)S(1)} %get-tuple-element.208), channel_id=1, source_target_pairs={{0,7},{1,8},{2,9},{3,10},{4,11},{5,12},{6,13},{7,14},{8,15},{16,23... | collective-permute-start | bytes 36872 | tf_op jit(solution)/shard_map/ppermute | solution.py:22
  20.0 5.5 %collective-permute-start.3 = (bf16[16,3,128]{2,1,0:T(4,128)(2,1)S(1)}, bf16[16,3,128]{2,1,0:T(4,128)(2,1)S(1)}, u32[]{:S(2)}, u32[]{:S(2)}) collective-permute-start(bf16[16,3,128]{2,1,0:T(4,128)(2,1)S(1)} %get-tuple-element.208), channel_id=1, source_target_pairs={{1,0},{2,1},{3,2},{4,3},{5,4},{6,5},{7,6},{8,7},{9,8},{10,9},{11,1... | collective-permute-start | bytes 36872 | tf_op jit(solution)/shard_map/ppermute | solution.py:22
  22.7 88.8 %copy-start.50 = (f32[128]{0:T(128)}, f32[128]{0:T(128)S(1)}, u32[]{:S(2)}) copy-start(f32[128]{0:T(128)S(1)} %get-tuple-element.270) | copy-start | bytes 1540
  23.4 88.1 %copy-start.52 = (f32[128]{0:T(128)}, f32[128]{0:T(128)S(1)}, u32[]{:S(2)}) copy-start(f32[128]{0:T(128)S(1)} %get-tuple-element.289) | copy-start | bytes 1540
  24.0 87.6 %copy-start.62 = (f32[128]{0:T(128)}, f32[128]{0:T(128)S(1)}, u32[]{:S(2)}) copy-start(f32[128]{0:T(128)S(1)} %get-tuple-element.218) | copy-start | bytes 1540
  24.0 87.6 %copy-start.64 = (f32[128]{0:T(128)}, f32[128]{0:T(128)S(1)}, u32[]{:S(2)}) copy-start(f32[128]{0:T(128)S(1)} %get-tuple-element.219) | copy-start | bytes 1540
  24.0 87.6 %copy-start.66 = (f32[128]{0:T(128)}, f32[128]{0:T(128)S(1)}, u32[]{:S(2)}) copy-start(f32[128]{0:T(128)S(1)} %get-tuple-element.220) | copy-start | bytes 1540
  25.6 16.5 %collective-permute-start.10 = (bf16[3,38,128]{2,1,0:T(8,128)(2,1)S(1)}, bf16[3,38,128]{2,1,0:T(8,128)(2,1)S(1)}, u32[]{:S(2)}, u32[]{:S(2)}) collective-permute-start(bf16[3,38,128]{2,1,0:T(8,128)(2,1)S(1)} %get-tuple-element.199), channel_id=1, source_target_pairs={{3,0},{4,1},{5,2},{6,3},{7,4},{8,5},{9,6},{10,7},{11,8},{12,9},{13... | collective-permute-start | bytes 87560 | tf_op jit(solution)/shard_map/ppermute | solution.py:22
  26.9 19.0 %collective-permute-start.11 = (bf16[3,38,128]{2,1,0:T(8,128)(2,1)S(1)}, bf16[3,38,128]{2,1,0:T(8,128)(2,1)S(1)}, u32[]{:S(2)}, u32[]{:S(2)}) collective-permute-start(bf16[3,38,128]{2,1,0:T(8,128)(2,1)S(1)} %get-tuple-element.199), channel_id=1, source_target_pairs={{5,0},{6,1},{7,2},{8,3},{9,4},{10,5},{11,6},{12,7},{13,8},{14,9},{... | collective-permute-start | bytes 87560 | tf_op jit(solution)/shard_map/ppermute | solution.py:22
  28.2 19.0 %collective-permute-start.12 = (bf16[3,38,128]{2,1,0:T(8,128)(2,1)S(1)}, bf16[3,38,128]{2,1,0:T(8,128)(2,1)S(1)}, u32[]{:S(2)}, u32[]{:S(2)}) collective-permute-start(bf16[3,38,128]{2,1,0:T(8,128)(2,1)S(1)} %get-tuple-element.199), channel_id=1, source_target_pairs={{7,0},{8,1},{9,2},{10,3},{11,4},{12,5},{13,6},{14,7},{15,8},{23,16... | collective-permute-start | bytes 87560 | tf_op jit(solution)/shard_map/ppermute | solution.py:22
  30.1 18.9 %collective-permute-start.5 = (bf16[3,38,128]{2,1,0:T(8,128)(2,1)S(1)}, bf16[3,38,128]{2,1,0:T(8,128)(2,1)S(1)}, u32[]{:S(2)}, u32[]{:S(2)}) collective-permute-start(bf16[3,38,128]{2,1,0:T(8,128)(2,1)S(1)} %get-tuple-element.199), channel_id=1, source_target_pairs={{0,7},{1,8},{2,9},{3,10},{4,11},{5,12},{6,13},{7,14},{8,15},{16,23... | collective-permute-start | bytes 87560 | tf_op jit(solution)/shard_map/ppermute | solution.py:22
  37.7 16.0 %collective-permute-start.6 = (bf16[3,38,128]{2,1,0:T(8,128)(2,1)S(1)}, bf16[3,38,128]{2,1,0:T(8,128)(2,1)S(1)}, u32[]{:S(2)}, u32[]{:S(2)}) collective-permute-start(bf16[3,38,128]{2,1,0:T(8,128)(2,1)S(1)} %get-tuple-element.199), channel_id=1, source_target_pairs={{0,5},{1,6},{2,7},{3,8},{4,9},{5,10},{6,11},{7,12},{8,13},{9,14},{... | collective-permute-start | bytes 87560 | tf_op jit(solution)/shard_map/ppermute | solution.py:22
  42.2 12.8 %collective-permute-start.7 = (bf16[3,38,128]{2,1,0:T(8,128)(2,1)S(1)}, bf16[3,38,128]{2,1,0:T(8,128)(2,1)S(1)}, u32[]{:S(2)}, u32[]{:S(2)}) collective-permute-start(bf16[3,38,128]{2,1,0:T(8,128)(2,1)S(1)} %get-tuple-element.199), channel_id=1, source_target_pairs={{0,3},{1,4},{2,5},{3,6},{4,7},{5,8},{6,9},{7,10},{8,11},{9,12},{10... | collective-permute-start | bytes 87560 | tf_op jit(solution)/shard_map/ppermute | solution.py:22
  45.9 9.1 %collective-permute-start.8 = (bf16[3,38,128]{2,1,0:T(8,128)(2,1)S(1)}, bf16[3,38,128]{2,1,0:T(8,128)(2,1)S(1)}, u32[]{:S(2)}, u32[]{:S(2)}) collective-permute-start(bf16[3,38,128]{2,1,0:T(8,128)(2,1)S(1)} %get-tuple-element.199), channel_id=1, source_target_pairs={{0,1},{1,2},{2,3},{3,4},{4,5},{5,6},{6,7},{7,8},{8,9},{9,10},{10,1... | collective-permute-start | bytes 87560 | tf_op jit(solution)/shard_map/ppermute | solution.py:22
  47.2 7.8 %collective-permute-start.9 = (bf16[3,38,128]{2,1,0:T(8,128)(2,1)S(1)}, bf16[3,38,128]{2,1,0:T(8,128)(2,1)S(1)}, u32[]{:S(2)}, u32[]{:S(2)}) collective-permute-start(bf16[3,38,128]{2,1,0:T(8,128)(2,1)S(1)} %get-tuple-element.199), channel_id=1, source_target_pairs={{1,0},{2,1},{3,2},{4,3},{5,4},{6,5},{7,6},{8,7},{9,8},{10,9},{11,1... | collective-permute-start | bytes 87560 | tf_op jit(solution)/shard_map/ppermute | solution.py:22
  49.1 11.3 %collective-permute-start.4 = (bf16[3,38,128]{2,1,0:T(8,128)(2,1)S(1)}, bf16[3,38,128]{2,1,0:T(8,128)(2,1)S(1)}, u32[]{:S(2)}, u32[]{:S(2)}) collective-permute-start(bf16[3,38,128]{2,1,0:T(8,128)(2,1)S(1)} %get-tuple-element.199), channel_id=1, source_target_pairs={{0,8},{1,9},{2,10},{3,11},{4,12},{5,13},{6,14},{7,15},{16,24},{17,... | collective-permute-start | bytes 87560 | tf_op jit(solution)/shard_map/ppermute | solution.py:22
  53.7 6.7 %collective-permute-start.13 = (bf16[3,38,128]{2,1,0:T(8,128)(2,1)S(1)}, bf16[3,38,128]{2,1,0:T(8,128)(2,1)S(1)}, u32[]{:S(2)}, u32[]{:S(2)}) collective-permute-start(bf16[3,38,128]{2,1,0:T(8,128)(2,1)S(1)} %get-tuple-element.198), channel_id=1, source_target_pairs={{8,0},{9,1},{10,2},{11,3},{12,4},{13,5},{14,6},{15,7},{24,16},{25,... | collective-permute-start | bytes 87560 | tf_op jit(solution)/shard_map/ppermute | solution.py:22
  67.5 9.7 %collective-permute-start.14 = (bf16[16,3,128]{2,1,0:T(4,128)(2,1)S(1)}, bf16[16,3,128]{2,1,0:T(4,128)(2,1)S(1)}, u32[]{:S(2)}, u32[]{:S(2)}) collective-permute-start(bf16[16,3,128]{2,1,0:T(4,128)(2,1)S(1)} %get-tuple-element.205), channel_id=1, source_target_pairs={{7,0},{8,1},{9,2},{10,3},{11,4},{12,5},{13,6},{14,7},{15,8},{23,16... | collective-permute-start | bytes 36872 | tf_op jit(solution)/shard_map/ppermute | solution.py:22
  68.8 8.4 %collective-permute-start.15 = (bf16[16,3,128]{2,1,0:T(4,128)(2,1)S(1)}, bf16[16,3,128]{2,1,0:T(4,128)(2,1)S(1)}, u32[]{:S(2)}, u32[]{:S(2)}) collective-permute-start(bf16[16,3,128]{2,1,0:T(4,128)(2,1)S(1)} %get-tuple-element.205), channel_id=1, source_target_pairs={{0,1},{1,2},{2,3},{3,4},{4,5},{5,6},{6,7},{7,8},{8,9},{9,10},{10,1... | collective-permute-start | bytes 36872 | tf_op jit(solution)/shard_map/ppermute | solution.py:22
  70.1 7.2 %collective-permute-start.16 = (bf16[16,3,128]{2,1,0:T(4,128)(2,1)S(1)}, bf16[16,3,128]{2,1,0:T(4,128)(2,1)S(1)}, u32[]{:S(2)}, u32[]{:S(2)}) collective-permute-start(bf16[16,3,128]{2,1,0:T(4,128)(2,1)S(1)} %get-tuple-element.206), channel_id=1, source_target_pairs={{0,7},{1,8},{2,9},{3,10},{4,11},{5,12},{6,13},{7,14},{8,15},{16,23... | collective-permute-start | bytes 36872 | tf_op jit(solution)/shard_map/ppermute | solution.py:22
  75.9 3.1 collective-permute-start.17
  79.0 11.8 %collective-permute-start.19 = (bf16[3,38,128]{2,1,0:T(8,128)(2,1)S(1)}, bf16[3,38,128]{2,1,0:T(8,128)(2,1)S(1)}, u32[]{:S(2)}, u32[]{:S(2)}) collective-permute-start(bf16[3,38,128]{2,1,0:T(8,128)(2,1)S(1)} %get-tuple-element.195), channel_id=1, source_target_pairs={{0,7},{1,8},{2,9},{3,10},{4,11},{5,12},{6,13},{7,14},{8,15},{16,23... | collective-permute-start | bytes 87560 | tf_op jit(solution)/shard_map/ppermute | solution.py:22
  83.8 8.3 %collective-permute-start.20 = (bf16[3,38,128]{2,1,0:T(8,128)(2,1)S(1)}, bf16[3,38,128]{2,1,0:T(8,128)(2,1)S(1)}, u32[]{:S(2)}, u32[]{:S(2)}) collective-permute-start(bf16[3,38,128]{2,1,0:T(8,128)(2,1)S(1)} %get-tuple-element.195), channel_id=1, source_target_pairs={{0,5},{1,6},{2,7},{3,8},{4,9},{5,10},{6,11},{7,12},{8,13},{9,14},{... | collective-permute-start | bytes 87560 | tf_op jit(solution)/shard_map/ppermute | solution.py:22
  85.1 8.4 %collective-permute-start.21 = (bf16[3,38,128]{2,1,0:T(8,128)(2,1)S(1)}, bf16[3,38,128]{2,1,0:T(8,128)(2,1)S(1)}, u32[]{:S(2)}, u32[]{:S(2)}) collective-permute-start(bf16[3,38,128]{2,1,0:T(8,128)(2,1)S(1)} %get-tuple-element.195), channel_id=1, source_target_pairs={{0,3},{1,4},{2,5},{3,6},{4,7},{5,8},{6,9},{7,10},{8,11},{9,12},{10... | collective-permute-start | bytes 87560 | tf_op jit(solution)/shard_map/ppermute | solution.py:22
  88.3 7.3 %collective-permute-start.22 = (bf16[3,38,128]{2,1,0:T(8,128)(2,1)S(1)}, bf16[3,38,128]{2,1,0:T(8,128)(2,1)S(1)}, u32[]{:S(2)}, u32[]{:S(2)}) collective-permute-start(bf16[3,38,128]{2,1,0:T(8,128)(2,1)S(1)} %get-tuple-element.195), channel_id=1, source_target_pairs={{0,1},{1,2},{2,3},{3,4},{4,5},{5,6},{6,7},{7,8},{8,9},{9,10},{10,1... | collective-permute-start | bytes 87560 | tf_op jit(solution)/shard_map/ppermute | solution.py:22
  89.6 15.1 %collective-permute-start.23 = (bf16[3,38,128]{2,1,0:T(8,128)(2,1)S(1)}, bf16[3,38,128]{2,1,0:T(8,128)(2,1)S(1)}, u32[]{:S(2)}, u32[]{:S(2)}) collective-permute-start(bf16[3,38,128]{2,1,0:T(8,128)(2,1)S(1)} %get-tuple-element.195), channel_id=1, source_target_pairs={{1,0},{2,1},{3,2},{4,3},{5,4},{6,5},{7,6},{8,7},{9,8},{10,9},{11,1... | collective-permute-start | bytes 87560 | tf_op jit(solution)/shard_map/ppermute | solution.py:22
  90.9 15.1 %collective-permute-start.24 = (bf16[3,38,128]{2,1,0:T(8,128)(2,1)S(1)}, bf16[3,38,128]{2,1,0:T(8,128)(2,1)S(1)}, u32[]{:S(2)}, u32[]{:S(2)}) collective-permute-start(bf16[3,38,128]{2,1,0:T(8,128)(2,1)S(1)} %get-tuple-element.195), channel_id=1, source_target_pairs={{3,0},{4,1},{5,2},{6,3},{7,4},{8,5},{9,6},{10,7},{11,8},{12,9},{13... | collective-permute-start | bytes 87560 | tf_op jit(solution)/shard_map/ppermute | solution.py:22
  92.2 13.8 %collective-permute-start.25 = (bf16[3,38,128]{2,1,0:T(8,128)(2,1)S(1)}, bf16[3,38,128]{2,1,0:T(8,128)(2,1)S(1)}, u32[]{:S(2)}, u32[]{:S(2)}) collective-permute-start(bf16[3,38,128]{2,1,0:T(8,128)(2,1)S(1)} %get-tuple-element.195), channel_id=1, source_target_pairs={{5,0},{6,1},{7,2},{8,3},{9,4},{10,5},{11,6},{12,7},{13,8},{14,9},{... | collective-permute-start | bytes 87560 | tf_op jit(solution)/shard_map/ppermute | solution.py:22
  93.5 12.5 %collective-permute-start.26 = (bf16[3,38,128]{2,1,0:T(8,128)(2,1)S(1)}, bf16[3,38,128]{2,1,0:T(8,128)(2,1)S(1)}, u32[]{:S(2)}, u32[]{:S(2)}) collective-permute-start(bf16[3,38,128]{2,1,0:T(8,128)(2,1)S(1)} %get-tuple-element.195), channel_id=1, source_target_pairs={{7,0},{8,1},{9,2},{10,3},{11,4},{12,5},{13,6},{14,7},{15,8},{23,16... | collective-permute-start | bytes 87560 | tf_op jit(solution)/shard_map/ppermute | solution.py:22
  95.6 15.8 %collective-permute-start.18 = (bf16[3,38,128]{2,1,0:T(8,128)(2,1)S(1)}, bf16[3,38,128]{2,1,0:T(8,128)(2,1)S(1)}, u32[]{:S(2)}, u32[]{:S(2)}) collective-permute-start(bf16[3,38,128]{2,1,0:T(8,128)(2,1)S(1)} %get-tuple-element.195), channel_id=1, source_target_pairs={{0,8},{1,9},{2,10},{3,11},{4,12},{5,13},{6,14},{7,15},{16,24},{17,... | collective-permute-start | bytes 87560 | tf_op jit(solution)/shard_map/ppermute | solution.py:22
  104.7 6.7 %collective-permute-start.27 = (bf16[3,38,128]{2,1,0:T(8,128)(2,1)S(1)}, bf16[3,38,128]{2,1,0:T(8,128)(2,1)S(1)}, u32[]{:S(2)}, u32[]{:S(2)}) collective-permute-start(bf16[3,38,128]{2,1,0:T(8,128)(2,1)S(1)} %get-tuple-element.194), channel_id=1, source_target_pairs={{8,0},{9,1},{10,2},{11,3},{12,4},{13,5},{14,6},{15,7},{24,16},{25,... | collective-permute-start | bytes 87560 | tf_op jit(solution)/shard_map/ppermute | solution.py:22
  118.9 13.3 %collective-permute-start.28 = (bf16[16,3,128]{2,1,0:T(4,128)(2,1)S(1)}, bf16[16,3,128]{2,1,0:T(4,128)(2,1)S(1)}, u32[]{:S(2)}, u32[]{:S(2)}) collective-permute-start(bf16[16,3,128]{2,1,0:T(4,128)(2,1)S(1)} %get-tuple-element.203), channel_id=1, source_target_pairs={{7,0},{8,1},{9,2},{10,3},{11,4},{12,5},{13,6},{14,7},{15,8},{23,16... | collective-permute-start | bytes 36872 | tf_op jit(solution)/shard_map/ppermute | solution.py:22
  120.2 12.0 %collective-permute-start.29 = (bf16[16,3,128]{2,1,0:T(4,128)(2,1)S(1)}, bf16[16,3,128]{2,1,0:T(4,128)(2,1)S(1)}, u32[]{:S(2)}, u32[]{:S(2)}) collective-permute-start(bf16[16,3,128]{2,1,0:T(4,128)(2,1)S(1)} %get-tuple-element.203), channel_id=1, source_target_pairs={{0,1},{1,2},{2,3},{3,4},{4,5},{5,6},{6,7},{7,8},{8,9},{9,10},{10,1... | collective-permute-start | bytes 36872 | tf_op jit(solution)/shard_map/ppermute | solution.py:22
  121.5 10.7 %collective-permute-start.30 = (bf16[16,3,128]{2,1,0:T(4,128)(2,1)S(1)}, bf16[16,3,128]{2,1,0:T(4,128)(2,1)S(1)}, u32[]{:S(2)}, u32[]{:S(2)}) collective-permute-start(bf16[16,3,128]{2,1,0:T(4,128)(2,1)S(1)} %get-tuple-element.204), channel_id=1, source_target_pairs={{0,7},{1,8},{2,9},{3,10},{4,11},{5,12},{6,13},{7,14},{8,15},{16,23... | collective-permute-start | bytes 36872 | tf_op jit(solution)/shard_map/ppermute | solution.py:22
  127.3 4.9 %collective-permute-start.31 = (bf16[16,3,128]{2,1,0:T(4,128)(2,1)S(1)}, bf16[16,3,128]{2,1,0:T(4,128)(2,1)S(1)}, u32[]{:S(2)}, u32[]{:S(2)}) collective-permute-start(bf16[16,3,128]{2,1,0:T(4,128)(2,1)S(1)} %get-tuple-element.204), channel_id=1, source_target_pairs={{1,0},{2,1},{3,2},{4,3},{5,4},{6,5},{7,6},{8,7},{9,8},{10,9},{11,1... | collective-permute-start | bytes 36872 | tf_op jit(solution)/shard_map/ppermute | solution.py:22
  132.2 15.1 %collective-permute-start.33 = (bf16[3,38,128]{2,1,0:T(8,128)(2,1)S(1)}, bf16[3,38,128]{2,1,0:T(8,128)(2,1)S(1)}, u32[]{:S(2)}, u32[]{:S(2)}) collective-permute-start(bf16[3,38,128]{2,1,0:T(8,128)(2,1)S(1)} %get-tuple-element.191), channel_id=1, source_target_pairs={{0,7},{1,8},{2,9},{3,10},{4,11},{5,12},{6,13},{7,14},{8,15},{16,23... | collective-permute-start | bytes 87560 | tf_op jit(solution)/shard_map/ppermute | solution.py:22
  138.9 9.7 %collective-permute-start.34 = (bf16[3,38,128]{2,1,0:T(8,128)(2,1)S(1)}, bf16[3,38,128]{2,1,0:T(8,128)(2,1)S(1)}, u32[]{:S(2)}, u32[]{:S(2)}) collective-permute-start(bf16[3,38,128]{2,1,0:T(8,128)(2,1)S(1)} %get-tuple-element.191), channel_id=1, source_target_pairs={{0,5},{1,6},{2,7},{3,8},{4,9},{5,10},{6,11},{7,12},{8,13},{9,14},{... | collective-permute-start | bytes 87560 | tf_op jit(solution)/shard_map/ppermute | solution.py:22
  140.2 9.7 %collective-permute-start.35 = (bf16[3,38,128]{2,1,0:T(8,128)(2,1)S(1)}, bf16[3,38,128]{2,1,0:T(8,128)(2,1)S(1)}, u32[]{:S(2)}, u32[]{:S(2)}) collective-permute-start(bf16[3,38,128]{2,1,0:T(8,128)(2,1)S(1)} %get-tuple-element.191), channel_id=1, source_target_pairs={{0,3},{1,4},{2,5},{3,6},{4,7},{5,8},{6,9},{7,10},{8,11},{9,12},{10... | collective-permute-start | bytes 87560 | tf_op jit(solution)/shard_map/ppermute | solution.py:22
  144.4 7.2 %collective-permute-start.36 = (bf16[3,38,128]{2,1,0:T(8,128)(2,1)S(1)}, bf16[3,38,128]{2,1,0:T(8,128)(2,1)S(1)}, u32[]{:S(2)}, u32[]{:S(2)}) collective-permute-start(bf16[3,38,128]{2,1,0:T(8,128)(2,1)S(1)} %get-tuple-element.191), channel_id=1, source_target_pairs={{0,1},{1,2},{2,3},{3,4},{4,5},{5,6},{6,7},{7,8},{8,9},{9,10},{10,1... | collective-permute-start | bytes 87560 | tf_op jit(solution)/shard_map/ppermute | solution.py:22
  146.1 14.6 %collective-permute-start.37 = (bf16[3,38,128]{2,1,0:T(8,128)(2,1)S(1)}, bf16[3,38,128]{2,1,0:T(8,128)(2,1)S(1)}, u32[]{:S(2)}, u32[]{:S(2)}) collective-permute-start(bf16[3,38,128]{2,1,0:T(8,128)(2,1)S(1)} %get-tuple-element.191), channel_id=1, source_target_pairs={{1,0},{2,1},{3,2},{4,3},{5,4},{6,5},{7,6},{8,7},{9,8},{10,9},{11,1... | collective-permute-start | bytes 87560 | tf_op jit(solution)/shard_map/ppermute | solution.py:22
  147.4 14.6 %collective-permute-start.38 = (bf16[3,38,128]{2,1,0:T(8,128)(2,1)S(1)}, bf16[3,38,128]{2,1,0:T(8,128)(2,1)S(1)}, u32[]{:S(2)}, u32[]{:S(2)}) collective-permute-start(bf16[3,38,128]{2,1,0:T(8,128)(2,1)S(1)} %get-tuple-element.191), channel_id=1, source_target_pairs={{3,0},{4,1},{5,2},{6,3},{7,4},{8,5},{9,6},{10,7},{11,8},{12,9},{13... | collective-permute-start | bytes 87560 | tf_op jit(solution)/shard_map/ppermute | solution.py:22
  148.7 13.3 %collective-permute-start.39 = (bf16[3,38,128]{2,1,0:T(8,128)(2,1)S(1)}, bf16[3,38,128]{2,1,0:T(8,128)(2,1)S(1)}, u32[]{:S(2)}, u32[]{:S(2)}) collective-permute-start(bf16[3,38,128]{2,1,0:T(8,128)(2,1)S(1)} %get-tuple-element.191), channel_id=1, source_target_pairs={{5,0},{6,1},{7,2},{8,3},{9,4},{10,5},{11,6},{12,7},{13,8},{14,9},{... | collective-permute-start | bytes 87560 | tf_op jit(solution)/shard_map/ppermute | solution.py:22
  150.0 12.0 %collective-permute-start.40 = (bf16[3,38,128]{2,1,0:T(8,128)(2,1)S(1)}, bf16[3,38,128]{2,1,0:T(8,128)(2,1)S(1)}, u32[]{:S(2)}, u32[]{:S(2)}) collective-permute-start(bf16[3,38,128]{2,1,0:T(8,128)(2,1)S(1)} %get-tuple-element.191), channel_id=1, source_target_pairs={{7,0},{8,1},{9,2},{10,3},{11,4},{12,5},{13,6},{14,7},{15,8},{23,16... | collective-permute-start | bytes 87560 | tf_op jit(solution)/shard_map/ppermute | solution.py:22
  151.5 15.8 %collective-permute-start.32 = (bf16[3,38,128]{2,1,0:T(8,128)(2,1)S(1)}, bf16[3,38,128]{2,1,0:T(8,128)(2,1)S(1)}, u32[]{:S(2)}, u32[]{:S(2)}) collective-permute-start(bf16[3,38,128]{2,1,0:T(8,128)(2,1)S(1)} %get-tuple-element.191), channel_id=1, source_target_pairs={{0,8},{1,9},{2,10},{3,11},{4,12},{5,13},{6,14},{7,15},{16,24},{17,... | collective-permute-start | bytes 87560 | tf_op jit(solution)/shard_map/ppermute | solution.py:22
  160.7 6.7 %collective-permute-start.41 = (bf16[3,38,128]{2,1,0:T(8,128)(2,1)S(1)}, bf16[3,38,128]{2,1,0:T(8,128)(2,1)S(1)}, u32[]{:S(2)}, u32[]{:S(2)}) collective-permute-start(bf16[3,38,128]{2,1,0:T(8,128)(2,1)S(1)} %get-tuple-element.190), channel_id=1, source_target_pairs={{8,0},{9,1},{10,2},{11,3},{12,4},{13,5},{14,6},{15,7},{24,16},{25,... | collective-permute-start | bytes 87560 | tf_op jit(solution)/shard_map/ppermute | solution.py:22
  178.2 17.9 %collective-permute-start.42 = (bf16[16,3,128]{2,1,0:T(4,128)(2,1)S(1)}, bf16[16,3,128]{2,1,0:T(4,128)(2,1)S(1)}, u32[]{:S(2)}, u32[]{:S(2)}) collective-permute-start(bf16[16,3,128]{2,1,0:T(4,128)(2,1)S(1)} %get-tuple-element.201), channel_id=1, source_target_pairs={{7,0},{8,1},{9,2},{10,3},{11,4},{12,5},{13,6},{14,7},{15,8},{23,16... | collective-permute-start | bytes 36872 | tf_op jit(solution)/shard_map/ppermute | solution.py:22
  179.5 16.6 %collective-permute-start.43 = (bf16[16,3,128]{2,1,0:T(4,128)(2,1)S(1)}, bf16[16,3,128]{2,1,0:T(4,128)(2,1)S(1)}, u32[]{:S(2)}, u32[]{:S(2)}) collective-permute-start(bf16[16,3,128]{2,1,0:T(4,128)(2,1)S(1)} %get-tuple-element.201), channel_id=1, source_target_pairs={{0,1},{1,2},{2,3},{3,4},{4,5},{5,6},{6,7},{7,8},{8,9},{9,10},{10,1... | collective-permute-start | bytes 36872 | tf_op jit(solution)/shard_map/ppermute | solution.py:22
  180.8 15.3 %collective-permute-start.44 = (bf16[16,3,128]{2,1,0:T(4,128)(2,1)S(1)}, bf16[16,3,128]{2,1,0:T(4,128)(2,1)S(1)}, u32[]{:S(2)}, u32[]{:S(2)}) collective-permute-start(bf16[16,3,128]{2,1,0:T(4,128)(2,1)S(1)} %get-tuple-element.202), channel_id=1, source_target_pairs={{0,7},{1,8},{2,9},{3,10},{4,11},{5,12},{6,13},{7,14},{8,15},{16,23... | collective-permute-start | bytes 36872 | tf_op jit(solution)/shard_map/ppermute | solution.py:22
  186.6 9.5 %collective-permute-start.45 = (bf16[16,3,128]{2,1,0:T(4,128)(2,1)S(1)}, bf16[16,3,128]{2,1,0:T(4,128)(2,1)S(1)}, u32[]{:S(2)}, u32[]{:S(2)}) collective-permute-start(bf16[16,3,128]{2,1,0:T(4,128)(2,1)S(1)} %get-tuple-element.202), channel_id=1, source_target_pairs={{1,0},{2,1},{3,2},{4,3},{5,4},{6,5},{7,6},{8,7},{9,8},{10,9},{11,1... | collective-permute-start | bytes 36872 | tf_op jit(solution)/shard_map/ppermute | solution.py:22
  196.2 13.7 %collective-permute-start.47 = (bf16[3,38,128]{2,1,0:T(8,128)(2,1)S(1)}, bf16[3,38,128]{2,1,0:T(8,128)(2,1)S(1)}, u32[]{:S(2)}, u32[]{:S(2)}) collective-permute-start(bf16[3,38,128]{2,1,0:T(8,128)(2,1)S(1)} %get-tuple-element.187), channel_id=1, source_target_pairs={{0,7},{1,8},{2,9},{3,10},{4,11},{5,12},{6,13},{7,14},{8,15},{16,23... | collective-permute-start | bytes 87560 | tf_op jit(solution)/shard_map/ppermute | solution.py:22
  202.9 8.4 %collective-permute-start.48 = (bf16[3,38,128]{2,1,0:T(8,128)(2,1)S(1)}, bf16[3,38,128]{2,1,0:T(8,128)(2,1)S(1)}, u32[]{:S(2)}, u32[]{:S(2)}) collective-permute-start(bf16[3,38,128]{2,1,0:T(8,128)(2,1)S(1)} %get-tuple-element.187), channel_id=1, source_target_pairs={{0,5},{1,6},{2,7},{3,8},{4,9},{5,10},{6,11},{7,12},{8,13},{9,14},{... | collective-permute-start | bytes 87560 | tf_op jit(solution)/shard_map/ppermute | solution.py:22
  204.2 8.4 %collective-permute-start.49 = (bf16[3,38,128]{2,1,0:T(8,128)(2,1)S(1)}, bf16[3,38,128]{2,1,0:T(8,128)(2,1)S(1)}, u32[]{:S(2)}, u32[]{:S(2)}) collective-permute-start(bf16[3,38,128]{2,1,0:T(8,128)(2,1)S(1)} %get-tuple-element.187), channel_id=1, source_target_pairs={{0,3},{1,4},{2,5},{3,6},{4,7},{5,8},{6,9},{7,10},{8,11},{9,12},{10... | collective-permute-start | bytes 87560 | tf_op jit(solution)/shard_map/ppermute | solution.py:22
  207.0 8.1 %collective-permute-start.50 = (bf16[3,38,128]{2,1,0:T(8,128)(2,1)S(1)}, bf16[3,38,128]{2,1,0:T(8,128)(2,1)S(1)}, u32[]{:S(2)}, u32[]{:S(2)}) collective-permute-start(bf16[3,38,128]{2,1,0:T(8,128)(2,1)S(1)} %get-tuple-element.187), channel_id=1, source_target_pairs={{0,1},{1,2},{2,3},{3,4},{4,5},{5,6},{6,7},{7,8},{8,9},{9,10},{10,1... | collective-permute-start | bytes 87560 | tf_op jit(solution)/shard_map/ppermute | solution.py:22
  208.6 15.6 %collective-permute-start.51 = (bf16[3,38,128]{2,1,0:T(8,128)(2,1)S(1)}, bf16[3,38,128]{2,1,0:T(8,128)(2,1)S(1)}, u32[]{:S(2)}, u32[]{:S(2)}) collective-permute-start(bf16[3,38,128]{2,1,0:T(8,128)(2,1)S(1)} %get-tuple-element.187), channel_id=1, source_target_pairs={{1,0},{2,1},{3,2},{4,3},{5,4},{6,5},{7,6},{8,7},{9,8},{10,9},{11,1... | collective-permute-start | bytes 87560 | tf_op jit(solution)/shard_map/ppermute | solution.py:22
  209.9 15.8 %collective-permute-start.52 = (bf16[3,38,128]{2,1,0:T(8,128)(2,1)S(1)}, bf16[3,38,128]{2,1,0:T(8,128)(2,1)S(1)}, u32[]{:S(2)}, u32[]{:S(2)}) collective-permute-start(bf16[3,38,128]{2,1,0:T(8,128)(2,1)S(1)} %get-tuple-element.187), channel_id=1, source_target_pairs={{3,0},{4,1},{5,2},{6,3},{7,4},{8,5},{9,6},{10,7},{11,8},{12,9},{13... | collective-permute-start | bytes 87560 | tf_op jit(solution)/shard_map/ppermute | solution.py:22
  211.2 14.5 %collective-permute-start.53 = (bf16[3,38,128]{2,1,0:T(8,128)(2,1)S(1)}, bf16[3,38,128]{2,1,0:T(8,128)(2,1)S(1)}, u32[]{:S(2)}, u32[]{:S(2)}) collective-permute-start(bf16[3,38,128]{2,1,0:T(8,128)(2,1)S(1)} %get-tuple-element.187), channel_id=1, source_target_pairs={{5,0},{6,1},{7,2},{8,3},{9,4},{10,5},{11,6},{12,7},{13,8},{14,9},{... | collective-permute-start | bytes 87560 | tf_op jit(solution)/shard_map/ppermute | solution.py:22
  212.5 13.2 %collective-permute-start.54 = (bf16[3,38,128]{2,1,0:T(8,128)(2,1)S(1)}, bf16[3,38,128]{2,1,0:T(8,128)(2,1)S(1)}, u32[]{:S(2)}, u32[]{:S(2)}) collective-permute-start(bf16[3,38,128]{2,1,0:T(8,128)(2,1)S(1)} %get-tuple-element.187), channel_id=1, source_target_pairs={{7,0},{8,1},{9,2},{10,3},{11,4},{12,5},{13,6},{14,7},{15,8},{23,16... | collective-permute-start | bytes 87560 | tf_op jit(solution)/shard_map/ppermute | solution.py:22
  215.1 16.0 %collective-permute-start.46 = (bf16[3,38,128]{2,1,0:T(8,128)(2,1)S(1)}, bf16[3,38,128]{2,1,0:T(8,128)(2,1)S(1)}, u32[]{:S(2)}, u32[]{:S(2)}) collective-permute-start(bf16[3,38,128]{2,1,0:T(8,128)(2,1)S(1)} %get-tuple-element.187), channel_id=1, source_target_pairs={{0,8},{1,9},{2,10},{3,11},{4,12},{5,13},{6,14},{7,15},{16,24},{17,... | collective-permute-start | bytes 87560 | tf_op jit(solution)/shard_map/ppermute | solution.py:22
  224.2 6.7 %collective-permute-start.55 = (bf16[3,38,128]{2,1,0:T(8,128)(2,1)S(1)}, bf16[3,38,128]{2,1,0:T(8,128)(2,1)S(1)}, u32[]{:S(2)}, u32[]{:S(2)}) collective-permute-start(bf16[3,38,128]{2,1,0:T(8,128)(2,1)S(1)} %get-tuple-element.186), channel_id=1, source_target_pairs={{8,0},{9,1},{10,2},{11,3},{12,4},{13,5},{14,6},{15,7},{24,16},{25,... | collective-permute-start | bytes 87560 | tf_op jit(solution)/shard_map/ppermute | solution.py:22
  236.1 185.3 %all-reduce.9.cloned.1.call-start = ((), (), s32[]{:S(2)}) async-start(), calls=%async_computation.1 | async-start | bytes 2097152 | tf_op jit(solution)/shard_map/psum | solution.py:190
  321.7 99.7 %copy-start.8 = (f32[75,128]{1,0:T(8,128)S(1)}, f32[75,128]{1,0:T(8,128)}, u32[]{:S(2)}) copy-start(f32[75,128]{1,0:T(8,128)} %get-tuple-element.322) | copy-start | bytes 115204
  (136 other events, 2224.4 us)
Sparse Core Ops, SparseCore 0:
  236.2 85.4 all-reduce.6
  325.8 95.5 all-reduce.8
where the time goes:
time: 435 us; the launch traced here: 433 us
  waiting for transfers between devices  206 us (47%)
  starting transfers between devices  150 us (34%)
  other arithmetic  26.5 us (6%)
  local copies, waits for them, and re-layouts  20.2 us (5%)
  between operations  16.6 us (4%)
  matrix products  13.7 us (3%)
    psum x2, waiting for transfers between devices, shards(): lax.psum((stem_gradient, kernel_stack, gain_stack, win_stack, wout_stack,...  183 us
    ppermute x56, starting transfers between devices, passed_along(): lax.ppermute(value, axis, [(source, source + steps) for source in range(i...  150 us
    ppermute x56, waiting for transfers between devices, passed_along(): lax.ppermute(value, axis, [(source, source + steps) for source in range(i...  22.7 us
    unnamed x290, local copies, waits for them, and re-layouts  12.4 us
  transfers between devices with their start and end apart: 58, of which 8 were waited for; matrix products, arithmetic and copies ran while one was open for 5% of the time, Pallas kernels for 0%

commit v1 on v0

v1 whole, which is shorter than its diff:
```python
import functools
import math

import jax
import jax.numpy as jnp
from jax import lax
from jax.experimental import pallas as pl
from jax.experimental.pallas import tpu as pltpu
from jax.sharding import PartitionSpec as P

TH = 16
TW = 32
TX = 8
LANES = 128

RIM = 6
PADC = 8
EH, EW = TH + 2 * RIM, TW + 2 * PADC
RH, RW = TH + 6, 40
RING_COL = 5

C0 = 0.7978845608028654
C1 = 0.7978845608028654 * 0.044715
NORM_STABILIZER = 1e-06

WIN_ROW, WOUT_ROW, SMALL_ROW = 0, 1024, 2048
STEM_AT, KERNEL_AT, GAIN_AT, SCALE_AT = 0, (80, 136), 192, 194
SMALL_ROWS = 256
PACKED = SMALL_ROW + SMALL_ROWS

BF = jnp.bfloat16
F32 = jnp.float32


def vmem(count):
    return [pl.BlockSpec(memory_space=pltpu.VMEM)] * count


def smem():
    return pl.BlockSpec(memory_space=pltpu.SMEM)


def contract_rows(left, right):
    return lax.dot_general(left, right, (((0,), (0,)), ((), ())), preferred_element_type=F32)


def contract_cols(left, right):
    return lax.dot_general(left, right, (((1,), (1,)), ((), ())), preferred_element_type=F32)


def prepare_kernel(levels_ref, ocean_ref, tile_ref, west_ref, east_ref, stage):
    count = levels_ref.shape[0]
    stage[...] = jnp.zeros_like(stage)
    stage[0:count, :] = levels_ref[...].astype(F32)
    stage[count : count + 1, :] = ocean_ref[...].astype(F32)
    rows = lax.broadcasted_iota(jnp.int32, (LANES, LANES), 0)
    cols = lax.broadcasted_iota(jnp.int32, (LANES, LANES), 1)
    eye = (rows == cols).astype(BF)
    turned = contract_rows(stage[...].astype(BF), eye).reshape(TH, TW, LANES)
    tile_ref[...] = turned.astype(BF)
    west_ref[...] = turned[:, :PADC].astype(BF)
    east_ref[...] = turned[:, TW - PADC :].astype(BF)


def load_column(ref, row, start):
    return ref[row, pl.ds(start, 8), :]


def conv_block(ref, taps, start, out_rows, in_rows, taps_of):
    totals = {o: None for o in out_rows}
    needed = sorted({o + a for o in out_rows for a in range(7) if o + a in in_rows})
    for d in range(7):
        column = {r: load_column(ref, r - in_rows.start, start + d) for r in needed}
        for a in range(7):
            held = {}
            for o in out_rows:
                r = o + a
                if r not in column:
                    continue
                which, index = taps_of(o, r, a, d)
                if (which, index) not in held:
                    held[(which, index)] = taps[which][index]
                term = held[(which, index)] * column[r]
                totals[o] = term if totals[o] is None else totals[o] + term
    return totals


def main_kernel(
    two_rows,
    rescale,
    top_ref,
    tile_ref,
    west_ref,
    east_ref,
    south_ref,
    north_ref,
    fold_ref,
    stem_ref,
    dw_ref,
    gain_ref,
    win_ref,
    wout_ref,
    scale_ref,
    up_ref,
    out_ref,
    packed_ref,
    ext,
    x0,
    m6,
    x1,
    weights,
    taps0,
    taps0n,
    taps1,
    conv0,
    xhat0,
    rinv0,
    branch0,
    normed0,
    act0,
    slope0,
    conv1,
    xhat1,
    rinv1,
    branch1,
    normed1,
    act1,
    slope1,
    wide,
    thin,
    gpre,
    pad0,
    pad1,
    g1,
    h0,
    gk0,
    gk0n,
    gk1,
    small,
):
    top = top_ref[0] == 1
    levels_count = stem_ref.shape[0]

    def mirrored(step):
        rows = lax.broadcasted_iota(jnp.int32, (EW, EW), 0)
        cols = lax.broadcasted_iota(jnp.int32, (EW, EW), 1)
        swap = (rows + cols == EW - 1).astype(BF)
        return jnp.dot(swap, fold_ref[RIM - 1 - step], preferred_element_type=F32)

    for step in range(RIM):
        south = south_ref[step].astype(F32)
        if two_rows:
            south = jnp.where(top, south, 0.0)
        ext[step] = south
        ext[RIM + TH + step] = jnp.where(top, mirrored(step), north_ref[step].astype(F32))
    ext[RIM : RIM + TH, 0:PADC] = west_ref[...].astype(F32)
    ext[RIM : RIM + TH, PADC : PADC + TW] = tile_ref[...].astype(F32)
    ext[RIM : RIM + TH, PADC + TW :] = east_ref[...].astype(F32)

    weights[...] = jnp.zeros_like(weights)
    weights[0:levels_count, 0:LANES] = stem_ref[...].astype(F32)
    weights[levels_count : levels_count + 1, LANES:] = jnp.ones((1, LANES), F32)
    joint = weights[...].astype(BF)

    def embed(row, _):
        both = jnp.dot(ext[row].astype(BF), joint, preferred_element_type=F32)
        mask = both[:, LANES:]
        m6[row] = mask
        x0[row] = (mask * both[:, :LANES]).astype(BF).astype(F32)
        return 0

    lax.fori_loop(0, EH, embed, 0)

    for t in range(49):
        first = dw_ref[0, t : t + 1, :]
        turned = dw_ref[0, 48 - t : 49 - t, :]
        taps0[t] = jnp.broadcast_to(first, (8, LANES))
        taps0n[t] = jnp.broadcast_to(jnp.where(top, turned, first), (8, LANES))
        taps1[t] = jnp.broadcast_to(dw_ref[1, t : t + 1, :], (8, LANES))

    north_at = 3 + TH

    def conv0_block(block, _):
        start = pl.multiple_of(block * 8, 8)
        for rows in (range(0, 10), range(10, 19), range(19, 22)):
            totals = conv_block(
                x0,
                (taps0, taps0n),
                start + 2,
                rows,
                range(0, EH),
                lambda o, r, a, d: (1 if o >= north_at else 0, a * 7 + d),
            )
            for o in rows:
                conv0[o, pl.ds(start, 8), :] = totals[o]
        return 0

    lax.fori_loop(0, RW // 8, conv0_block, 0)

    def norm_rows(conv, xhat, rinv, normed, gain):
        def step(row, _):
            values = conv[row]
            width = values.shape[0]
            average = jnp.mean(values, axis=-1, keepdims=True)
            centered = values - average
            inverse = lax.rsqrt(jnp.mean(centered * centered, axis=-1, keepdims=True) + NORM_STABILIZER)
            scaled = centered * inverse
            xhat[row] = scaled
            rinv[row] = jnp.broadcast_to(inverse, (width, LANES))
            normed[row] = (scaled * gain).astype(BF)
            return 0

        lax.fori_loop(0, conv.shape[0], step, 0)

    def gelu_rows(pre, act, slope, count):
        def step(index, _):
            at = pl.ds(pl.multiple_of(index * 16, 16), 16)
            v = pre[at, :]
            square = v * v
            inner = v * (C0 + C1 * square)
            half = 0.5 * jnp.tanh(inner) + 0.5
            active = v * half
            act[at, :] = active.astype(BF)
            slope[at, :] = half + active * (1.0 - half) * (2.0 * C0 + (6.0 * C1) * square)
            return 0

        lax.fori_loop(0, count // 16, step, 0)

    count0, count1 = RH * RW, TH * TW
    norm_rows(conv0, xhat0, rinv0, normed0, gain_ref[0:1, :])
    wide[0:count0] = jnp.dot(
        normed0[...].astype(F32).reshape(count0, LANES).astype(BF), win_ref[0], preferred_element_type=F32
    )
    gelu_rows(wide, act0, slope0, count0)
    branch0[...] = jnp.dot(act0[...], wout_ref[0], preferred_element_type=F32).reshape(RH, RW, LANES)

    def next0(row, _):
        mask = m6[row + 3, pl.ds(RING_COL, RW), :]
        held = x0[row + 3, pl.ds(RING_COL, RW), :]
        x1[row] = (mask * (held + scale_ref[0:1, :] * branch0[row])).astype(BF).astype(F32)
        return 0

    lax.fori_loop(0, RH, next0, 0)

    def conv1_block(block, _):
        start = pl.multiple_of(block * 8, 8)
        for rows in (range(0, 8), range(8, 16)):
            totals = conv_block(
                x1, (taps1,), start, rows, range(0, RH), lambda o, r, a, d: (0, a * 7 + d)
            )
            for o in rows:
                conv1[o, pl.ds(start, 8), :] = totals[o]
        return 0

    lax.fori_loop(0, TW // 8, conv1_block, 0)
    norm_rows(conv1, xhat1, rinv1, normed1, gain_ref[1:2, :])
    wide[0:count1] = jnp.dot(
        normed1[...].reshape(count1, LANES), win_ref[1], preferred_element_type=F32
    )
    gelu_rows(wide, act1, slope1, count1)
    branch1[...] = jnp.dot(act1[...], wout_ref[1], preferred_element_type=F32).reshape(TH, TW, LANES)

    small[...] = jnp.zeros_like(small)
    g1[...] = jnp.zeros_like(g1)

    def next1(row, total):
        mask = m6[row + RIM, pl.ds(PADC, TW), :]
        held = x1[row + 3, pl.ds(3, TW), :]
        branch = branch1[row]
        out_ref[row] = (mask * (held + scale_ref[1:2, :] * branch)).astype(BF)
        masked = mask * (up_ref[row].astype(F32) * rescale)
        g1[row + 3, pl.ds(3, TW), :] = masked
        thin[pl.ds(pl.multiple_of(row * TW, TW), TW), :] = (masked * scale_ref[1:2, :]).astype(BF)
        return total + jnp.sum((masked * branch).reshape(TW // 8, 8, LANES), axis=0)

    total = lax.fori_loop(0, TH, next1, jnp.zeros((8, LANES), F32))
    small[SCALE_AT + 1 : SCALE_AT + 2, :] = jnp.sum(total, axis=0, keepdims=True)

    def mlp_backward(layer, count, shape, normed, act, slope, xhat, rinv, store):
        gb = thin[0:count]
        packed_ref[WOUT_ROW + 512 * layer : WOUT_ROW + 512 * layer + 512, :] = contract_rows(
            act[...], gb
        ).astype(BF)
        wide[0:count] = contract_cols(gb, wout_ref[layer])

        def step(index, _):
            at = pl.ds(pl.multiple_of(index * 16, 16), 16)
            gpre[at, :] = (wide[at, :] * slope[at, :]).astype(BF)
            return 0

        lax.fori_loop(0, count // 16, step, 0)
        gp = gpre[0:count]
        grad_in = contract_rows(normed, gp).astype(BF)
        for part in range(4):
            at = WIN_ROW + 512 * layer + 128 * part
            packed_ref[at : at + 128, :] = grad_in[:, 128 * part : 128 * part + 128]
        wide[0:count, 0:LANES] = contract_cols(gp, win_ref[layer])
        rows, width = shape
        gain = gain_ref[layer : layer + 1, :]

        def finish(row, total):
            gn = wide[pl.ds(pl.multiple_of(row * width, 8), width), 0:LANES]
            scaled = xhat[row]
            gx = gn * gain
            both = gx - jnp.mean(gx, axis=-1, keepdims=True)
            both = both - scaled * jnp.mean(gx * scaled, axis=-1, keepdims=True)
            store(row, (rinv[row] * both).astype(BF).astype(F32))
            return total + jnp.sum((gn * scaled).reshape(width // 8, 8, LANES), axis=0)

        total = lax.fori_loop(0, rows, finish, jnp.zeros((8, LANES), F32))
        small[GAIN_AT + layer : GAIN_AT + layer + 1, :] = jnp.sum(total, axis=0, keepdims=True)

    pad1[...] = jnp.zeros_like(pad1)

    def store1(row, value):
        pad1[row, pl.ds(PADC, TW), :] = value

    mlp_backward(
        1, count1, (TH, TW), normed1[...].reshape(count1, LANES), act1, slope1, xhat1, rinv1, store1
    )

    gk1[...] = jnp.zeros_like(gk1)

    def kernel1_block(block, _):
        start = pl.multiple_of(block * 8, 8)
        grads = [pad1[j, pl.ds(start + PADC, 8), :] for j in range(TH)]
        for d in range(7):
            column = [load_column(x1, r, start + d) for r in range(RH)]
            for a in range(7):
                total = gk1[a * 7 + d]
                for j in range(TH):
                    total = total + grads[j] * column[j + a]
                gk1[a * 7 + d] = total
        return 0

    lax.fori_loop(0, TW // 8, kernel1_block, 0)

    def back1_block(block, _):
        start = pl.multiple_of(block * 8, 8)
        for rows in (range(0, 11), range(11, 22)):
            totals = conv_block(
                pad1, (taps1,), start + 2, rows, range(6, 6 + TH), lambda o, r, a, d: (0, 48 - (a * 7 + d))
            )
            for o in rows:
                g1[o, pl.ds(start, 8), :] += totals[o]
        return 0

    lax.fori_loop(0, RW // 8, back1_block, 0)

    def masked0(row, total):
        masked = m6[row + 3, pl.ds(RING_COL, RW), :] * g1[row]
        g1[row] = masked
        gpad = (masked * scale_ref[0:1, :]).astype(BF)
        normed_at = pl.ds(pl.multiple_of(row * RW, 8), RW)
        h0[normed_at, :] = gpad.astype(F32)
        return total + jnp.sum((masked * branch0[row]).reshape(RW // 8, 8, LANES), axis=0)

    total = lax.fori_loop(0, RH, masked0, jnp.zeros((8, LANES), F32))
    small[SCALE_AT : SCALE_AT + 1, :] = jnp.sum(total, axis=0, keepdims=True)
    thin[0:count0] = h0[0:count0].astype(BF)
    pad0[...] = jnp.zeros_like(pad0)

    def store0(row, value):
        pad0[row, pl.ds(PADC, RW), :] = value

    mlp_backward(
        0,
        count0,
        (RH, RW),
        normed0[...].astype(F32).reshape(count0, LANES).astype(BF),
        act0,
        slope0,
        xhat0,
        rinv0,
        store0,
    )

    gk0[...] = jnp.zeros_like(gk0)
    gk0n[...] = jnp.zeros_like(gk0n)

    def kernel0_block(block, _):
        start = pl.multiple_of(block * 8, 8)
        grads = [pad0[j, pl.ds(start + PADC, 8), :] for j in range(RH)]
        for d in range(7):
            column = [load_column(x0, r, start + 2 + d) for r in range(EH)]
            for a in range(7):
                total = gk0[a * 7 + d]
                for j in range(north_at):
                    total = total + grads[j] * column[j + a]
                gk0[a * 7 + d] = total
                total = gk0n[a * 7 + d]
                for j in range(north_at, RH):
                    total = total + grads[j] * column[j + a]
                gk0n[a * 7 + d] = total
        return 0

    lax.fori_loop(0, RW // 8, kernel0_block, 0)
    for t in range(49):
        north = jnp.where(top, gk0n[48 - t], gk0n[t])
        small[KERNEL_AT[0] + t : KERNEL_AT[0] + t + 1, :] = jnp.sum(gk0[t] + north, axis=0, keepdims=True)
        small[KERNEL_AT[1] + t : KERNEL_AT[1] + t + 1, :] = jnp.sum(gk1[t], axis=0, keepdims=True)

    def back0_block(block, _):
        start = pl.multiple_of(block * 8, 8)
        for rows in (range(0, 7), range(7, 14), range(14, 21), range(21, 28)):
            totals = conv_block(
                pad0,
                (taps0, taps0n),
                start,
                rows,
                range(6, 6 + RH),
                lambda o, r, a, d: (1 if r - 6 >= north_at else 0, 48 - (a * 7 + d)),
            )
            for o in rows:
                h0[pl.ds(pl.multiple_of(o * EW + start, 8), 8), :] = totals[o]
        return 0

    lax.fori_loop(0, EW // 8, back0_block, 0)

    def carry0(row, _):
        at = pl.multiple_of((row + 3) * EW, 8) + RING_COL
        h0[pl.ds(at, RW), :] += g1[row]
        return 0

    lax.fori_loop(0, RH, carry0, 0)
    stem_side = (m6[...].reshape(EH * EW, LANES) * h0[...]).astype(BF)
    stem_grad = contract_rows(ext[...].reshape(EH * EW, LANES).astype(BF), stem_side)
    small[STEM_AT : STEM_AT + 80, :] = stem_grad[0:80, :]
    packed_ref[SMALL_ROW : SMALL_ROW + SMALL_ROWS, :] = small[...].astype(BF)


def unpack_kernel(order_ref, pieces_ref, stem_ref, kernel_ref, gain_ref, win_ref, wout_ref, scale_ref, rows):
    count, size = pieces_ref.shape[0], pieces_ref.shape[1]
    for index in range(count):
        rows[index * size : (index + 1) * size, :] = pieces_ref[order_ref[index]].astype(F32)
    for layer in range(2):
        for part in range(4):
            at = WIN_ROW + 512 * layer + 128 * part
            win_ref[layer, :, 128 * part : 128 * part + 128] = rows[at : at + 128, :]
        at = WOUT_ROW + 512 * layer
        wout_ref[layer] = rows[at : at + 512, :]
        at = SMALL_ROW + KERNEL_AT[layer]
        kernel_ref[layer] = rows[at : at + 49, :]
    at = SMALL_ROW + STEM_AT
    stem_ref[...] = rows[at : at + stem_ref.shape[0], :]
    gain_ref[...] = rows[SMALL_ROW + GAIN_AT : SMALL_ROW + GAIN_AT + 2, :]
    scale_ref[...] = rows[SMALL_ROW + SCALE_AT : SMALL_ROW + SCALE_AT + 2, :]


def permuted(value, pairs):
    return lax.ppermute(value, "gy", pairs)


def crossed(value, bits):
    return permuted(value, [(i, i ^ bits) for i in range(lax.axis_size("gy"))])


def summed_pieces(packed):
    size = lax.axis_size("gy")
    if size != 16:
        return lax.psum(packed.astype(F32), "gy").astype(BF)[None], jnp.zeros((1,), jnp.int32)
    me = lax.axis_index("gy")
    core, side, deep = me & 1, (me >> 1) & 1, me >> 2

    def halves(value, bit):
        half = value.shape[0] // 2
        low, high = value[:half], value[half:]
        return jnp.where(bit == 0, low, high), jnp.where(bit == 0, high, low)

    keep, send = halves(packed, core)
    total = keep.astype(F32) + crossed(send, 1).astype(F32)
    keep, send = halves(total, side)
    total = keep + crossed(send.astype(BF), 2).astype(F32)
    quarter = total.shape[0] // 4

    def shard(step):
        return lax.dynamic_slice_in_dim(total, (deep ^ step) * quarter, quarter, 0)

    arrived = [crossed(shard(step).astype(BF), 4 * step) for step in (1, 2, 3)]
    mine = shard(0)
    for other in arrived:
        mine = mine + other.astype(F32)
    mine = mine.astype(BF)
    pieces = jnp.stack([mine] + [crossed(mine, 4 * step) for step in (1, 2, 3)])
    pieces = jnp.concatenate([pieces, crossed(pieces, 2)], axis=0)
    pieces = jnp.concatenate([pieces, crossed(pieces, 1)], axis=0)
    index = jnp.arange(16, dtype=jnp.int32)
    mixed = (core << 3) | (side << 2) | deep
    return pieces, index ^ mixed.astype(jnp.int32)


def shards(levels, ocean, stem, dw_kernel, ln_gain, w_in, w_out, layer_scale, upstream):
    size = lax.axis_size("gy")
    rows = size // TX
    me = lax.axis_index("gy")
    is_top = me // TX == rows - 1
    count = levels.shape[2]
    tile, west_cols, east_cols = pl.pallas_call(
        prepare_kernel,
        out_shape=[
            jax.ShapeDtypeStruct((TH, TW, LANES), BF),
            jax.ShapeDtypeStruct((TH, PADC, LANES), BF),
            jax.ShapeDtypeStruct((TH, PADC, LANES), BF),
        ],
        in_specs=vmem(2),
        out_specs=vmem(3),
        scratch_shapes=[pltpu.VMEM((LANES, count), F32)],
    )(levels[0], ocean)

    def column_pairs(step):
        return [(i, i // TX * TX + (i % TX + step) % TX) for i in range(size)]

    west = permuted(east_cols, column_pairs(1))
    east = permuted(west_cols, column_pairs(-1))
    upper = jnp.concatenate([west[-RIM:], tile[-RIM:], east[-RIM:]], axis=1)
    lower = jnp.concatenate([west[:RIM], tile[:RIM], east[:RIM]], axis=1)
    fold = permuted(upper, [(i, i // TX * TX + TX - 1 - i % TX) for i in range(size - TX, size)])
    two_rows = rows == 2
    if two_rows:
        south = north = permuted(
            jnp.where(is_top, lower, upper), [(i, (i + TX) % size) for i in range(size)]
        )
    else:
        south = permuted(upper, [(i, i + TX) for i in range(size - TX)])
        north = permuted(lower, [(i + TX, i) for i in range(size - TX)])

    def scratch(*shape, dtype=F32):
        return pltpu.VMEM(shape, dtype)

    count0 = RH * RW
    hidden = w_in.shape[2]
    result, packed = pl.pallas_call(
        functools.partial(main_kernel, two_rows, 1.0 / math.sqrt(size * count)),
        out_shape=[
            jax.ShapeDtypeStruct((TH, TW, LANES), BF),
            jax.ShapeDtypeStruct((PACKED, LANES), BF),
        ],
        in_specs=[smem()] + vmem(13),
        out_specs=vmem(2),
        scratch_shapes=[
            scratch(EH, EW, LANES),
            scratch(EH, EW, LANES),
            scratch(EH, EW, LANES),
            scratch(RH, RW, LANES),
            scratch(LANES, 2 * LANES),
            scratch(49, 8, LANES),
            scratch(49, 8, LANES),
            scratch(49, 8, LANES),
            scratch(RH, RW, LANES),
            scratch(RH, RW, LANES),
            scratch(RH, RW, LANES),
            scratch(RH, RW, LANES),
            scratch(RH, RW, LANES, dtype=BF),
            scratch(count0, hidden, dtype=BF),
            scratch(count0, hidden),
            scratch(TH, TW, LANES),
            scratch(TH, TW, LANES),
            scratch(TH, TW, LANES),
            scratch(TH, TW, LANES),
            scratch(TH, TW, LANES, dtype=BF),
            scratch(count, hidden, dtype=BF),
            scratch(count, hidden),
            scratch(count0, hidden),
            scratch(count0, LANES, dtype=BF),
            scratch(count0, hidden, dtype=BF),
            scratch(RH, EW + 8, LANES),
            scratch(TH, EW, LANES),
            scratch(RH, RW, LANES),
            scratch(EH * EW, LANES),
            scratch(49, 8, LANES),
            scratch(49, 8, LANES),
            scratch(49, 8, LANES),
            scratch(SMALL_ROWS, LANES),
        ],
        compiler_params=pltpu.CompilerParams(vmem_limit_bytes=40 << 20),
    )(
        is_top.astype(jnp.int32)[None],
        tile,
        west,
        east,
        south,
        north,
        fold,
        stem,
        dw_kernel,
        ln_gain,
        w_in,
        w_out,
        layer_scale,
        upstream[0].reshape(TH, TW, LANES),
    )
    pieces, order = summed_pieces(packed)
    shapes = [stem, dw_kernel, ln_gain, w_in, w_out, layer_scale]
    grads = pl.pallas_call(
        unpack_kernel,
        out_shape=[jax.ShapeDtypeStruct(array.shape, F32) for array in shapes],
        in_specs=[smem()] + vmem(1),
        out_specs=vmem(6),
        scratch_shapes=[scratch(PACKED, LANES)],
    )(order, pieces)
    return (result.reshape(1, TH * TW, LANES), *grads)


def solution(mesh):
    in_specs = (
        P(("groups", "gy"), None, None),
        P(("groups", "gy"), None),
        P(),
        P(),
        P(),
        P(),
        P(),
        P(),
        P(("groups", "gy"), None, None),
    )
    out_specs = (
        P(("groups", "gy"), None, None),
        P("groups", None),
        P("groups", None, None),
        P("groups", None),
        P("groups", None, None),
        P("groups", None, None),
        P("groups", None),
    )
    return jax.shard_map(shards, mesh=mesh, in_specs=in_specs, out_specs=out_specs, check_vma=False)
```

time: 435 us -> 86.1 us (0.20)
  waiting for transfers between devices: 206 us -> 23.5 us
  starting transfers between devices: 150 us -> 19.3 us
  Pallas kernels: 0 us -> 36.6 us
  other arithmetic: 26.5 us -> 0.78 us
  between operations: 16.6 us -> 0.83 us
  local copies, waits for them, and re-layouts: 20.2 us -> 4.8 us
  matrix products: 13.7 us -> 0 us
    psum x2 -> x0, waiting for transfers between devices: 183 us -> none  [shards(): lax.psum((stem_gradient, kernel_stack, gain_stack, win_stack, wout_stack,...]
    ppermute x56 -> x14, starting transfers between devices: 150 us -> 19.3 us  [permuted(): return lax.ppermute(value, 'gy', pairs)]
    pallas_call x0 -> x3, Pallas kernels: none -> 36.6 us  [the longest x1 32.7 us: shards(): pl.pallas_call(functools.partial(main_kernel, two_rows, 1.0 / math.sqrt(s...]
    dot_general x14 -> x0, matrix products: 13.7 us -> none  [the longest x4 4.76 us: contract_cols(): lax.dot_general(left_side, right_side, (((1,), (1,)), ((), ())), preferre...]
    reduce_sum x11 -> x0, other arithmetic: 10.9 us -> none  [the longest x2 5.46 us: normalize(): average = jnp.mean(conv_out, axis=-1, keepdims=True)]
    unnamed x290 -> x22, local copies, waits for them, and re-layouts: 12.4 us -> 3.8 us
    add x4 -> x2, other arithmetic: 6.16 us -> 0.14 us  [the longest x1 0.1 us: summed_pieces(): total = keep.astype(F32) + crossed(send, 1).astype(F32)]
    mul x8 -> x0, local copies, waits for them, and re-layouts: 4.82 us -> none  [the longest x6 3.72 us: depthwise(): total = total + kernel[row_tap * 7 + col_tap] * window]
  transfers between devices with their start and end apart: 58 -> 14, of which waited for: 8 -> 10; matrix products, arithmetic and copies ran while one was open for 5% -> 3% of each run, Pallas kernels for 0% -> 0%
where the time goes in v1:
time: 86.1 us; the launch traced here: 85.8 us
  Pallas kernels  36.6 us (43%)
  waiting for transfers between devices  23.5 us (27%)
  starting transfers between devices  19.3 us (22%)
  local copies, waits for them, and re-layouts  4.8 us (6%)
    pallas_call x1, Pallas kernels, shards(): pl.pallas_call(functools.partial(main_kernel, two_rows, 1.0 / math.sqrt(s...  32.7 us
    ppermute x14, waiting for transfers between devices, permuted(): return lax.ppermute(value, 'gy', pairs)  23.5 us
    ppermute x14, starting transfers between devices, permuted(): return lax.ppermute(value, 'gy', pairs)  19.3 us
    unnamed x22, local copies, waits for them, and re-layouts  3.8 us
    pallas_call x1, Pallas kernels, shards(): pl.pallas_call(unpack_kernel, out_shape=[jax.ShapeDtypeStruct(array.shape...  2.11 us
    pallas_call x1, Pallas kernels, shards(): pl.pallas_call(prepare_kernel, out_shape=[jax.ShapeDtypeStruct((TH, TW, L...  1.82 us
  transfers between devices with their start and end apart: 14, of which 10 were waited for; matrix products, arithmetic and copies ran while one was open for 3% of the time, Pallas kernels for 0%

profile of v1, /device:TPU:0, one launch (start us, length us, event | category | flops | bytes accessed | tf_op | source)
XLA Modules:
  0.0 85.8 jit_solution(16751194176205121404)
XLA Ops:
  0.6 0.0 copy-start.3
  0.6 1.8 %shard_map.144 = (bf16[16,32,128]{2,1,0:T(8,128)(2,1)}, bf16[16,8,128]{2,1,0:T(8,128)(2,1)}, bf16[16,8,128]{2,1,0:T(8,128)(2,1)}) custom-call(bf16[75,512]{1,0:T(8,128)(2,1)} %bitcast.21, s32[1,512]{1,0:T(1,128)} %ocean_ref.1), custom_call_target="tpu_custom_call" | custom-call | tf_op jit(solution)/shard_map/pallas_call | solution.py:498
  2.5 0.5 collective-permute-start
  2.9 2.9 %collective-permute-start.1 = (bf16[16,8,128]{2,1,0:T(8,128)(2,1)}, bf16[16,8,128]{2,1,0:T(8,128)(2,1)S(1)}, u32[]{:S(2)}, u32[]{:S(2)}) collective-permute-start(bf16[16,8,128]{2,1,0:T(8,128)(2,1)} %get-tuple-element.20), channel_id=1, source_target_pairs={{0,7},{1,0},{2,1},{3,2},{4,3},{5,4},{6,5},{7,6},{8,15},{9,8},{10,9... | collective-permute-start | bytes 98312 | tf_op jit(solution)/shard_map/ppermute | solution.py:451
  5.9 0.0 copy-start.2
  5.9 0.9 %fusion = (bf16[6,32,128]{2,1,0:T(8,128)(2,1)S(1)}, bf16[6,32,128]{2,1,0:T(8,128)(2,1)S(1)}) fusion(bf16[16,32,128]{2,1,0:T(8,128)(2,1)} %get-tuple-element.18.tile_ref), kind=kLoop, calls=%fused_computation.23 | loop fusion | bytes 196608 | tf_op jit(solution)/shard_map/slice | solution.py:515
  6.7 0.0 copy-start.1
  6.7 1.0 %collective-permute-done.1.east_ref = bf16[16,8,128]{2,1,0:T(8,128)(2,1)S(1)} collective-permute-done((bf16[16,8,128]{2,1,0:T(8,128)(2,1)}, bf16[16,8,128]{2,1,0:T(8,128)(2,1)S(1)}, u32[]{:S(2)}, u32[]{:S(2)}) %collective-permute-start.1) | collective-permute-done | bytes 32800 | tf_op jit(solution)/shard_map/ppermute | solution.py:451
  7.8 0.0 collective-permute-done.west_ref
  7.8 0.0 copy-start
  7.8 3.4 %collective-permute-start.2 = (bf16[6,48,128]{2,1,0:T(8,128)(2,1)S(1)}, bf16[6,48,128]{2,1,0:T(8,128)(2,1)S(1)}, u32[]{:S(2)}, u32[]{:S(2)}) collective-permute-start(bf16[6,48,128]{2,1,0:T(8,128)(2,1)S(1)} %get-tuple-element.46), channel_id=1, source_target_pairs={{0,8},{1,9},{2,10},{3,11},{4,12},{5,13},{6,14},{7,15},{8,0},{9,1},... | collective-permute-start | bytes 221192 | tf_op jit(solution)/shard_map/ppermute | solution.py:451
  11.2 0.7 collective-permute-start.3
  11.8 0.0 copy-start.4
  11.9 0.0 copy-start.6
  11.9 0.8 copy.16.dw_ref
  12.7 3.2 %collective-permute-done.2.south_ref.north_ref = bf16[6,48,128]{2,1,0:T(8,128)(2,1)S(1)} collective-permute-done((bf16[6,48,128]{2,1,0:T(8,128)(2,1)S(1)}, bf16[6,48,128]{2,1,0:T(8,128)(2,1)S(1)}, u32[]{:S(2)}, u32[]{:S(2)}) %collective-permute-start.2) | collective-permute-done | bytes 73760 | tf_op jit(solution)/shard_map/ppermute | solution.py:451
  15.8 0.0 collective-permute-done.3.fold_ref
  15.8 0.0 copy-start.5
  15.8 0.0 copy-done.3
  15.9 0.0 copy-done.2
  15.9 0.0 copy-done.1
  15.9 0.0 copy-done
  15.9 0.0 copy-done.4
  15.9 0.0 copy-done.6
  15.9 0.6 copy-done.5
  16.5 32.7 %shard_map.145 = (bf16[16,32,128]{2,1,0:T(8,128)(2,1)}, bf16[2304,128]{1,0:T(8,128)(2,1)S(1)}) custom-call(s32[1]{0:T(128)} %bitcast.top_ref, bf16[16,32,128]{2,1,0:T(8,128)(2,1)S(1)} %copy-done, bf16[16,8,128]{2,1,0:T(8,128)(2,1)S(1)} %collective-permute-done.west_ref, bf16[16,8,128]{2,1,0:T(8,128)(2,1)S(1)} %collective-permute-done.1.east_ref, ...), custom_call_target="tpu_custom_call" | custom-call | tf_op jit(solution)/shard_map/pallas_call | solution.py:532
  49.3 0.1 collective-permute-start.4
  49.4 1.5 %collective-permute-done.4 = bf16[1152,128]{1,0:T(8,128)(2,1)S(1)} collective-permute-done((bf16[1152,128]{1,0:T(8,128)(2,1)S(1)}, bf16[1152,128]{1,0:T(8,128)(2,1)S(1)}, u32[]{:S(2)}, u32[]{:S(2)}) %collective-permute-start.4) | collective-permute-done | bytes 294944 | tf_op jit(solution)/shard_map/ppermute | solution.py:451
  50.9 0.1 convert_add_fusion
  51.1 0.7 collective-permute-start.5
  51.8 5.2 %collective-permute-done.5 = bf16[576,128]{1,0:T(8,128)(2,1)S(1)} collective-permute-done((bf16[576,128]{1,0:T(8,128)(2,1)S(1)}, bf16[576,128]{1,0:T(8,128)(2,1)S(1)}, u32[]{:S(2)}, u32[]{:S(2)}) %collective-permute-start.5) | collective-permute-done | bytes 147488 | tf_op jit(solution)/shard_map/ppermute | solution.py:451
  57.1 4.6 %collective-permute-start.8 = (bf16[144,128]{1,0:T(8,128)(2,1)S(1)}, bf16[144,128]{1,0:T(8,128)(2,1)S(1)}, u32[]{:S(2)}, u32[]{:S(2)}) collective-permute-start(bf16[144,128]{1,0:T(8,128)(2,1)S(1)} %get-tuple-element.39), channel_id=1, source_target_pairs={{0,12},{1,13},{2,14},{3,15},{4,8},{5,9},{6,10},{7,11},{8,4},{9,5},... | collective-permute-start | bytes 110600 | tf_op jit(solution)/shard_map/ppermute | solution.py:451
  61.7 0.0 collective-permute-start.7
  61.7 0.6 collective-permute-start.6
  62.3 1.6 %collective-permute-done.8 = bf16[144,128]{1,0:T(8,128)(2,1)S(1)} collective-permute-done((bf16[144,128]{1,0:T(8,128)(2,1)S(1)}, bf16[144,128]{1,0:T(8,128)(2,1)S(1)}, u32[]{:S(2)}, u32[]{:S(2)}) %collective-permute-start.8) | collective-permute-done | bytes 36896 | tf_op jit(solution)/shard_map/ppermute | solution.py:451
  63.9 2.6 %collective-permute-done.7 = bf16[144,128]{1,0:T(8,128)(2,1)S(1)} collective-permute-done((bf16[144,128]{1,0:T(8,128)(2,1)S(1)}, bf16[144,128]{1,0:T(8,128)(2,1)S(1)}, u32[]{:S(2)}, u32[]{:S(2)}) %collective-permute-start.7) | collective-permute-done | bytes 36896 | tf_op jit(solution)/shard_map/ppermute | solution.py:451
  66.5 0.0 collective-permute-done.6
  66.5 0.1 collective-permute-start.9
  66.6 2.1 %collective-permute-start.10 = (bf16[144,128]{1,0:T(8,128)(2,1)S(1)}, bf16[144,128]{1,0:T(8,128)(2,1)S(1)}, u32[]{:S(2)}, u32[]{:S(2)}) collective-permute-start(bf16[144,128]{1,0:T(8,128)(2,1)S(1)} %get-tuple-element.37), channel_id=1, source_target_pairs={{0,8},{1,9},{2,10},{3,11},{4,12},{5,13},{6,14},{7,15},{8,0},{9,1},... | collective-permute-start | bytes 110600 | tf_op jit(solution)/shard_map/ppermute | solution.py:451
  68.7 2.3 %collective-permute-start.11 = (bf16[144,128]{1,0:T(8,128)(2,1)S(1)}, bf16[144,128]{1,0:T(8,128)(2,1)S(1)}, u32[]{:S(2)}, u32[]{:S(2)}) collective-permute-start(bf16[144,128]{1,0:T(8,128)(2,1)S(1)} %get-tuple-element.37), channel_id=1, source_target_pairs={{0,12},{1,13},{2,14},{3,15},{4,8},{5,9},{6,10},{7,11},{8,4},{9,5},... | collective-permute-start | bytes 110600 | tf_op jit(solution)/shard_map/ppermute | solution.py:451
  71.0 0.0 collective-permute-done.9
  71.0 0.7 collective-permute-done.10
  71.7 2.8 %collective-permute-done.11 = bf16[144,128]{1,0:T(8,128)(2,1)S(1)} collective-permute-done((bf16[144,128]{1,0:T(8,128)(2,1)S(1)}, bf16[144,128]{1,0:T(8,128)(2,1)S(1)}, u32[]{:S(2)}, u32[]{:S(2)}) %collective-permute-start.11) | collective-permute-done | bytes 36896 | tf_op jit(solution)/shard_map/ppermute | solution.py:451
  74.5 1.4 %collective-permute-start.12 = (bf16[4,144,128]{2,1,0:T(8,128)(2,1)S(1)}, bf16[4,144,128]{2,1,0:T(8,128)(2,1)S(1)}, u32[]{:S(2)}, u32[]{:S(2)}) collective-permute-start(bf16[4,144,128]{2,1,0:T(8,128)(2,1)S(1)} %pad_maximum_fusion), channel_id=1, source_target_pairs={{0,2},{1,3},{2,0},{3,1},{4,6},{5,7},{6,4},{7,5},{8,10},{9,11},{10,... | collective-permute-start | bytes 442376 | tf_op jit(solution)/shard_map/ppermute | solution.py:451
  75.9 3.8 %collective-permute-done.12 = bf16[4,144,128]{2,1,0:T(8,128)(2,1)S(1)} collective-permute-done((bf16[4,144,128]{2,1,0:T(8,128)(2,1)S(1)}, bf16[4,144,128]{2,1,0:T(8,128)(2,1)S(1)}, u32[]{:S(2)}, u32[]{:S(2)}) %collective-permute-start.12) | collective-permute-done | bytes 147488 | tf_op jit(solution)/shard_map/ppermute | solution.py:451
  79.7 0.1 constant_dynamic-update-slice_fusion
  79.8 0.1 collective-permute-start.13
  79.9 0.5 iota_xor_fusion.order_ref
  80.4 1.0 %collective-permute-done.13 = bf16[8,144,128]{2,1,0:T(8,128)(2,1)S(1)} collective-permute-done((bf16[8,144,128]{2,1,0:T(8,128)(2,1)S(1)}, bf16[8,144,128]{2,1,0:T(8,128)(2,1)S(1)}, u32[]{:S(2)}, u32[]{:S(2)}) %collective-permute-start.13) | collective-permute-done | bytes 294944 | tf_op jit(solution)/shard_map/ppermute | solution.py:451
  81.5 0.0 copy-start.7
  81.5 0.8 copy-done.7
  82.3 2.1 %shard_map.146 = (f32[75,128]{1,0:T(8,128)}, f32[2,49,128]{2,1,0:T(8,128)}, f32[2,128]{1,0:T(2,128)}, f32[2,128,512]{2,1,0:T(8,128)}, f32[2,512,128]{2,1,0:T(8,128)}, /*index=5*/f32[2,128]{1,0:T(2,128)}) custom-call(s32[16]{0:T(128)} %iota_xor_fusion.order_ref, bf16[16,144,128]{2,1,0:T(8,128)(2,1)} %copy-done.7), custom_call_target="tpu_custom_call" | custom-call | tf_op jit(solution)/shard_map/pallas_call | solution.py:594
  84.4 1.5 %copy.17 = f32[2,49,128]{2,0,1:T(2,128)} copy(f32[2,49,128]{2,1,0:T(8,128)} %get-tuple-element.31) | data formatting | bytes 100352
  (14 shorter events, 0.3 us)
Async XLA Ops:
  0.6 15.2 %copy-start.3 = (bf16[1,512,128]{2,1,0:T(8,128)(2,1)S(1)}, bf16[1,512,128]{2,1,0:T(8,128)(2,1)}, u32[]{:S(2)}) copy-start(bf16[1,512,128]{2,1,0:T(8,128)(2,1)} %param.17) | copy-start | bytes 393220
  2.5 5.3 %collective-permute-start = (bf16[16,8,128]{2,1,0:T(8,128)(2,1)}, bf16[16,8,128]{2,1,0:T(8,128)(2,1)S(1)}, u32[]{:S(2)}, u32[]{:S(2)}) collective-permute-start(bf16[16,8,128]{2,1,0:T(8,128)(2,1)} %get-tuple-element.19), channel_id=1, source_target_pairs={{0,1},{1,2},{2,3},{3,4},{4,5},{5,6},{6,7},{7,0},{8,9},{9,10},{10,1... | collective-permute-start | bytes 98312 | tf_op jit(solution)/shard_map/ppermute | solution.py:451
  2.9 4.9 %collective-permute-start.1 = (bf16[16,8,128]{2,1,0:T(8,128)(2,1)}, bf16[16,8,128]{2,1,0:T(8,128)(2,1)S(1)}, u32[]{:S(2)}, u32[]{:S(2)}) collective-permute-start(bf16[16,8,128]{2,1,0:T(8,128)(2,1)} %get-tuple-element.20), channel_id=1, source_target_pairs={{0,7},{1,0},{2,1},{3,2},{4,3},{5,4},{6,5},{7,6},{8,15},{9,8},{10,9... | collective-permute-start | bytes 98312 | tf_op jit(solution)/shard_map/ppermute | solution.py:451
  5.9 10.0 %copy-start.2 = (bf16[2,512,128]{2,1,0:T(8,128)(2,1)S(1)}, bf16[2,512,128]{2,1,0:T(8,128)(2,1)}, u32[]{:S(2)}) copy-start(bf16[2,512,128]{2,1,0:T(8,128)(2,1)} %wout_ref.1) | copy-start | bytes 786436
  6.7 9.1 %copy-start.1 = (bf16[2,128,512]{2,1,0:T(8,128)(2,1)S(1)}, bf16[2,128,512]{2,1,0:T(8,128)(2,1)}, u32[]{:S(2)}) copy-start(bf16[2,128,512]{2,1,0:T(8,128)(2,1)} %win_ref.1) | copy-start | bytes 786436
  7.8 8.1 %copy-start = (bf16[16,32,128]{2,1,0:T(8,128)(2,1)S(1)}, bf16[16,32,128]{2,1,0:T(8,128)(2,1)}, u32[]{:S(2)}) copy-start(bf16[16,32,128]{2,1,0:T(8,128)(2,1)} %get-tuple-element.18.tile_ref) | copy-start | bytes 393220
  7.8 8.0 %collective-permute-start.2 = (bf16[6,48,128]{2,1,0:T(8,128)(2,1)S(1)}, bf16[6,48,128]{2,1,0:T(8,128)(2,1)S(1)}, u32[]{:S(2)}, u32[]{:S(2)}) collective-permute-start(bf16[6,48,128]{2,1,0:T(8,128)(2,1)S(1)} %get-tuple-element.46), channel_id=1, source_target_pairs={{0,8},{1,9},{2,10},{3,11},{4,12},{5,13},{6,14},{7,15},{8,0},{9,1},... | collective-permute-start | bytes 221192 | tf_op jit(solution)/shard_map/ppermute | solution.py:451
  11.2 4.7 %collective-permute-start.3 = (bf16[6,48,128]{2,1,0:T(8,128)(2,1)S(1)}, bf16[6,48,128]{2,1,0:T(8,128)(2,1)S(1)}, u32[]{:S(2)}, u32[]{:S(2)}) collective-permute-start(bf16[6,48,128]{2,1,0:T(8,128)(2,1)S(1)} %get-tuple-element.45), channel_id=1, source_target_pairs={{8,15},{9,14},{10,13},{11,12},{12,11},{13,10},{14,9},{15,8},{24,31... | collective-permute-start | bytes 221192 | tf_op jit(solution)/shard_map/ppermute | solution.py:451
  11.8 4.0 %copy-start.4 = (bf16[75,128]{1,0:T(8,128)(2,1)S(1)}, bf16[75,128]{1,0:T(8,128)(2,1)}, u32[]{:S(2)}) copy-start(bf16[75,128]{1,0:T(8,128)(2,1)} %stem_ref.1) | copy-start | bytes 57604
  11.9 4.0 %copy-start.6 = (f32[2,128]{1,0:T(2,128)S(1)}, f32[2,128]{1,0:T(2,128)}, u32[]{:S(2)}) copy-start(f32[2,128]{1,0:T(2,128)} %scale_ref.1) | copy-start | bytes 3076
  15.8 0.7 copy-start.5
  49.3 1.6 %collective-permute-start.4 = (bf16[1152,128]{1,0:T(8,128)(2,1)S(1)}, bf16[1152,128]{1,0:T(8,128)(2,1)S(1)}, u32[]{:S(2)}, u32[]{:S(2)}) collective-permute-start(bf16[1152,128]{1,0:T(8,128)(2,1)S(1)} %broadcast_select_fusion), channel_id=1, source_target_pairs={{0,1},{1,0},{2,3},{3,2},{4,5},{5,4},{6,7},{7,6},{8,9},{9,8},{10,11... | collective-permute-start | bytes 884744 | tf_op jit(solution)/shard_map/ppermute | solution.py:451
  51.1 6.0 %collective-permute-start.5 = (bf16[576,128]{1,0:T(8,128)(2,1)S(1)}, bf16[576,128]{1,0:T(8,128)(2,1)S(1)}, u32[]{:S(2)}, u32[]{:S(2)}) collective-permute-start(bf16[576,128]{1,0:T(8,128)(2,1)S(1)} %select_convert_fusion), channel_id=1, source_target_pairs={{0,2},{1,3},{2,0},{3,1},{4,6},{5,7},{6,4},{7,5},{8,10},{9,11},{10,... | collective-permute-start | bytes 442376 | tf_op jit(solution)/shard_map/ppermute | solution.py:451
  57.1 6.9 %collective-permute-start.8 = (bf16[144,128]{1,0:T(8,128)(2,1)S(1)}, bf16[144,128]{1,0:T(8,128)(2,1)S(1)}, u32[]{:S(2)}, u32[]{:S(2)}) collective-permute-start(bf16[144,128]{1,0:T(8,128)(2,1)S(1)} %get-tuple-element.39), channel_id=1, source_target_pairs={{0,12},{1,13},{2,14},{3,15},{4,8},{5,9},{6,10},{7,11},{8,4},{9,5},... | collective-permute-start | bytes 110600 | tf_op jit(solution)/shard_map/ppermute | solution.py:451
  61.7 4.9 %collective-permute-start.7 = (bf16[144,128]{1,0:T(8,128)(2,1)S(1)}, bf16[144,128]{1,0:T(8,128)(2,1)S(1)}, u32[]{:S(2)}, u32[]{:S(2)}) collective-permute-start(bf16[144,128]{1,0:T(8,128)(2,1)S(1)} %get-tuple-element.40), channel_id=1, source_target_pairs={{0,8},{1,9},{2,10},{3,11},{4,12},{5,13},{6,14},{7,15},{8,0},{9,1},... | collective-permute-start | bytes 110600 | tf_op jit(solution)/shard_map/ppermute | solution.py:451
  61.7 4.9 %collective-permute-start.6 = (bf16[144,128]{1,0:T(8,128)(2,1)S(1)}, bf16[144,128]{1,0:T(8,128)(2,1)S(1)}, u32[]{:S(2)}, u32[]{:S(2)}) collective-permute-start(bf16[144,128]{1,0:T(8,128)(2,1)S(1)} %get-tuple-element.38), channel_id=1, source_target_pairs={{0,4},{1,5},{2,6},{3,7},{4,0},{5,1},{6,2},{7,3},{8,12},{9,13},{10,... | collective-permute-start | bytes 110600 | tf_op jit(solution)/shard_map/ppermute | solution.py:451
  66.5 4.5 %collective-permute-start.9 = (bf16[144,128]{1,0:T(8,128)(2,1)S(1)}, bf16[144,128]{1,0:T(8,128)(2,1)S(1)}, u32[]{:S(2)}, u32[]{:S(2)}) collective-permute-start(bf16[144,128]{1,0:T(8,128)(2,1)S(1)} %get-tuple-element.37), channel_id=1, source_target_pairs={{0,4},{1,5},{2,6},{3,7},{4,0},{5,1},{6,2},{7,3},{8,12},{9,13},{10,... | collective-permute-start | bytes 110600 | tf_op jit(solution)/shard_map/ppermute | solution.py:451
  66.6 5.0 %collective-permute-start.10 = (bf16[144,128]{1,0:T(8,128)(2,1)S(1)}, bf16[144,128]{1,0:T(8,128)(2,1)S(1)}, u32[]{:S(2)}, u32[]{:S(2)}) collective-permute-start(bf16[144,128]{1,0:T(8,128)(2,1)S(1)} %get-tuple-element.37), channel_id=1, source_target_pairs={{0,8},{1,9},{2,10},{3,11},{4,12},{5,13},{6,14},{7,15},{8,0},{9,1},... | collective-permute-start | bytes 110600 | tf_op jit(solution)/shard_map/ppermute | solution.py:451
  68.7 5.8 %collective-permute-start.11 = (bf16[144,128]{1,0:T(8,128)(2,1)S(1)}, bf16[144,128]{1,0:T(8,128)(2,1)S(1)}, u32[]{:S(2)}, u32[]{:S(2)}) collective-permute-start(bf16[144,128]{1,0:T(8,128)(2,1)S(1)} %get-tuple-element.37), channel_id=1, source_target_pairs={{0,12},{1,13},{2,14},{3,15},{4,8},{5,9},{6,10},{7,11},{8,4},{9,5},... | collective-permute-start | bytes 110600 | tf_op jit(solution)/shard_map/ppermute | solution.py:451
  74.5 5.2 %collective-permute-start.12 = (bf16[4,144,128]{2,1,0:T(8,128)(2,1)S(1)}, bf16[4,144,128]{2,1,0:T(8,128)(2,1)S(1)}, u32[]{:S(2)}, u32[]{:S(2)}) collective-permute-start(bf16[4,144,128]{2,1,0:T(8,128)(2,1)S(1)} %pad_maximum_fusion), channel_id=1, source_target_pairs={{0,2},{1,3},{2,0},{3,1},{4,6},{5,7},{6,4},{7,5},{8,10},{9,11},{10,... | collective-permute-start | bytes 442376 | tf_op jit(solution)/shard_map/ppermute | solution.py:451
  79.8 1.6 %collective-permute-start.13 = (bf16[8,144,128]{2,1,0:T(8,128)(2,1)S(1)}, bf16[8,144,128]{2,1,0:T(8,128)(2,1)S(1)}, u32[]{:S(2)}, u32[]{:S(2)}) collective-permute-start(bf16[8,144,128]{2,1,0:T(8,128)(2,1)S(1)} %get-tuple-element.41), channel_id=1, source_target_pairs={{0,1},{1,0},{2,3},{3,2},{4,5},{5,4},{6,7},{7,6},{8,9},{9,8},{10,11... | collective-permute-start | bytes 884744 | tf_op jit(solution)/shard_map/ppermute | solution.py:451
  81.5 0.8 copy-start.7

commit v2 on v1

v2 whole, which is shorter than its diff:
```python
import functools
import math

import jax
import jax.numpy as jnp
from jax import lax
from jax.experimental import pallas as pl
from jax.experimental.pallas import tpu as pltpu
from jax.sharding import PartitionSpec as P

TH = 16
TW = 32
TX = 8
LANES = 128

RIM = 6
PADC = 8
EH, EW = TH + 2 * RIM, TW + 2 * PADC
RH, RW = TH + 6, 40
RING_COL = 5

C0 = 0.7978845608028654
C1 = 0.7978845608028654 * 0.044715
NORM_STABILIZER = 1e-06

WIN_ROW, WOUT_ROW, SMALL_ROW = 0, 1024, 2048
STEM_AT, KERNEL_AT, GAIN_AT, SCALE_AT = 0, (80, 136), 192, 194
SMALL_ROWS = 256
PACKED = SMALL_ROW + SMALL_ROWS

BF = jnp.bfloat16
F32 = jnp.float32


def vmem(count):
    return [pl.BlockSpec(memory_space=pltpu.VMEM)] * count


def smem():
    return pl.BlockSpec(memory_space=pltpu.SMEM)


def contract_rows(left, right):
    return lax.dot_general(left, right, (((0,), (0,)), ((), ())), preferred_element_type=F32)


def contract_cols(left, right):
    return lax.dot_general(left, right, (((1,), (1,)), ((), ())), preferred_element_type=F32)


def prepare_kernel(top_ref, levels_ref, ocean_ref, tile_ref, strip_ref, fold_ref, stage):
    count, cells = levels_ref.shape
    stage[...] = jnp.zeros_like(stage)
    stage[0:count, :] = levels_ref[...].astype(F32)
    stage[count : count + 1, :] = ocean_ref[...].astype(F32)
    rows = lax.broadcasted_iota(jnp.int32, (LANES, LANES), 0)
    cols = lax.broadcasted_iota(jnp.int32, (LANES, LANES), 1)
    eye = (rows == cols).astype(BF)
    turned = contract_rows(stage[...].astype(BF), eye)
    tile_ref[...] = turned.reshape(TH, TW, LANES).astype(BF)
    side = RIM * TW
    lower, upper = turned[0:side], turned[cells - side :]
    strip_ref[...] = jnp.where(top_ref[0] == 1, lower, upper).reshape(RIM, TW, LANES).astype(BF)
    rows = lax.broadcasted_iota(jnp.int32, (side, side), 0)
    cols = lax.broadcasted_iota(jnp.int32, (side, side), 1)
    swap = (rows + cols == side - 1).astype(BF)
    fold_ref[...] = jnp.dot(swap, upper.astype(BF), preferred_element_type=F32).reshape(RIM, TW, LANES).astype(BF)


def load_column(ref, row, start):
    return ref[row, pl.ds(start, 8), :]


def conv_block(ref, taps, start, out_rows, in_rows, taps_of):
    totals = {o: None for o in out_rows}
    needed = sorted({o + a for o in out_rows for a in range(7) if o + a in in_rows})
    for d in range(7):
        column = {r: load_column(ref, r - in_rows.start, start + d) for r in needed}
        for a in range(7):
            held = {}
            for o in out_rows:
                r = o + a
                if r not in column:
                    continue
                which, index = taps_of(o, r, a, d)
                if (which, index) not in held:
                    held[(which, index)] = taps[which][index]
                term = held[(which, index)] * column[r]
                totals[o] = term if totals[o] is None else totals[o] + term
    return totals


def main_kernel(
    rescale,
    top_ref,
    tile_ref,
    west_ref,
    east_ref,
    south_ref,
    north_ref,
    stem_hbm,
    dw_hbm,
    gain_hbm,
    win_hbm,
    wout_hbm,
    scale_hbm,
    up_hbm,
    out_ref,
    packed_ref,
    ext,
    x0,
    m6,
    x1,
    weights,
    taps0,
    taps0n,
    taps1,
    conv0,
    xhat0,
    rinv0,
    branch0,
    normed0,
    act0,
    slope0,
    conv1,
    xhat1,
    rinv1,
    branch1,
    normed1,
    act1,
    slope1,
    wide,
    thin,
    gpre,
    pad0,
    pad1,
    g1,
    h0,
    gk0,
    gk0n,
    gk1,
    small,
    stem_ref,
    dw_ref,
    gain_ref,
    win_ref,
    wout_ref,
    scale_ref,
    up_ref,
    arrived,
):
    top = top_ref[0] == 1
    levels_count = stem_ref.shape[0]
    count0, count1 = RH * RW, TH * TW

    loads = [
        pltpu.make_async_copy(source, target, arrived.at[index])
        for index, (source, target) in enumerate(
            (
                (stem_hbm, stem_ref),
                (dw_hbm, dw_ref),
                (gain_hbm, gain_ref),
                (win_hbm, win_ref),
                (wout_hbm, wout_ref),
                (scale_hbm, scale_ref),
                (up_hbm, up_ref),
            )
        )
    ]
    for load in loads:
        load.start()

    ext[0:RIM, PADC : PADC + TW] = south_ref[...].astype(F32)
    ext[RIM : RIM + TH, PADC : PADC + TW] = tile_ref[...].astype(F32)
    ext[RIM + TH :, PADC : PADC + TW] = north_ref[...].astype(F32)
    ext[:, 0:PADC] = west_ref[...].astype(F32)
    ext[:, PADC + TW :] = east_ref[...].astype(F32)

    weights[...] = jnp.zeros_like(weights)
    loads[0].wait()
    weights[0:levels_count, 0:LANES] = stem_ref[...].astype(F32)
    weights[levels_count : levels_count + 1, LANES:] = jnp.ones((1, LANES), F32)
    joint = weights[...].astype(BF)

    for index in range(EH // 4):
        at = slice(index * 4, index * 4 + 4)
        both = jnp.dot(
            ext[at].reshape(4 * EW, LANES).astype(BF), joint, preferred_element_type=F32
        )
        mask = both[:, LANES:]
        m6[at] = mask.reshape(4, EW, LANES)
        x0[at] = (mask * both[:, :LANES]).astype(BF).astype(F32).reshape(4, EW, LANES)

    for load in loads[1:]:
        load.wait()
    for t in range(49):
        first = dw_ref[t, 0:1, :]
        turned = dw_ref[48 - t, 0:1, :]
        taps0[t] = jnp.broadcast_to(first, (8, LANES))
        taps0n[t] = jnp.broadcast_to(jnp.where(top, turned, first), (8, LANES))
        taps1[t] = jnp.broadcast_to(dw_ref[t, 1:2, :], (8, LANES))

    north_at = 3 + TH

    def conv0_block(block, _):
        start = pl.multiple_of(block * 8, 8)
        for rows in (range(0, 19), range(19, 22)):
            totals = conv_block(
                x0,
                (taps0, taps0n),
                start + 2,
                rows,
                range(0, EH),
                lambda o, r, a, d: (1 if o >= north_at else 0, a * 7 + d),
            )
            for o in rows:
                conv0[pl.ds(pl.multiple_of(o * RW + start, 8), 8), :] = totals[o]
        return 0

    lax.fori_loop(0, RW // 8, conv0_block, 0)

    def chunks(count, size, body):
        def run(carry):
            for index in range(count // size):
                carry = body(index, slice(index * size, index * size + size), carry)
            return carry

        return run

    def norm_rows(conv, xhat, rinv, normed, gain, count, size):
        def step(index, at, _):
            values = conv[at, :]
            average = jnp.mean(values, axis=-1, keepdims=True)
            centered = values - average
            inverse = lax.rsqrt(jnp.mean(centered * centered, axis=-1, keepdims=True) + NORM_STABILIZER)
            scaled = centered * inverse
            xhat[at, :] = scaled
            rinv[at, :] = jnp.broadcast_to(inverse, (size, LANES))
            normed[at, :] = (scaled * gain).astype(BF)
            return 0

        chunks(count, size, step)(0)

    def gelu_rows(pre, act, slope, count, size):
        def step(index, at, _):
            for part in range(size // 16):
                here = slice(index * size + part * 16, index * size + part * 16 + 16)
                v = pre[here, :]
                square = v * v
                inner = v * (C0 + C1 * square)
                half = 0.5 * jnp.tanh(inner) + 0.5
                active = v * half
                act[here, :] = active.astype(BF)
                slope[here, :] = half + active * (1.0 - half) * (2.0 * C0 + (6.0 * C1) * square)
            return 0

        chunks(count, size, step)(0)

    norm_rows(conv0, xhat0, rinv0, normed0, gain_ref[0:1, :], count0, 80)
    wide[0:count0] = jnp.dot(normed0[...], win_ref[0], preferred_element_type=F32)
    gelu_rows(wide, act0, slope0, count0, 80)
    branch0[...] = jnp.dot(act0[...], wout_ref[0], preferred_element_type=F32)

    def next0(index, at, _):
        rows = pl.ds(index * 2 + 3, 2)
        mask = m6[rows, RING_COL : RING_COL + RW, :]
        held = x0[rows, RING_COL : RING_COL + RW, :]
        branch = branch0[at, :].reshape(2, RW, LANES)
        x1[pl.ds(index * 2, 2)] = (mask * (held + scale_ref[0:1, :] * branch)).astype(BF).astype(F32)
        return 0

    chunks(count0, 2 * RW, next0)(0)

    def conv1_block(block, _):
        start = pl.multiple_of(block * 8, 8)
        for rows in (range(0, 16),):
            totals = conv_block(
                x1, (taps1,), start, rows, range(0, RH), lambda o, r, a, d: (0, a * 7 + d)
            )
            for o in rows:
                conv1[pl.ds(pl.multiple_of(o * TW + start, 8), 8), :] = totals[o]
        return 0

    lax.fori_loop(0, TW // 8, conv1_block, 0)
    norm_rows(conv1, xhat1, rinv1, normed1, gain_ref[1:2, :], count1, 64)
    wide[0:count1] = jnp.dot(normed1[...], win_ref[1], preferred_element_type=F32)
    gelu_rows(wide, act1, slope1, count1, 64)
    branch1[...] = jnp.dot(act1[...], wout_ref[1], preferred_element_type=F32)

    small[...] = jnp.zeros_like(small)
    g1[...] = jnp.zeros_like(g1)

    def folded(value):
        return jnp.sum(value.reshape(-1, 8, LANES), axis=0)

    def next1(index, at, total):
        rows = 2
        mask = m6[pl.ds(index * rows + RIM, rows), PADC : PADC + TW, :]
        held = x1[pl.ds(index * rows + 3, rows), 3 : 3 + TW, :]
        branch = branch1[at, :].reshape(rows, TW, LANES)
        out_ref[at, :] = (mask * (held + scale_ref[1:2, :] * branch)).astype(BF).reshape(rows * TW, LANES)
        masked = mask * (up_ref[at, :].astype(F32) * rescale).reshape(rows, TW, LANES)
        g1[pl.ds(index * rows + 3, rows), 3 : 3 + TW, :] = masked
        thin[at, :] = (masked * scale_ref[1:2, :]).reshape(rows * TW, LANES).astype(BF)
        return total + folded(masked * branch)

    total = chunks(count1, 2 * TW, next1)(jnp.zeros((8, LANES), F32))
    small[SCALE_AT + 1 : SCALE_AT + 2, :] = jnp.sum(total, axis=0, keepdims=True)

    def grad_wout(layer, count, act):
        packed_ref[WOUT_ROW + 512 * layer : WOUT_ROW + 512 * layer + 512, :] = contract_rows(
            act[...], thin[0:count]
        ).astype(BF)

    def grad_pre(layer, count, size, slope):
        wide[0:count] = contract_cols(thin[0:count], wout_ref[layer])

        def step(index, at, _):
            for part in range(size // 16):
                here = slice(index * size + part * 16, index * size + part * 16 + 16)
                gpre[here, :] = (wide[here, :] * slope[here, :]).astype(BF)
            return 0

        chunks(count, size, step)(0)

    def grad_win(layer, count, normed):
        gp = gpre[0:count]
        grad_in = contract_rows(normed[...], gp).astype(BF)
        for part in range(4):
            at = WIN_ROW + 512 * layer + 128 * part
            packed_ref[at : at + 128, :] = grad_in[:, 128 * part : 128 * part + 128]
        wide[0:count, 0:LANES] = contract_cols(gp, win_ref[layer])

    def grad_conv(layer, count, shape, xhat, rinv, pad):
        rows, width = shape
        gain = gain_ref[layer : layer + 1, :]

        def step(index, at, total):
            gn = wide[at, 0:LANES]
            scaled = xhat[at, :]
            gx = gn * gain
            first = jnp.mean(gx, axis=-1, keepdims=True)
            second = jnp.mean(gx * scaled, axis=-1, keepdims=True)
            value = (rinv[at, :] * (gx - first - scaled * second)).astype(BF).astype(F32)
            pad[pl.ds(index * rows, rows), PADC : PADC + width, :] = value.reshape(rows, width, LANES)
            return total + folded(gn * scaled)

        total = chunks(count, rows * width, step)(jnp.zeros((8, LANES), F32))
        small[GAIN_AT + layer : GAIN_AT + layer + 1, :] = jnp.sum(total, axis=0, keepdims=True)

    pad1[...] = jnp.zeros_like(pad1)
    grad_wout(1, count1, act1)
    grad_pre(1, count1, 64, slope1)
    grad_win(1, count1, normed1)
    grad_conv(1, count1, (2, TW), xhat1, rinv1, pad1)

    gk1[...] = jnp.zeros_like(gk1)

    def kernel1_block(block, _):
        start = pl.multiple_of(block * 8, 8)
        grads = [pad1[j, pl.ds(start + PADC, 8), :] for j in range(TH)]
        for d in range(7):
            column = [load_column(x1, r, start + d) for r in range(RH)]
            for a in range(7):
                total = gk1[a * 7 + d]
                for j in range(TH):
                    total = total + grads[j] * column[j + a]
                gk1[a * 7 + d] = total
        return 0

    lax.fori_loop(0, TW // 8, kernel1_block, 0)

    def back1_block(block, _):
        start = pl.multiple_of(block * 8, 8)
        for rows in (range(0, 22),):
            totals = conv_block(
                pad1, (taps1,), start + 2, rows, range(6, 6 + TH), lambda o, r, a, d: (0, 48 - (a * 7 + d))
            )
            for o in rows:
                g1[o, pl.ds(start, 8), :] += totals[o]
        return 0

    lax.fori_loop(0, RW // 8, back1_block, 0)

    def masked0(index, at, total):
        rows = pl.ds(index * 2, 2)
        masked = m6[pl.ds(index * 2 + 3, 2), RING_COL : RING_COL + RW, :] * g1[rows]
        g1[rows] = masked
        flat = masked.reshape(2 * RW, LANES)
        thin[at, :] = (flat * scale_ref[0:1, :]).astype(BF)
        return total + folded(flat * branch0[at, :])

    total = chunks(count0, 2 * RW, masked0)(jnp.zeros((8, LANES), F32))
    small[SCALE_AT : SCALE_AT + 1, :] = jnp.sum(total, axis=0, keepdims=True)
    pad0[...] = jnp.zeros_like(pad0)
    grad_wout(0, count0, act0)
    grad_pre(0, count0, 80, slope0)
    grad_win(0, count0, normed0)
    grad_conv(0, count0, (2, RW), xhat0, rinv0, pad0)

    gk0[...] = jnp.zeros_like(gk0)
    gk0n[...] = jnp.zeros_like(gk0n)

    def kernel0_block(block, _):
        start = pl.multiple_of(block * 8, 8)
        grads = [pad0[j, pl.ds(start + PADC, 8), :] for j in range(RH)]
        for d in range(7):
            column = [load_column(x0, r, start + 2 + d) for r in range(EH)]
            for a in range(7):
                total = gk0[a * 7 + d]
                for j in range(north_at):
                    total = total + grads[j] * column[j + a]
                gk0[a * 7 + d] = total
                total = gk0n[a * 7 + d]
                for j in range(north_at, RH):
                    total = total + grads[j] * column[j + a]
                gk0n[a * 7 + d] = total
        return 0

    lax.fori_loop(0, RW // 8, kernel0_block, 0)
    for t in range(49):
        north = jnp.where(top, gk0n[48 - t], gk0n[t])
        small[KERNEL_AT[0] + t : KERNEL_AT[0] + t + 1, :] = jnp.sum(gk0[t] + north, axis=0, keepdims=True)
        small[KERNEL_AT[1] + t : KERNEL_AT[1] + t + 1, :] = jnp.sum(gk1[t], axis=0, keepdims=True)

    def back0_block(block, _):
        start = pl.multiple_of(block * 8, 8)
        for rows in (range(0, 14), range(14, 28)):
            totals = conv_block(
                pad0,
                (taps0, taps0n),
                start,
                rows,
                range(6, 6 + RH),
                lambda o, r, a, d: (1 if r - 6 >= north_at else 0, 48 - (a * 7 + d)),
            )
            for o in rows:
                h0[o, pl.ds(start, 8), :] = totals[o]
        return 0

    lax.fori_loop(0, EW // 8, back0_block, 0)
    def carry0(index, _):
        h0[pl.ds(index * 2 + 3, 2), RING_COL : RING_COL + RW, :] += g1[pl.ds(index * 2, 2)]
        return 0

    lax.fori_loop(0, RH // 2, carry0, 0)
    stem_side = (m6[...].reshape(EH * EW, LANES) * h0[...].reshape(EH * EW, LANES)).astype(BF)
    stem_grad = contract_rows(ext[...].reshape(EH * EW, LANES).astype(BF), stem_side)
    small[STEM_AT : STEM_AT + 80, :] = stem_grad[0:80, :]
    packed_ref[SMALL_ROW : SMALL_ROW + SMALL_ROWS, :] = small[...].astype(BF)


def unpack_kernel(order_ref, pieces_ref, stem_ref, kernel_ref, gain_ref, win_ref, wout_ref, scale_ref, rows):
    count, size = pieces_ref.shape[0], pieces_ref.shape[1]
    for index in range(count):
        rows[index * size : (index + 1) * size, :] = pieces_ref[order_ref[index]].astype(F32)
    for layer in range(2):
        for part in range(4):
            at = WIN_ROW + 512 * layer + 128 * part
            win_ref[layer, :, 128 * part : 128 * part + 128] = rows[at : at + 128, :]
        at = WOUT_ROW + 512 * layer
        wout_ref[layer] = rows[at : at + 512, :]
        at = SMALL_ROW + KERNEL_AT[layer]
        kernel_ref[:, layer, :] = rows[at : at + 49, :]
    at = SMALL_ROW + STEM_AT
    stem_ref[...] = rows[at : at + stem_ref.shape[0], :]
    gain_ref[...] = rows[SMALL_ROW + GAIN_AT : SMALL_ROW + GAIN_AT + 2, :]
    scale_ref[...] = rows[SMALL_ROW + SCALE_AT : SMALL_ROW + SCALE_AT + 2, :]


def permuted(value, pairs):
    return lax.ppermute(value, "gy", pairs)


def crossed(value, bits):
    return permuted(value, [(i, i ^ bits) for i in range(lax.axis_size("gy"))])


def summed_pieces(packed):
    size = lax.axis_size("gy")
    if size != 16:
        return lax.psum(packed.astype(F32), "gy").astype(BF)[None], jnp.zeros((1,), jnp.int32)
    me = lax.axis_index("gy")
    core, side, deep = me & 1, (me >> 1) & 1, me >> 2

    def halves(value, bit):
        half = value.shape[0] // 2
        low, high = value[:half], value[half:]
        return jnp.where(bit == 0, low, high), jnp.where(bit == 0, high, low)

    keep, send = halves(packed, core)
    total = keep.astype(F32) + crossed(send, 1).astype(F32)
    keep, send = halves(total, side)
    total = keep + crossed(send.astype(BF), 2).astype(F32)
    quarter = total.shape[0] // 4

    def shard(step):
        return lax.dynamic_slice_in_dim(total, (deep ^ step) * quarter, quarter, 0)

    arrived = [crossed(shard(step).astype(BF), 4 * step) for step in (1, 2, 3)]
    mine = shard(0)
    for other in arrived:
        mine = mine + other.astype(F32)
    mine = mine.astype(BF)
    pieces = jnp.stack([mine] + [crossed(mine, 4 * step) for step in (1, 2, 3)])
    pieces = jnp.concatenate([pieces, crossed(pieces, 2)], axis=0)
    pieces = jnp.concatenate([pieces, crossed(pieces, 1)], axis=0)
    index = jnp.arange(16, dtype=jnp.int32)
    mixed = (core << 3) | (side << 2) | deep
    return pieces, index ^ mixed.astype(jnp.int32)


def shards(levels, ocean, stem, dw_kernel, ln_gain, w_in, w_out, layer_scale, upstream):
    size = lax.axis_size("gy")
    rows = size // TX
    me = lax.axis_index("gy")
    is_top = me // TX == rows - 1
    count = levels.shape[2]
    top = is_top.astype(jnp.int32)[None]
    tile, strip, folded = pl.pallas_call(
        prepare_kernel,
        out_shape=[
            jax.ShapeDtypeStruct((TH, TW, LANES), BF),
            jax.ShapeDtypeStruct((RIM, TW, LANES), BF),
            jax.ShapeDtypeStruct((RIM, TW, LANES), BF),
        ],
        in_specs=[smem()] + vmem(2),
        out_specs=vmem(3),
        scratch_shapes=[pltpu.VMEM((LANES, count), F32)],
        compiler_params=pltpu.CompilerParams(vmem_limit_bytes=4 << 20),
    )(top, levels[0], ocean)
    if rows == 2:
        south = north = permuted(strip, [(i, (i + TX) % size) for i in range(size)])
        south = jnp.where(is_top, south, jnp.zeros_like(south))
    else:
        south = permuted(tile[-RIM:], [(i, i + TX) for i in range(size - TX)])
        north = permuted(tile[:RIM], [(i + TX, i) for i in range(size - TX)])
    folded = permuted(folded, [(i, i // TX * TX + TX - 1 - i % TX) for i in range(size - TX, size)])
    north = jnp.where(is_top, folded, north)

    def columns(at):
        return jnp.concatenate([south[:, at], tile[:, at], north[:, at]], axis=0)

    def column_pairs(step):
        return [(i, i // TX * TX + (i % TX + step) % TX) for i in range(size)]

    west = permuted(columns(slice(TW - PADC, TW)), column_pairs(1))
    east = permuted(columns(slice(0, PADC)), column_pairs(-1))

    def scratch(*shape, dtype=F32):
        return pltpu.VMEM(shape, dtype)

    count0 = RH * RW
    hidden = w_in.shape[2]
    result, packed = pl.pallas_call(
        functools.partial(main_kernel, 1.0 / math.sqrt(size * count)),
        out_shape=[
            jax.ShapeDtypeStruct((count, LANES), BF),
            jax.ShapeDtypeStruct((PACKED, LANES), BF),
        ],
        in_specs=[smem()] + vmem(5) + [pl.BlockSpec(memory_space=pltpu.HBM)] * 7,
        out_specs=vmem(2),
        scratch_shapes=[
            scratch(EH, EW, LANES),
            scratch(EH, EW, LANES),
            scratch(EH, EW, LANES),
            scratch(RH, RW, LANES),
            scratch(LANES, 2 * LANES),
            scratch(49, 8, LANES),
            scratch(49, 8, LANES),
            scratch(49, 8, LANES),
            scratch(count0, LANES),
            scratch(count0, LANES),
            scratch(count0, LANES),
            scratch(count0, LANES),
            scratch(count0, LANES, dtype=BF),
            scratch(count0, hidden, dtype=BF),
            scratch(count0, hidden),
            scratch(count, LANES),
            scratch(count, LANES),
            scratch(count, LANES),
            scratch(count, LANES),
            scratch(count, LANES, dtype=BF),
            scratch(count, hidden, dtype=BF),
            scratch(count, hidden),
            scratch(count0, hidden),
            scratch(count0, LANES, dtype=BF),
            scratch(count0, hidden, dtype=BF),
            scratch(RH, EW + 8, LANES),
            scratch(TH, EW, LANES),
            scratch(RH, RW, LANES),
            scratch(EH, EW, LANES),
            scratch(49, 8, LANES),
            scratch(49, 8, LANES),
            scratch(49, 8, LANES),
            scratch(SMALL_ROWS, LANES),
            pltpu.VMEM(stem.shape, BF),
            scratch(dw_kernel.shape[1], dw_kernel.shape[0], LANES),
            scratch(*ln_gain.shape),
            scratch(*w_in.shape, dtype=BF),
            scratch(*w_out.shape, dtype=BF),
            scratch(*layer_scale.shape),
            scratch(count, LANES, dtype=BF),
            pltpu.SemaphoreType.DMA((7,)),
        ],
        compiler_params=pltpu.CompilerParams(vmem_limit_bytes=28 << 20),
    )(
        top,
        tile,
        west,
        east,
        south,
        north,
        stem,
        dw_kernel.transpose(1, 0, 2),
        ln_gain,
        w_in,
        w_out,
        layer_scale,
        upstream[0],
    )
    pieces, order = summed_pieces(packed)
    shapes = [array.shape for array in (stem, dw_kernel, ln_gain, w_in, w_out, layer_scale)]
    shapes[1] = (shapes[1][1], shapes[1][0], shapes[1][2])
    grads = pl.pallas_call(
        unpack_kernel,
        out_shape=[jax.ShapeDtypeStruct(shape, F32) for shape in shapes],
        in_specs=[smem()] + vmem(1),
        out_specs=vmem(6),
        scratch_shapes=[scratch(PACKED, LANES)],
        compiler_params=pltpu.CompilerParams(vmem_limit_bytes=8 << 20),
    )(order, pieces)
    grads = list(grads)
    grads[1] = grads[1].transpose(1, 0, 2)
    return (result[None], *grads)


def solution(mesh):
    in_specs = (
        P(("groups", "gy"), None, None),
        P(("groups", "gy"), None),
        P(),
        P(),
        P(),
        P(),
        P(),
        P(),
        P(("groups", "gy"), None, None),
    )
    out_specs = (
        P(("groups", "gy"), None, None),
        P("groups", None),
        P("groups", None, None),
        P("groups", None),
        P("groups", None, None),
        P("groups", None, None),
        P("groups", None),
    )
    return jax.shard_map(shards, mesh=mesh, in_specs=in_specs, out_specs=out_specs, check_vma=False)
```

time: 86.1 us -> 66.6 us (0.77)
  Pallas kernels: 36.6 us -> 17.9 us
  starting transfers between devices: 19.3 us -> 22.6 us
  local copies, waits for them, and re-layouts: 4.8 us -> 2.43 us
  waiting for transfers between devices: 23.5 us -> 22.4 us
    pallas_call x2, Pallas kernels: 34.8 us -> 17.5 us  [the longest x1 15.8 us: shards(): pl.pallas_call(functools.partial(main_kernel, 1.0 / math.sqrt(size * coun...]
    ppermute x14, starting transfers between devices: 19.3 us -> 22.6 us  [permuted(): return lax.ppermute(value, 'gy', pairs)]
    unnamed x22, local copies, waits for them, and re-layouts: 3.8 us -> 2.28 us
    pallas_call x1, Pallas kernels: 1.82 us -> 0.4 us  [shards(): pl.pallas_call(prepare_kernel, out_shape=[jax.ShapeDtypeStruct((TH, TW, L...]
    ppermute x14, waiting for transfers between devices: 23.5 us -> 22.4 us  [permuted(): return lax.ppermute(value, 'gy', pairs)]
  transfers between devices with their start and end apart: 14 -> 14, of which waited for: 10 -> 10; matrix products, arithmetic and copies ran while one was open for 3% -> 0% of each run, Pallas kernels for 0% -> 0%
where the time goes in v2:
time: 66.6 us; the launch traced here: 66.4 us
  starting transfers between devices  22.6 us (34%)
  waiting for transfers between devices  22.4 us (34%)
  Pallas kernels  17.9 us (27%)
  local copies, waits for them, and re-layouts  2.43 us (4%)
  between operations  0.89 us (1%)
    ppermute x14, starting transfers between devices, permuted(): return lax.ppermute(value, 'gy', pairs)  22.6 us
    ppermute x14, waiting for transfers between devices, permuted(): return lax.ppermute(value, 'gy', pairs)  22.4 us
    pallas_call x1, Pallas kernels, shards(): pl.pallas_call(functools.partial(main_kernel, 1.0 / math.sqrt(size * coun...  15.8 us
    unnamed x22, local copies, waits for them, and re-layouts  2.28 us
    pallas_call x1, Pallas kernels, shards(): pl.pallas_call(unpack_kernel, out_shape=[jax.ShapeDtypeStruct(shape, F32)...  1.6 us
  transfers between devices with their start and end apart: 14, of which 10 were waited for; matrix products, arithmetic and copies ran while one was open for 0% of the time, Pallas kernels for 0%

profile of v2, /device:TPU:0, one launch (start us, length us, event | category | flops | bytes accessed | tf_op | source)
XLA Modules:
  0.0 66.4 jit_solution(10300835841127804370)
XLA Ops:
  0.6 0.0 copy-start.6
  0.7 0.7 %copy-done.6 = s32[1,512]{1,0:T(1,128)S(1)} copy-done((s32[1,512]{1,0:T(1,128)S(1)}, s32[1,512]{1,0:T(1,128)}, u32[]{:S(2)}) %copy-start.6) | copy-done | bytes 2072
  1.3 0.0 copy-start.3
  1.3 0.9 %copy-done.3 = bf16[1,75,512]{2,1,0:T(8,128)(2,1)S(1)} copy-done((bf16[1,75,512]{2,1,0:T(8,128)(2,1)S(1)}, bf16[1,75,512]{2,1,0:T(8,128)(2,1)}, u32[]{:S(2)}) %copy-start.3) | copy-done | bytes 76824
  2.2 0.0 copy-start.4
  2.2 0.4 shard_map.144
  2.6 4.1 %collective-permute-start = (bf16[6,32,128]{2,1,0:T(8,128)(2,1)S(1)}, bf16[6,32,128]{2,1,0:T(8,128)(2,1)S(1)}, u32[]{:S(2)}, u32[]{:S(2)}) collective-permute-start(bf16[6,32,128]{2,1,0:T(8,128)(2,1)S(1)} %get-tuple-element.19), channel_id=1, source_target_pairs={{0,8},{1,9},{2,10},{3,11},{4,12},{5,13},{6,14},{7,15},{8,0},{9,1},... | collective-permute-start | bytes 147464 | tf_op jit(solution)/shard_map/ppermute | solution.py:472
  6.7 0.7 collective-permute-start.1
  7.4 0.0 copy-start.2
  7.4 0.0 copy-start
  7.4 0.0 copy-start.1
  7.4 1.9 %collective-permute-done = bf16[6,32,128]{2,1,0:T(8,128)(2,1)S(1)} collective-permute-done((bf16[6,32,128]{2,1,0:T(8,128)(2,1)S(1)}, bf16[6,32,128]{2,1,0:T(8,128)(2,1)S(1)}, u32[]{:S(2)}, u32[]{:S(2)}) %collective-permute-start) | collective-permute-done | bytes 49184 | tf_op jit(solution)/shard_map/ppermute | solution.py:472
  9.3 0.0 collective-permute-done.1
  9.4 0.1 collective-permute-start.2
  9.4 0.0 copy-start.5
  9.5 0.0 copy-start.8
  9.5 2.7 %collective-permute-start.3 = (bf16[28,8,128]{2,1,0:T(8,128)(2,1)S(1)}, bf16[28,8,128]{2,1,0:T(8,128)(2,1)S(1)}, u32[]{:S(2)}, u32[]{:S(2)}) collective-permute-start(bf16[28,8,128]{2,1,0:T(8,128)(2,1)S(1)} %pad_maximum_fusion.2), channel_id=1, source_target_pairs={{0,7},{1,0},{2,1},{3,2},{4,3},{5,4},{6,5},{7,6},{8,15},{9,8},{10,9... | collective-permute-start | bytes 172040 | tf_op jit(solution)/shard_map/ppermute | solution.py:472
  12.1 1.8 %collective-permute-done.2.west_ref = bf16[28,8,128]{2,1,0:T(8,128)(2,1)S(1)} collective-permute-done((bf16[28,8,128]{2,1,0:T(8,128)(2,1)S(1)}, bf16[28,8,128]{2,1,0:T(8,128)(2,1)S(1)}, u32[]{:S(2)}, u32[]{:S(2)}) %collective-permute-start.2) | collective-permute-done | bytes 57376 | tf_op jit(solution)/shard_map/ppermute | solution.py:472
  13.9 0.0 collective-permute-done.3.east_ref
  14.0 0.0 copy-start.7
  14.0 0.0 copy-done.4
  14.0 0.0 copy-done.2
  14.0 0.0 copy-done
  14.0 0.0 copy-done.1
  14.0 0.0 copy-done.5
  14.0 0.0 copy-done.8
  14.0 0.6 copy-done.7
  14.7 15.8 %shard_map.145 = (bf16[512,128]{1,0:T(8,128)(2,1)}, bf16[2304,128]{1,0:T(8,128)(2,1)S(1)}) custom-call(s32[1]{0:T(128)} %bitcast.top_ref, bf16[16,32,128]{2,1,0:T(8,128)(2,1)S(1)} %get-tuple-element.18.tile_ref, bf16[28,8,128]{2,1,0:T(8,128)(2,1)S(1)} %collective-permute-done.2.west_ref, bf16[28,8,128]{2,1,0:T(8,128)(2,1)S(1)} %collective-permute-done.3.east_ref, ...), custom_call_target="tpu_custom_call" | custom-call | tf_op jit(solution)/shard_map/pallas_call | solution.py:555
  30.6 1.0 %collective-permute-start.4 = (bf16[1152,128]{1,0:T(8,128)(2,1)S(1)}, bf16[1152,128]{1,0:T(8,128)(2,1)S(1)}, u32[]{:S(2)}, u32[]{:S(2)}) collective-permute-start(bf16[1152,128]{1,0:T(8,128)(2,1)S(1)} %broadcast_select_fusion), channel_id=1, source_target_pairs={{0,1},{1,0},{2,3},{3,2},{4,5},{5,4},{6,7},{7,6},{8,9},{9,8},{10,11... | collective-permute-start | bytes 884744 | tf_op jit(solution)/shard_map/ppermute | solution.py:472
  31.6 1.2 %collective-permute-done.4 = bf16[1152,128]{1,0:T(8,128)(2,1)S(1)} collective-permute-done((bf16[1152,128]{1,0:T(8,128)(2,1)S(1)}, bf16[1152,128]{1,0:T(8,128)(2,1)S(1)}, u32[]{:S(2)}, u32[]{:S(2)}) %collective-permute-start.4) | collective-permute-done | bytes 294944 | tf_op jit(solution)/shard_map/ppermute | solution.py:472
  32.8 0.1 convert_add_fusion
  32.9 2.1 %collective-permute-start.5 = (bf16[576,128]{1,0:T(8,128)(2,1)S(1)}, bf16[576,128]{1,0:T(8,128)(2,1)S(1)}, u32[]{:S(2)}, u32[]{:S(2)}) collective-permute-start(bf16[576,128]{1,0:T(8,128)(2,1)S(1)} %select_convert_fusion), channel_id=1, source_target_pairs={{0,2},{1,3},{2,0},{3,1},{4,6},{5,7},{6,4},{7,5},{8,10},{9,11},{10,... | collective-permute-start | bytes 442376 | tf_op jit(solution)/shard_map/ppermute | solution.py:472
  35.0 4.4 %collective-permute-done.5 = bf16[576,128]{1,0:T(8,128)(2,1)S(1)} collective-permute-done((bf16[576,128]{1,0:T(8,128)(2,1)S(1)}, bf16[576,128]{1,0:T(8,128)(2,1)S(1)}, u32[]{:S(2)}, u32[]{:S(2)}) %collective-permute-start.5) | collective-permute-done | bytes 147488 | tf_op jit(solution)/shard_map/ppermute | solution.py:472
  39.5 5.0 %collective-permute-start.8 = (bf16[144,128]{1,0:T(8,128)(2,1)S(1)}, bf16[144,128]{1,0:T(8,128)(2,1)S(1)}, u32[]{:S(2)}, u32[]{:S(2)}) collective-permute-start(bf16[144,128]{1,0:T(8,128)(2,1)S(1)} %get-tuple-element.32), channel_id=1, source_target_pairs={{0,12},{1,13},{2,14},{3,15},{4,8},{5,9},{6,10},{7,11},{8,4},{9,5},... | collective-permute-start | bytes 110600 | tf_op jit(solution)/shard_map/ppermute | solution.py:472
  44.5 0.1 collective-permute-start.7
  44.6 0.5 collective-permute-start.6
  45.1 1.3 %collective-permute-done.8 = bf16[144,128]{1,0:T(8,128)(2,1)S(1)} collective-permute-done((bf16[144,128]{1,0:T(8,128)(2,1)S(1)}, bf16[144,128]{1,0:T(8,128)(2,1)S(1)}, u32[]{:S(2)}, u32[]{:S(2)}) %collective-permute-start.8) | collective-permute-done | bytes 36896 | tf_op jit(solution)/shard_map/ppermute | solution.py:472
  46.5 3.3 %collective-permute-done.7 = bf16[144,128]{1,0:T(8,128)(2,1)S(1)} collective-permute-done((bf16[144,128]{1,0:T(8,128)(2,1)S(1)}, bf16[144,128]{1,0:T(8,128)(2,1)S(1)}, u32[]{:S(2)}, u32[]{:S(2)}) %collective-permute-start.7) | collective-permute-done | bytes 36896 | tf_op jit(solution)/shard_map/ppermute | solution.py:472
  49.7 0.0 collective-permute-done.6
  49.8 0.4 collective-permute-start.9
  50.1 1.9 %collective-permute-start.10 = (bf16[144,128]{1,0:T(8,128)(2,1)S(1)}, bf16[144,128]{1,0:T(8,128)(2,1)S(1)}, u32[]{:S(2)}, u32[]{:S(2)}) collective-permute-start(bf16[144,128]{1,0:T(8,128)(2,1)S(1)} %get-tuple-element.30), channel_id=1, source_target_pairs={{0,8},{1,9},{2,10},{3,11},{4,12},{5,13},{6,14},{7,15},{8,0},{9,1},... | collective-permute-start | bytes 110600 | tf_op jit(solution)/shard_map/ppermute | solution.py:472
  52.1 2.2 %collective-permute-start.11 = (bf16[144,128]{1,0:T(8,128)(2,1)S(1)}, bf16[144,128]{1,0:T(8,128)(2,1)S(1)}, u32[]{:S(2)}, u32[]{:S(2)}) collective-permute-start(bf16[144,128]{1,0:T(8,128)(2,1)S(1)} %get-tuple-element.30), channel_id=1, source_target_pairs={{0,12},{1,13},{2,14},{3,15},{4,8},{5,9},{6,10},{7,11},{8,4},{9,5},... | collective-permute-start | bytes 110600 | tf_op jit(solution)/shard_map/ppermute | solution.py:472
  54.2 0.0 collective-permute-done.9
  54.2 1.0 %collective-permute-done.10 = bf16[144,128]{1,0:T(8,128)(2,1)S(1)} collective-permute-done((bf16[144,128]{1,0:T(8,128)(2,1)S(1)}, bf16[144,128]{1,0:T(8,128)(2,1)S(1)}, u32[]{:S(2)}, u32[]{:S(2)}) %collective-permute-start.10) | collective-permute-done | bytes 36896 | tf_op jit(solution)/shard_map/ppermute | solution.py:472
  55.2 2.6 %collective-permute-done.11 = bf16[144,128]{1,0:T(8,128)(2,1)S(1)} collective-permute-done((bf16[144,128]{1,0:T(8,128)(2,1)S(1)}, bf16[144,128]{1,0:T(8,128)(2,1)S(1)}, u32[]{:S(2)}, u32[]{:S(2)}) %collective-permute-start.11) | collective-permute-done | bytes 36896 | tf_op jit(solution)/shard_map/ppermute | solution.py:472
  57.8 1.8 %collective-permute-start.12 = (bf16[4,144,128]{2,1,0:T(8,128)(2,1)S(1)}, bf16[4,144,128]{2,1,0:T(8,128)(2,1)S(1)}, u32[]{:S(2)}, u32[]{:S(2)}) collective-permute-start(bf16[4,144,128]{2,1,0:T(8,128)(2,1)S(1)} %pad_maximum_fusion), channel_id=1, source_target_pairs={{0,2},{1,3},{2,0},{3,1},{4,6},{5,7},{6,4},{7,5},{8,10},{9,11},{10,... | collective-permute-start | bytes 442376 | tf_op jit(solution)/shard_map/ppermute | solution.py:472
  59.7 3.3 %collective-permute-done.12 = bf16[4,144,128]{2,1,0:T(8,128)(2,1)S(1)} collective-permute-done((bf16[4,144,128]{2,1,0:T(8,128)(2,1)S(1)}, bf16[4,144,128]{2,1,0:T(8,128)(2,1)S(1)}, u32[]{:S(2)}, u32[]{:S(2)}) %collective-permute-start.12) | collective-permute-done | bytes 147488 | tf_op jit(solution)/shard_map/ppermute | solution.py:472
  63.1 0.1 constant_dynamic-update-slice_fusion
  63.1 0.1 collective-permute-start.13
  63.2 1.5 %collective-permute-done.13 = bf16[8,144,128]{2,1,0:T(8,128)(2,1)S(1)} collective-permute-done((bf16[8,144,128]{2,1,0:T(8,128)(2,1)S(1)}, bf16[8,144,128]{2,1,0:T(8,128)(2,1)S(1)}, u32[]{:S(2)}, u32[]{:S(2)}) %collective-permute-start.13) | collective-permute-done | bytes 294944 | tf_op jit(solution)/shard_map/ppermute | solution.py:472
  64.8 1.6 %shard_map.146 = (f32[75,128]{1,0:T(8,128)}, f32[49,2,128]{2,1,0:T(2,128)}, f32[2,128]{1,0:T(2,128)}, f32[2,128,512]{2,1,0:T(8,128)}, f32[2,512,128]{2,1,0:T(8,128)}, /*index=5*/f32[2,128]{1,0:T(2,128)}) custom-call(s32[16]{0:T(128)S(1)} %iota_xor_fusion.order_ref, bf16[16,144,128]{2,1,0:T(8,128)(2,1)S(1)} %constant_dynamic-update-slice_fusion.5.pieces_ref), custom_call_target="tpu_custom_call" | custom-call | tf_op jit(solution)/shard_map/pallas_call | solution.py:625
  (17 shorter events, 0.3 us)
Async XLA Ops:
  0.6 0.7 %copy-start.6 = (s32[1,512]{1,0:T(1,128)S(1)}, s32[1,512]{1,0:T(1,128)}, u32[]{:S(2)}) copy-start(s32[1,512]{1,0:T(1,128)} %ocean_ref.1) | copy-start | bytes 6148
  1.3 0.9 %copy-start.3 = (bf16[1,75,512]{2,1,0:T(8,128)(2,1)S(1)}, bf16[1,75,512]{2,1,0:T(8,128)(2,1)}, u32[]{:S(2)}) copy-start(bf16[1,75,512]{2,1,0:T(8,128)(2,1)} %param.9) | copy-start | bytes 230404
  2.2 11.8 %copy-start.4 = (f32[2,49,128]{2,0,1:T(2,128)S(1)}, f32[2,49,128]{2,0,1:T(2,128)}, u32[]{:S(2)}) copy-start(f32[2,49,128]{2,0,1:T(2,128)} %param.12) | copy-start | bytes 150532
  2.6 6.7 %collective-permute-start = (bf16[6,32,128]{2,1,0:T(8,128)(2,1)S(1)}, bf16[6,32,128]{2,1,0:T(8,128)(2,1)S(1)}, u32[]{:S(2)}, u32[]{:S(2)}) collective-permute-start(bf16[6,32,128]{2,1,0:T(8,128)(2,1)S(1)} %get-tuple-element.19), channel_id=1, source_target_pairs={{0,8},{1,9},{2,10},{3,11},{4,12},{5,13},{6,14},{7,15},{8,0},{9,1},... | collective-permute-start | bytes 147464 | tf_op jit(solution)/shard_map/ppermute | solution.py:472
  6.7 2.6 %collective-permute-start.1 = (bf16[6,32,128]{2,1,0:T(8,128)(2,1)S(1)}, bf16[6,32,128]{2,1,0:T(8,128)(2,1)S(1)}, u32[]{:S(2)}, u32[]{:S(2)}) collective-permute-start(bf16[6,32,128]{2,1,0:T(8,128)(2,1)S(1)} %get-tuple-element.20), channel_id=1, source_target_pairs={{8,15},{9,14},{10,13},{11,12},{12,11},{13,10},{14,9},{15,8},{24,31... | collective-permute-start | bytes 147464 | tf_op jit(solution)/shard_map/ppermute | solution.py:472
  7.4 6.6 %copy-start.2 = (bf16[1,512,128]{2,1,0:T(8,128)(2,1)S(1)}, bf16[1,512,128]{2,1,0:T(8,128)(2,1)}, u32[]{:S(2)}) copy-start(bf16[1,512,128]{2,1,0:T(8,128)(2,1)} %param.17) | copy-start | bytes 393220
  7.4 6.6 %copy-start = (bf16[2,128,512]{2,1,0:T(8,128)(2,1)S(1)}, bf16[2,128,512]{2,1,0:T(8,128)(2,1)}, u32[]{:S(2)}) copy-start(bf16[2,128,512]{2,1,0:T(8,128)(2,1)} %win_hbm.1) | copy-start | bytes 786436
  7.4 6.6 %copy-start.1 = (bf16[2,512,128]{2,1,0:T(8,128)(2,1)S(1)}, bf16[2,512,128]{2,1,0:T(8,128)(2,1)}, u32[]{:S(2)}) copy-start(bf16[2,512,128]{2,1,0:T(8,128)(2,1)} %wout_hbm.1) | copy-start | bytes 786436
  9.4 4.6 %collective-permute-start.2 = (bf16[28,8,128]{2,1,0:T(8,128)(2,1)S(1)}, bf16[28,8,128]{2,1,0:T(8,128)(2,1)S(1)}, u32[]{:S(2)}, u32[]{:S(2)}) collective-permute-start(bf16[28,8,128]{2,1,0:T(8,128)(2,1)S(1)} %pad_maximum_fusion.1), channel_id=1, source_target_pairs={{0,1},{1,2},{2,3},{3,4},{4,5},{5,6},{6,7},{7,0},{8,9},{9,10},{10,1... | collective-permute-start | bytes 172040 | tf_op jit(solution)/shard_map/ppermute | solution.py:472
  9.4 4.6 %copy-start.5 = (bf16[75,128]{1,0:T(8,128)(2,1)S(1)}, bf16[75,128]{1,0:T(8,128)(2,1)}, u32[]{:S(2)}) copy-start(bf16[75,128]{1,0:T(8,128)(2,1)} %stem_hbm.1) | copy-start | bytes 57604
  9.5 4.6 %copy-start.8 = (f32[2,128]{1,0:T(2,128)S(1)}, f32[2,128]{1,0:T(2,128)}, u32[]{:S(2)}) copy-start(f32[2,128]{1,0:T(2,128)} %scale_hbm.1) | copy-start | bytes 3076
  9.5 4.5 %collective-permute-start.3 = (bf16[28,8,128]{2,1,0:T(8,128)(2,1)S(1)}, bf16[28,8,128]{2,1,0:T(8,128)(2,1)S(1)}, u32[]{:S(2)}, u32[]{:S(2)}) collective-permute-start(bf16[28,8,128]{2,1,0:T(8,128)(2,1)S(1)} %pad_maximum_fusion.2), channel_id=1, source_target_pairs={{0,7},{1,0},{2,1},{3,2},{4,3},{5,4},{6,5},{7,6},{8,15},{9,8},{10,9... | collective-permute-start | bytes 172040 | tf_op jit(solution)/shard_map/ppermute | solution.py:472
  14.0 0.7 %copy-start.7 = (f32[2,128]{1,0:T(2,128)S(1)}, f32[2,128]{1,0:T(2,128)}, u32[]{:S(2)}) copy-start(f32[2,128]{1,0:T(2,128)} %gain_hbm.1) | copy-start | bytes 3076
  30.6 2.2 %collective-permute-start.4 = (bf16[1152,128]{1,0:T(8,128)(2,1)S(1)}, bf16[1152,128]{1,0:T(8,128)(2,1)S(1)}, u32[]{:S(2)}, u32[]{:S(2)}) collective-permute-start(bf16[1152,128]{1,0:T(8,128)(2,1)S(1)} %broadcast_select_fusion), channel_id=1, source_target_pairs={{0,1},{1,0},{2,3},{3,2},{4,5},{5,4},{6,7},{7,6},{8,9},{9,8},{10,11... | collective-permute-start | bytes 884744 | tf_op jit(solution)/shard_map/ppermute | solution.py:472
  32.9 6.5 %collective-permute-start.5 = (bf16[576,128]{1,0:T(8,128)(2,1)S(1)}, bf16[576,128]{1,0:T(8,128)(2,1)S(1)}, u32[]{:S(2)}, u32[]{:S(2)}) collective-permute-start(bf16[576,128]{1,0:T(8,128)(2,1)S(1)} %select_convert_fusion), channel_id=1, source_target_pairs={{0,2},{1,3},{2,0},{3,1},{4,6},{5,7},{6,4},{7,5},{8,10},{9,11},{10,... | collective-permute-start | bytes 442376 | tf_op jit(solution)/shard_map/ppermute | solution.py:472
  39.5 7.0 %collective-permute-start.8 = (bf16[144,128]{1,0:T(8,128)(2,1)S(1)}, bf16[144,128]{1,0:T(8,128)(2,1)S(1)}, u32[]{:S(2)}, u32[]{:S(2)}) collective-permute-start(bf16[144,128]{1,0:T(8,128)(2,1)S(1)} %get-tuple-element.32), channel_id=1, source_target_pairs={{0,12},{1,13},{2,14},{3,15},{4,8},{5,9},{6,10},{7,11},{8,4},{9,5},... | collective-permute-start | bytes 110600 | tf_op jit(solution)/shard_map/ppermute | solution.py:472
  44.5 5.3 %collective-permute-start.7 = (bf16[144,128]{1,0:T(8,128)(2,1)S(1)}, bf16[144,128]{1,0:T(8,128)(2,1)S(1)}, u32[]{:S(2)}, u32[]{:S(2)}) collective-permute-start(bf16[144,128]{1,0:T(8,128)(2,1)S(1)} %get-tuple-element.33), channel_id=1, source_target_pairs={{0,8},{1,9},{2,10},{3,11},{4,12},{5,13},{6,14},{7,15},{8,0},{9,1},... | collective-permute-start | bytes 110600 | tf_op jit(solution)/shard_map/ppermute | solution.py:472
  44.6 5.1 %collective-permute-start.6 = (bf16[144,128]{1,0:T(8,128)(2,1)S(1)}, bf16[144,128]{1,0:T(8,128)(2,1)S(1)}, u32[]{:S(2)}, u32[]{:S(2)}) collective-permute-start(bf16[144,128]{1,0:T(8,128)(2,1)S(1)} %get-tuple-element.31), channel_id=1, source_target_pairs={{0,4},{1,5},{2,6},{3,7},{4,0},{5,1},{6,2},{7,3},{8,12},{9,13},{10,... | collective-permute-start | bytes 110600 | tf_op jit(solution)/shard_map/ppermute | solution.py:472
  49.8 4.5 %collective-permute-start.9 = (bf16[144,128]{1,0:T(8,128)(2,1)S(1)}, bf16[144,128]{1,0:T(8,128)(2,1)S(1)}, u32[]{:S(2)}, u32[]{:S(2)}) collective-permute-start(bf16[144,128]{1,0:T(8,128)(2,1)S(1)} %get-tuple-element.30), channel_id=1, source_target_pairs={{0,4},{1,5},{2,6},{3,7},{4,0},{5,1},{6,2},{7,3},{8,12},{9,13},{10,... | collective-permute-start | bytes 110600 | tf_op jit(solution)/shard_map/ppermute | solution.py:472
  50.1 5.1 %collective-permute-start.10 = (bf16[144,128]{1,0:T(8,128)(2,1)S(1)}, bf16[144,128]{1,0:T(8,128)(2,1)S(1)}, u32[]{:S(2)}, u32[]{:S(2)}) collective-permute-start(bf16[144,128]{1,0:T(8,128)(2,1)S(1)} %get-tuple-element.30), channel_id=1, source_target_pairs={{0,8},{1,9},{2,10},{3,11},{4,12},{5,13},{6,14},{7,15},{8,0},{9,1},... | collective-permute-start | bytes 110600 | tf_op jit(solution)/shard_map/ppermute | solution.py:472
  52.1 5.8 %collective-permute-start.11 = (bf16[144,128]{1,0:T(8,128)(2,1)S(1)}, bf16[144,128]{1,0:T(8,128)(2,1)S(1)}, u32[]{:S(2)}, u32[]{:S(2)}) collective-permute-start(bf16[144,128]{1,0:T(8,128)(2,1)S(1)} %get-tuple-element.30), channel_id=1, source_target_pairs={{0,12},{1,13},{2,14},{3,15},{4,8},{5,9},{6,10},{7,11},{8,4},{9,5},... | collective-permute-start | bytes 110600 | tf_op jit(solution)/shard_map/ppermute | solution.py:472
  57.8 5.2 %collective-permute-start.12 = (bf16[4,144,128]{2,1,0:T(8,128)(2,1)S(1)}, bf16[4,144,128]{2,1,0:T(8,128)(2,1)S(1)}, u32[]{:S(2)}, u32[]{:S(2)}) collective-permute-start(bf16[4,144,128]{2,1,0:T(8,128)(2,1)S(1)} %pad_maximum_fusion), channel_id=1, source_target_pairs={{0,2},{1,3},{2,0},{3,1},{4,6},{5,7},{6,4},{7,5},{8,10},{9,11},{10,... | collective-permute-start | bytes 442376 | tf_op jit(solution)/shard_map/ppermute | solution.py:472
  63.1 1.6 %collective-permute-start.13 = (bf16[8,144,128]{2,1,0:T(8,128)(2,1)S(1)}, bf16[8,144,128]{2,1,0:T(8,128)(2,1)S(1)}, u32[]{:S(2)}, u32[]{:S(2)}) collective-permute-start(bf16[8,144,128]{2,1,0:T(8,128)(2,1)S(1)} %get-tuple-element.34), channel_id=1, source_target_pairs={{0,1},{1,0},{2,3},{3,2},{4,5},{5,4},{6,7},{7,6},{8,9},{9,8},{10,11... | collective-permute-start | bytes 884744 | tf_op jit(solution)/shard_map/ppermute | solution.py:472

commit v3 on v2

--- a/solution.py
+++ b/solution.py
@@ -23,10 +23,9 @@
 C1 = 0.7978845608028654 * 0.044715
 NORM_STABILIZER = 1e-06
 
-WIN_ROW, WOUT_ROW, SMALL_ROW = 0, 1024, 2048
-STEM_AT, KERNEL_AT, GAIN_AT, SCALE_AT = 0, (80, 136), 192, 194
-SMALL_ROWS = 256
-PACKED = SMALL_ROW + SMALL_ROWS
+WIN_ROW, WOUT_ROW, BULK = 0, 1024, 2048
+STEM_AT, KERNEL_AT, GAIN_AT, SCALE_AT = 0, (75, 124), 173, 175
+SMALL = 192
 
 BF = jnp.bfloat16
 F32 = jnp.float32
@@ -90,6 +89,23 @@
     return totals
 
 
+def spread_taps(dw_ref, layer, taps, top=None):
+    for t in range(49):
+        row = dw_ref[t, layer : layer + 1, :]
+        if top is not None:
+            row = jnp.where(top, dw_ref[48 - t, layer : layer + 1, :], row)
+        taps[t] = jnp.broadcast_to(row, (8, LANES))
+
+
+def padded(flat, pad, width):
+    rows = flat.shape[0] // width
+    pad[:, 0:PADC, :] = jnp.zeros((rows, PADC, LANES), F32)
+    pad[:, PADC + width :, :] = jnp.zeros((rows, pad.shape[1] - PADC - width, LANES), F32)
+    for row in range(0, rows, 2):
+        value = flat[row * width : (row + 2) * width, :].astype(F32)
+        pad[row : row + 2, PADC : PADC + width, :] = value.reshape(2, width, LANES)
+
+
 def main_kernel(
     rescale,
     top_ref,
@@ -107,13 +123,22 @@
     up_hbm,
     out_ref,
     packed_ref,
-    ext,
+    sums,
+    cells,
+    flat0,
+    flat1,
+    grad0,
+    grad1,
+    carry0,
     x0,
     m6,
     x1,
-    weights,
     taps0,
     taps0n,
+    pad1,
+    g1,
+    ext,
+    weights,
     taps1,
     conv0,
     xhat0,
@@ -132,14 +157,6 @@
     wide,
     thin,
     gpre,
-    pad0,
-    pad1,
-    g1,
-    h0,
-    gk0,
-    gk0n,
-    gk1,
-    small,
     stem_ref,
     dw_ref,
     gain_ref,
@@ -184,21 +201,20 @@
 
     for index in range(EH // 4):
         at = slice(index * 4, index * 4 + 4)
-        both = jnp.dot(
-            ext[at].reshape(4 * EW, LANES).astype(BF), joint, preferred_element_type=F32
-        )
+        here = ext[at].reshape(4 * EW, LANES).astype(BF)
+        cells[index * 4 * EW : (index + 1) * 4 * EW, :] = here
+        both = jnp.dot(here, joint, preferred_element_type=F32)
         mask = both[:, LANES:]
         m6[at] = mask.reshape(4, EW, LANES)
-        x0[at] = (mask * both[:, :LANES]).astype(BF).astype(F32).reshape(4, EW, LANES)
+        value = (mask * both[:, :LANES]).astype(BF)
+        flat0[index * 4 * EW : (index + 1) * 4 * EW, :] = value
+        x0[at] = value.astype(F32).reshape(4, EW, LANES)
 
     for load in loads[1:]:
         load.wait()
-    for t in range(49):
-        first = dw_ref[t, 0:1, :]
-        turned = dw_ref[48 - t, 0:1, :]
-        taps0[t] = jnp.broadcast_to(first, (8, LANES))
-        taps0n[t] = jnp.broadcast_to(jnp.where(top, turned, first), (8, LANES))
-        taps1[t] = jnp.broadcast_to(dw_ref[t, 1:2, :], (8, LANES))
+    spread_taps(dw_ref, 0, taps0)
+    spread_taps(dw_ref, 0, taps0n, top)
+    spread_taps(dw_ref, 1, taps1)
 
     north_at = 3 + TH
 
@@ -266,7 +282,9 @@
         mask = m6[rows, RING_COL : RING_COL + RW, :]
         held = x0[rows, RING_COL : RING_COL + RW, :]
         branch = branch0[at, :].reshape(2, RW, LANES)
-        x1[pl.ds(index * 2, 2)] = (mask * (held + scale_ref[0:1, :] * branch)).astype(BF).astype(F32)
+        value = (mask * (held + scale_ref[0:1, :] * branch)).astype(BF)
+        flat1[at, :] = value.reshape(2 * RW, LANES)
+        x1[pl.ds(index * 2, 2)] = value.astype(F32)
         return 0
 
     chunks(count0, 2 * RW, next0)(0)
@@ -287,7 +305,7 @@
     gelu_rows(wide, act1, slope1, count1, 64)
     branch1[...] = jnp.dot(act1[...], wout_ref[1], preferred_element_type=F32)
 
-    small[...] = jnp.zeros_like(small)
+    sums[...] = jnp.zeros_like(sums)
     g1[...] = jnp.zeros_like(g1)
 
     def folded(value):
@@ -305,7 +323,7 @@
         return total + folded(masked * branch)
 
     total = chunks(count1, 2 * TW, next1)(jnp.zeros((8, LANES), F32))
-    small[SCALE_AT + 1 : SCALE_AT + 2, :] = jnp.sum(total, axis=0, keepdims=True)
+    sums[3:4, :] = jnp.sum(total, axis=0, keepdims=True)
 
     def grad_wout(layer, count, act):
         packed_ref[WOUT_ROW + 512 * layer : WOUT_ROW + 512 * layer + 512, :] = contract_rows(
@@ -331,8 +349,7 @@
             packed_ref[at : at + 128, :] = grad_in[:, 128 * part : 128 * part + 128]
         wide[0:count, 0:LANES] = contract_cols(gp, win_ref[layer])
 
-    def grad_conv(layer, count, shape, xhat, rinv, pad):
-        rows, width = shape
+    def grad_conv(layer, count, size, xhat, rinv, grad):
         gain = gain_ref[layer : layer + 1, :]
 
         def step(index, at, total):
@@ -341,18 +358,81 @@
             gx = gn * gain
             first = jnp.mean(gx, axis=-1, keepdims=True)
             second = jnp.mean(gx * scaled, axis=-1, keepdims=True)
-            value = (rinv[at, :] * (gx - first - scaled * second)).astype(BF).astype(F32)
-            pad[pl.ds(index * rows, rows), PADC : PADC + width, :] = value.reshape(rows, width, LANES)
+            grad[at, :] = (rinv[at, :] * (gx - first - scaled * second)).astype(BF)
             return total + folded(gn * scaled)
 
-        total = chunks(count, rows * width, step)(jnp.zeros((8, LANES), F32))
-        small[GAIN_AT + layer : GAIN_AT + layer + 1, :] = jnp.sum(total, axis=0, keepdims=True)
-
-    pad1[...] = jnp.zeros_like(pad1)
+        total = chunks(count, size, step)(jnp.zeros((8, LANES), F32))
+        sums[layer : layer + 1, :] = jnp.sum(total, axis=0, keepdims=True)
+
     grad_wout(1, count1, act1)
     grad_pre(1, count1, 64, slope1)
     grad_win(1, count1, normed1)
-    grad_conv(1, count1, (2, TW), xhat1, rinv1, pad1)
+    grad_conv(1, count1, 2 * TW, xhat1, rinv1, grad1)
+    padded(grad1, pad1, TW)
+
+    def back1_block(block, _):
+        start = pl.multiple_of(block * 8, 8)
+        for rows in (range(0, 22),):
+            totals = conv_block(
+                pad1, (taps1,), start + 2, rows, range(6, 6 + TH), lambda o, r, a, d: (0, 48 - (a * 7 + d))
+            )
+            for o in rows:
+                g1[o, pl.ds(start, 8), :] += totals[o]
+        return 0
+
+    lax.fori_loop(0, RW // 8, back1_block, 0)
+
+    def masked0(index, at, total):
+        rows = pl.ds(index * 2, 2)
+        masked = m6[pl.ds(index * 2 + 3, 2), RING_COL : RING_COL + RW, :] * g1[rows]
+        flat = masked.reshape(2 * RW, LANES)
+        carry0[at, :] = flat
+        thin[at, :] = (flat * scale_ref[0:1, :]).astype(BF)
+        return total + folded(flat * branch0[at, :])
+
+    total = chunks(count0, 2 * RW, masked0)(jnp.zeros((8, LANES), F32))
+    sums[2:3, :] = jnp.sum(total, axis=0, keepdims=True)
+    grad_wout(0, count0, act0)
+    grad_pre(0, count0, 80, slope0)
+    grad_win(0, count0, normed0)
+    grad_conv(0, count0, 2 * RW, xhat0, rinv0, grad0)
+
+
+def rest_kernel(
+    top_ref,
+    dw_ref,
+    sums,
+    cells,
+    flat0,
+    flat1,
+    grad0,
+    grad1,
+    carry0,
+    small_ref,
+    small,
+    x0,
+    x1,
+    pad0,
+    pad1,
+    taps0,
+    taps0n,
+    h0,
+    gk0,
+    gk0n,
+    gk1,
+):
+    top = top_ref[0] == 1
+    north_at = 3 + TH
+    levels_count = KERNEL_AT[0] - STEM_AT
+
+    for row in range(0, EH, 4):
+        x0[row : row + 4] = flat0[row * EW : (row + 4) * EW, :].astype(F32).reshape(4, EW, LANES)
+    for row in range(0, RH, 2):
+        x1[row : row + 2] = flat1[row * RW : (row + 2) * RW, :].astype(F32).reshape(2, RW, LANES)
+    padded(grad0, pad0, RW)
+    padded(grad1, pad1, TW)
+    spread_taps(dw_ref, 0, taps0)
+    spread_taps(dw_ref, 0, taps0n, top)
 
     gk1[...] = jnp.zeros_like(gk1)
 
@@ -369,34 +449,6 @@
         return 0
 
     lax.fori_loop(0, TW // 8, kernel1_block, 0)
-
-    def back1_block(block, _):
-        start = pl.multiple_of(block * 8, 8)
-        for rows in (range(0, 22),):
-            totals = conv_block(
-                pad1, (taps1,), start + 2, rows, range(6, 6 + TH), lambda o, r, a, d: (0, 48 - (a * 7 + d))
-            )
-            for o in rows:
-                g1[o, pl.ds(start, 8), :] += totals[o]
-        return 0
-
-    lax.fori_loop(0, RW // 8, back1_block, 0)
-
-    def masked0(index, at, total):
-        rows = pl.ds(index * 2, 2)
-        masked = m6[pl.ds(index * 2 + 3, 2), RING_COL : RING_COL + RW, :] * g1[rows]
-        g1[rows] = masked
-        flat = masked.reshape(2 * RW, LANES)
-        thin[at, :] = (flat * scale_ref[0:1, :]).astype(BF)
-        return total + folded(flat * branch0[at, :])
-
-    total = chunks(count0, 2 * RW, masked0)(jnp.zeros((8, LANES), F32))
-    small[SCALE_AT : SCALE_AT + 1, :] = jnp.sum(total, axis=0, keepdims=True)
-    pad0[...] = jnp.zeros_like(pad0)
-    grad_wout(0, count0, act0)
-    grad_pre(0, count0, 80, slope0)
-    grad_win(0, count0, normed0)
-    grad_conv(0, count0, (2, RW), xhat0, rinv0, pad0)
 
     gk0[...] = jnp.zeros_like(gk0)
     gk0n[...] = jnp.zeros_like(gk0n)
@@ -439,33 +491,41 @@
         return 0
 
     lax.fori_loop(0, EW // 8, back0_block, 0)
-    def carry0(index, _):
-        h0[pl.ds(index * 2 + 3, 2), RING_COL : RING_COL + RW, :] += g1[pl.ds(index * 2, 2)]
-        return 0
-
-    lax.fori_loop(0, RH // 2, carry0, 0)
-    stem_side = (m6[...].reshape(EH * EW, LANES) * h0[...].reshape(EH * EW, LANES)).astype(BF)
-    stem_grad = contract_rows(ext[...].reshape(EH * EW, LANES).astype(BF), stem_side)
-    small[STEM_AT : STEM_AT + 80, :] = stem_grad[0:80, :]
-    packed_ref[SMALL_ROW : SMALL_ROW + SMALL_ROWS, :] = small[...].astype(BF)
-
-
-def unpack_kernel(order_ref, pieces_ref, stem_ref, kernel_ref, gain_ref, win_ref, wout_ref, scale_ref, rows):
+    for row in range(0, RH, 2):
+        h0[row + 3 : row + 5, RING_COL : RING_COL + RW, :] += carry0[
+            row * RW : (row + 2) * RW, :
+        ].reshape(2, RW, LANES)
+    rows = lax.broadcasted_iota(jnp.int32, (LANES, LANES), 0)
+    mask = jnp.dot(cells[...], (rows == levels_count).astype(BF), preferred_element_type=F32)
+    stem_side = (mask * h0[...].reshape(EH * EW, LANES)).astype(BF)
+    stem_grad = contract_rows(cells[...], stem_side)
+    small[STEM_AT : KERNEL_AT[0], :] = stem_grad[0:levels_count, :]
+    small[GAIN_AT : GAIN_AT + 4, :] = sums[0:4, :]
+    small[GAIN_AT + 4 :, :] = jnp.zeros((SMALL - GAIN_AT - 4, LANES), F32)
+    small_ref[...] = small[...].astype(BF)
+
+
+def unpack_kernel(
+    order_ref, pieces_ref, mine_ref, other_ref, stem_ref, kernel_ref, gain_ref, win_ref, wout_ref, scale_ref, rows, small
+):
     count, size = pieces_ref.shape[0], pieces_ref.shape[1]
     for index in range(count):
         rows[index * size : (index + 1) * size, :] = pieces_ref[order_ref[index]].astype(F32)
+    count, size = mine_ref.shape[0], mine_ref.shape[1]
+    for index in range(count):
+        at = order_ref[pieces_ref.shape[0] + index]
+        small[index * size : (index + 1) * size, :] = mine_ref[at].astype(F32) + other_ref[at].astype(F32)
     for layer in range(2):
         for part in range(4):
             at = WIN_ROW + 512 * layer + 128 * part
             win_ref[layer, :, 128 * part : 128 * part + 128] = rows[at : at + 128, :]
         at = WOUT_ROW + 512 * layer
         wout_ref[layer] = rows[at : at + 512, :]
-        at = SMALL_ROW + KERNEL_AT[layer]
-        kernel_ref[:, layer, :] = rows[at : at + 49, :]
-    at = SMALL_ROW + STEM_AT
-    stem_ref[...] = rows[at : at + stem_ref.shape[0], :]
-    gain_ref[...] = rows[SMALL_ROW + GAIN_AT : SMALL_ROW + GAIN_AT + 2, :]
-    scale_ref[...] = rows[SMALL_ROW + SCALE_AT : SMALL_ROW + SCALE_AT + 2, :]
+        at = KERNEL_AT[layer]
+        kernel_ref[:, layer, :] = small[at : at + 49, :]
+    stem_ref[...] = small[STEM_AT : STEM_AT + stem_ref.shape[0], :]
+    gain_ref[...] = small[GAIN_AT : GAIN_AT + 2, :]
+    scale_ref[...] = small[SCALE_AT : SCALE_AT + 2, :]
 
 
 def permuted(value, pairs):
@@ -476,10 +536,12 @@
     return permuted(value, [(i, i ^ bits) for i in range(lax.axis_size("gy"))])
 
 
-def summed_pieces(packed):
+def summed_pieces(packed, top, rest):
     size = lax.axis_size("gy")
     if size != 16:
-        return lax.psum(packed.astype(F32), "gy").astype(BF)[None], jnp.zeros((1,), jnp.int32)
+        bulk, small = lax.psum((packed.astype(F32), rest(top).astype(F32)), "gy")
+        small = small.astype(BF)[None]
+        return bulk.astype(BF)[None], small, jnp.zeros_like(small), jnp.zeros((2,), jnp.int32)
     me = lax.axis_index("gy")
     core, side, deep = me & 1, (me >> 1) & 1, me >> 2
 
@@ -489,25 +551,43 @@
         return jnp.where(bit == 0, low, high), jnp.where(bit == 0, high, low)
 
     keep, send = halves(packed, core)
-    total = keep.astype(F32) + crossed(send, 1).astype(F32)
-    keep, send = halves(total, side)
+    came = crossed(send, 1)
+    came, top = lax.optimization_barrier((came, top))
+    small = rest(top)
+    keep, send = halves(keep.astype(F32) + came.astype(F32), side)
     total = keep + crossed(send.astype(BF), 2).astype(F32)
     quarter = total.shape[0] // 4
+    part = small.shape[0] // 4
 
     def shard(step):
-        return lax.dynamic_slice_in_dim(total, (deep ^ step) * quarter, quarter, 0)
-
-    arrived = [crossed(shard(step).astype(BF), 4 * step) for step in (1, 2, 3)]
-    mine = shard(0)
+        at = deep ^ step
+        return jnp.concatenate(
+            [
+                lax.dynamic_slice_in_dim(total, at * quarter, quarter, 0).astype(BF),
+                lax.dynamic_slice_in_dim(small, at * part, part, 0),
+            ],
+            axis=0,
+        )
+
+    arrived = [crossed(shard(step), 4 * step) for step in (1, 2, 3)]
+    bulk = lax.dynamic_slice_in_dim(total, deep * quarter, quarter, 0)
+    rest_sum = lax.dynamic_slice_in_dim(small, deep * part, part, 0).astype(F32)
     for other in arrived:
-        mine = mine + other.astype(F32)
-    mine = mine.astype(BF)
+        bulk = bulk + other[:quarter].astype(F32)
+        rest_sum = rest_sum + other[quarter:].astype(F32)
+    mine = jnp.concatenate([bulk.astype(BF), rest_sum.astype(BF)], axis=0)
     pieces = jnp.stack([mine] + [crossed(mine, 4 * step) for step in (1, 2, 3)])
-    pieces = jnp.concatenate([pieces, crossed(pieces, 2)], axis=0)
-    pieces = jnp.concatenate([pieces, crossed(pieces, 1)], axis=0)
-    index = jnp.arange(16, dtype=jnp.int32)
-    mixed = (core << 3) | (side << 2) | deep
-    return pieces, index ^ mixed.astype(jnp.int32)
+    came = crossed(pieces, 2)
+    bulk = jnp.concatenate([pieces[:, :quarter], came[:, :quarter]], axis=0)
+    small = (pieces[:, quarter:].astype(F32) + came[:, quarter:].astype(F32)).astype(BF)
+    rows = bulk.shape[0] * quarter
+    joined = jnp.concatenate([bulk.reshape(rows, LANES), small.reshape(4 * part, LANES)], axis=0)
+    came = crossed(joined, 1)
+    bulk = jnp.concatenate([bulk, came[:rows].reshape(bulk.shape)], axis=0)
+    mixed = ((core << 3) | (side << 2) | deep).astype(jnp.int32)
+    order = jnp.arange(20, dtype=jnp.int32) & 15
+    order = order ^ jnp.where(jnp.arange(20) < 16, mixed, deep.astype(jnp.int32))
+    return bulk, small, came[rows:].reshape(small.shape), order
 
 
 def shards(levels, ocean, stem, dw_kernel, ln_gain, w_in, w_out, layer_scale, upstream):
@@ -517,6 +597,7 @@
     is_top = me // TX == rows - 1
     count = levels.shape[2]
     top = is_top.astype(jnp.int32)[None]
+    taps = dw_kernel.transpose(1, 0, 2)
     tile, strip, folded = pl.pallas_call(
         prepare_kernel,
         out_shape=[
@@ -552,22 +633,34 @@
 
     count0 = RH * RW
     hidden = w_in.shape[2]
-    result, packed = pl.pallas_call(
+    ring_shapes = [
+        jax.ShapeDtypeStruct((8, LANES), F32),
+        jax.ShapeDtypeStruct((EH * EW, LANES), BF),
+        jax.ShapeDtypeStruct((EH * EW, LANES), BF),
+        jax.ShapeDtypeStruct((RH * RW, LANES), BF),
+        jax.ShapeDtypeStruct((RH * RW, LANES), BF),
+        jax.ShapeDtypeStruct((TH * TW, LANES), BF),
+        jax.ShapeDtypeStruct((RH * RW, LANES), F32),
+    ]
+    result, packed, *ring = pl.pallas_call(
         functools.partial(main_kernel, 1.0 / math.sqrt(size * count)),
         out_shape=[
             jax.ShapeDtypeStruct((count, LANES), BF),
-            jax.ShapeDtypeStruct((PACKED, LANES), BF),
-        ],
+            jax.ShapeDtypeStruct((BULK, LANES), BF),
+        ]
+        + ring_shapes,
         in_specs=[smem()] + vmem(5) + [pl.BlockSpec(memory_space=pltpu.HBM)] * 7,
-        out_specs=vmem(2),
+        out_specs=vmem(9),
         scratch_shapes=[
             scratch(EH, EW, LANES),
             scratch(EH, EW, LANES),
-            scratch(EH, EW, LANES),
             scratch(RH, RW, LANES),
-            scratch(LANES, 2 * LANES),
             scratch(49, 8, LANES),
             scratch(49, 8, LANES),
+            scratch(TH, EW, LANES),
+            scratch(RH, RW, LANES),
+            scratch(EH, EW, LANES),
+            scratch(LANES, 2 * LANES),
             scratch(49, 8, LANES),
             scratch(count0, LANES),
             scratch(count0, LANES),
@@ -586,14 +679,6 @@
             scratch(count0, hidden),
             scratch(count0, LANES, dtype=BF),
             scratch(count0, hidden, dtype=BF),
-            scratch(RH, EW + 8, LANES),
-            scratch(TH, EW, LANES),
-            scratch(RH, RW, LANES),
-            scratch(EH, EW, LANES),
-            scratch(49, 8, LANES),
-            scratch(49, 8, LANES),
-            scratch(49, 8, LANES),
-            scratch(SMALL_ROWS, LANES),
             pltpu.VMEM(stem.shape, BF),
             scratch(dw_kernel.shape[1], dw_kernel.shape[0], LANES),
             scratch(*ln_gain.shape),
@@ -603,7 +688,7 @@
             scratch(count, LANES, dtype=BF),
             pltpu.SemaphoreType.DMA((7,)),
         ],
-        compiler_params=pltpu.CompilerParams(vmem_limit_bytes=28 << 20),
+        compiler_params=pltpu.CompilerParams(vmem_limit_bytes=20 << 20),
     )(
         top,
         tile,
@@ -612,24 +697,48 @@
         south,
         north,
         stem,
-        dw_kernel.transpose(1, 0, 2),
+        taps,
         ln_gain,
         w_in,
         w_out,
         layer_scale,
         upstream[0],
     )
-    pieces, order = summed_pieces(packed)
+
+    def rest(top):
+        return pl.pallas_call(
+            rest_kernel,
+            out_shape=jax.ShapeDtypeStruct((SMALL, LANES), BF),
+            in_specs=[smem()] + vmem(8),
+            out_specs=vmem(1)[0],
+            scratch_shapes=[
+                scratch(SMALL, LANES),
+                scratch(EH, EW, LANES),
+                scratch(RH, RW, LANES),
+                scratch(RH, EW + 8, LANES),
+                scratch(TH, EW, LANES),
+                scratch(49, 8, LANES),
+                scratch(49, 8, LANES),
+                scratch(EH, EW, LANES),
+                scratch(49, 8, LANES),
+                scratch(49, 8, LANES),
+                scratch(49, 8, LANES),
+            ],
+            compiler_params=pltpu.CompilerParams(vmem_limit_bytes=10 << 20),
+            cost_estimate=pl.CostEstimate(flops=10_000_000_000, bytes_accessed=4_000_000, transcendentals=0),
+        )(top, taps, *ring)
+
+    pieces, mine, other, order = summed_pieces(packed, top, rest)
     shapes = [array.shape for array in (stem, dw_kernel, ln_gain, w_in, w_out, layer_scale)]
     shapes[1] = (shapes[1][1], shapes[1][0], shapes[1][2])
     grads = pl.pallas_call(
         unpack_kernel,
         out_shape=[jax.ShapeDtypeStruct(shape, F32) for shape in shapes],
-        in_specs=[smem()] + vmem(1),
+        in_specs=[smem()] + vmem(3),
         out_specs=vmem(6),
-        scratch_shapes=[scratch(PACKED, LANES)],
+        scratch_shapes=[scratch(BULK, LANES), scratch(SMALL, LANES)],
         compiler_params=pltpu.CompilerParams(vmem_limit_bytes=8 << 20),
-    )(order, pieces)
+    )(order, pieces, mine, other)
     grads = list(grads)
     grads[1] = grads[1].transpose(1, 0, 2)
     return (result[None], *grads)

time: 66.6 us -> 62 us (0.931)
  waiting for transfers between devices: 22.4 us -> 19.3 us
  starting transfers between devices: 22.6 us -> 21 us
    pallas_call x1, Pallas kernels: 15.8 us -> 9.97 us  [shards(): pl.pallas_call(functools.partial(main_kernel, 1.0 / math.sqrt(size * coun...]
    pallas_call x0 -> x1, Pallas kernels: none -> 5.77 us  [rest(): pl.pallas_call(rest_kernel, out_shape=jax.ShapeDtypeStruct((SMALL, LANES)...]
    ppermute x14, waiting for transfers between devices: 22.4 us -> 19.3 us  [permuted(): return lax.ppermute(value, 'gy', pairs)]
    ppermute x14, starting transfers between devices: 22.6 us -> 21 us  [permuted(): return lax.ppermute(value, 'gy', pairs)]
    unnamed x22 -> x18, local copies, waits for them, and re-layouts: 2.28 us -> 2.23 us
  transfers between devices with their start and end apart: 14 -> 14, of which waited for: 10 -> 10; matrix products, arithmetic and copies ran while one was open for 0% -> 0% of each run, Pallas kernels for 0% -> 9%
where the time goes in v3:
time: 62 us; the launch traced here: 61.8 us
  starting transfers between devices  21 us (34%)
  waiting for transfers between devices  19.3 us (31%)
  Pallas kernels  17.8 us (29%)
  local copies, waits for them, and re-layouts  2.34 us (4%)
  between operations  0.97 us (2%)
    ppermute x14, starting transfers between devices, permuted(): return lax.ppermute(value, 'gy', pairs)  21 us
    ppermute x14, waiting for transfers between devices, permuted(): return lax.ppermute(value, 'gy', pairs)  19.3 us
    pallas_call x1, Pallas kernels, shards(): pl.pallas_call(functools.partial(main_kernel, 1.0 / math.sqrt(size * coun...  9.97 us
    pallas_call x1, Pallas kernels, rest(): pl.pallas_call(rest_kernel, out_shape=jax.ShapeDtypeStruct((SMALL, LANES)...  5.77 us
    unnamed x18, local copies, waits for them, and re-layouts  2.23 us
    pallas_call x1, Pallas kernels, shards(): pl.pallas_call(unpack_kernel, out_shape=[jax.ShapeDtypeStruct(shape, F32)...  1.61 us
  transfers between devices with their start and end apart: 14, of which 10 were waited for; matrix products, arithmetic and copies ran while one was open for 0% of the time, Pallas kernels for 9%

profile of v3, /device:TPU:0, one launch (start us, length us, event | category | flops | bytes accessed | tf_op | source)
XLA Modules:
  0.0 61.8 jit_solution(14091102938101737511)
XLA Ops:
  0.7 0.0 copy-start.6
  0.7 0.7 %copy-done.6 = s32[1,512]{1,0:T(1,128)S(1)} copy-done((s32[1,512]{1,0:T(1,128)S(1)}, s32[1,512]{1,0:T(1,128)}, u32[]{:S(2)}) %copy-start.6) | copy-done | bytes 2072
  1.3 0.0 copy-start.3
  1.3 0.9 %copy-done.3 = bf16[1,75,512]{2,1,0:T(8,128)(2,1)S(1)} copy-done((bf16[1,75,512]{2,1,0:T(8,128)(2,1)S(1)}, bf16[1,75,512]{2,1,0:T(8,128)(2,1)}, u32[]{:S(2)}) %copy-start.3) | copy-done | bytes 76824
  2.2 0.0 copy-start.4
  2.2 0.4 shard_map.144
  2.6 4.1 %collective-permute-start = (bf16[6,32,128]{2,1,0:T(8,128)(2,1)S(1)}, bf16[6,32,128]{2,1,0:T(8,128)(2,1)S(1)}, u32[]{:S(2)}, u32[]{:S(2)}) collective-permute-start(bf16[6,32,128]{2,1,0:T(8,128)(2,1)S(1)} %get-tuple-element.28), channel_id=1, source_target_pairs={{0,8},{1,9},{2,10},{3,11},{4,12},{5,13},{6,14},{7,15},{8,0},{9,1},... | collective-permute-start | bytes 147464 | tf_op jit(solution)/shard_map/ppermute | solution.py:532
  6.7 0.7 %collective-permute-start.1 = (bf16[6,32,128]{2,1,0:T(8,128)(2,1)S(1)}, bf16[6,32,128]{2,1,0:T(8,128)(2,1)S(1)}, u32[]{:S(2)}, u32[]{:S(2)}) collective-permute-start(bf16[6,32,128]{2,1,0:T(8,128)(2,1)S(1)} %get-tuple-element.29), channel_id=1, source_target_pairs={{8,15},{9,14},{10,13},{11,12},{12,11},{13,10},{14,9},{15,8},{24,31... | collective-permute-start | bytes 147464 | tf_op jit(solution)/shard_map/ppermute | solution.py:532
  7.4 0.0 copy-start.2
  7.4 0.0 copy-start
  7.4 0.0 copy-start.1
  7.4 1.9 %collective-permute-done = bf16[6,32,128]{2,1,0:T(8,128)(2,1)S(1)} collective-permute-done((bf16[6,32,128]{2,1,0:T(8,128)(2,1)S(1)}, bf16[6,32,128]{2,1,0:T(8,128)(2,1)S(1)}, u32[]{:S(2)}, u32[]{:S(2)}) %collective-permute-start) | collective-permute-done | bytes 49184 | tf_op jit(solution)/shard_map/ppermute | solution.py:532
  9.3 0.0 collective-permute-done.1
  9.4 0.1 collective-permute-start.2
  9.5 0.0 copy-start.5
  9.5 0.0 copy-start.8
  9.5 2.7 %collective-permute-start.3 = (bf16[28,8,128]{2,1,0:T(8,128)(2,1)S(1)}, bf16[28,8,128]{2,1,0:T(8,128)(2,1)S(1)}, u32[]{:S(2)}, u32[]{:S(2)}) collective-permute-start(bf16[28,8,128]{2,1,0:T(8,128)(2,1)S(1)} %pad_maximum_fusion.5), channel_id=1, source_target_pairs={{0,7},{1,0},{2,1},{3,2},{4,3},{5,4},{6,5},{7,6},{8,15},{9,8},{10,9... | collective-permute-start | bytes 172040 | tf_op jit(solution)/shard_map/ppermute | solution.py:532
  12.2 1.8 %collective-permute-done.2.west_ref = bf16[28,8,128]{2,1,0:T(8,128)(2,1)S(1)} collective-permute-done((bf16[28,8,128]{2,1,0:T(8,128)(2,1)S(1)}, bf16[28,8,128]{2,1,0:T(8,128)(2,1)S(1)}, u32[]{:S(2)}, u32[]{:S(2)}) %collective-permute-start.2) | collective-permute-done | bytes 57376 | tf_op jit(solution)/shard_map/ppermute | solution.py:532
  13.9 0.0 collective-permute-done.3.east_ref
  14.0 0.0 copy-start.7
  14.0 0.0 copy-done.4
  14.0 0.0 copy-done.2
  14.0 0.0 copy-done
  14.0 0.0 copy-done.1
  14.0 0.0 copy-done.5
  14.0 0.0 copy-done.8
  14.0 0.6 %copy-done.7 = f32[2,128]{1,0:T(2,128)S(1)} copy-done((f32[2,128]{1,0:T(2,128)S(1)}, f32[2,128]{1,0:T(2,128)}, u32[]{:S(2)}) %copy-start.7) | copy-done | bytes 1048
  14.7 10.0 %shard_map.145 = (bf16[512,128]{1,0:T(8,128)(2,1)}, bf16[2048,128]{1,0:T(8,128)(2,1)S(1)}, f32[8,128]{1,0:T(8,128)S(1)}, bf16[1344,128]{1,0:T(8,128)(2,1)S(1)}, ...) custom-call(s32[1]{0:T(128)} %bitcast.top_ref, ...), custom_call_target="tpu_custom_call" | custom-call | tf_op jit(solution)/shard_map/pallas_call | solution.py:645
  24.7 1.0 %collective-permute-start.4 = (bf16[1024,128]{1,0:T(8,128)(2,1)S(1)}, bf16[1024,128]{1,0:T(8,128)(2,1)S(1)}, u32[]{:S(2)}, u32[]{:S(2)}) collective-permute-start(bf16[1024,128]{1,0:T(8,128)(2,1)S(1)} %broadcast_select_fusion), channel_id=1, source_target_pairs={{0,1},{1,0},{2,3},{3,2},{4,5},{5,4},{6,7},{7,6},{8,9},{9,8},{10,11... | collective-permute-start | bytes 786440 | tf_op jit(solution)/shard_map/ppermute | solution.py:532
  25.7 1.2 %collective-permute-done.4 = bf16[1024,128]{1,0:T(8,128)(2,1)S(1)} collective-permute-done((bf16[1024,128]{1,0:T(8,128)(2,1)S(1)}, bf16[1024,128]{1,0:T(8,128)(2,1)S(1)}, u32[]{:S(2)}, u32[]{:S(2)}) %collective-permute-start.4) | collective-permute-done | bytes 262176 | tf_op jit(solution)/shard_map/ppermute | solution.py:532
  26.8 0.1 convert_add_fusion
  27.0 2.1 %collective-permute-start.5 = (bf16[512,128]{1,0:T(8,128)(2,1)S(1)}, bf16[512,128]{1,0:T(8,128)(2,1)S(1)}, u32[]{:S(2)}, u32[]{:S(2)}) collective-permute-start(bf16[512,128]{1,0:T(8,128)(2,1)S(1)} %select_convert_fusion), channel_id=1, source_target_pairs={{0,2},{1,3},{2,0},{3,1},{4,6},{5,7},{6,4},{7,5},{8,10},{9,11},{10,... | collective-permute-start | bytes 393224 | tf_op jit(solution)/shard_map/ppermute | solution.py:532
  29.1 5.8 %shard_map.146 = bf16[192,128]{1,0:T(8,128)(2,1)S(1)} custom-call(s32[1]{0:T(128)} %bitcast.top_ref, f32[49,2,128]{2,1,0:T(2,128)S(1)} %bitcast.20, f32[8,128]{1,0:T(8,128)S(1)} %get-tuple-element.34.sums, bf16[1344,128]{1,0:T(8,128)(2,1)S(1)} %get-tuple-element.35.cells, bf16[1344,128]{1,0:T(8,128)(2,1)S(1)} %get-tuple-element.36.flat0, ...), custom_call_target="tpu_custom_call" | custom-call | flops 10000000000 | bytes 4000000 | tf_op jit(solution)/shard_map/pallas_call | solution.py:709
  34.9 0.0 collective-permute-done.5
  35.0 4.0 %collective-permute-start.8 = (bf16[176,128]{1,0:T(8,128)(2,1)S(1)}, bf16[176,128]{1,0:T(8,128)(2,1)S(1)}, u32[]{:S(2)}, u32[]{:S(2)}) collective-permute-start(bf16[176,128]{1,0:T(8,128)(2,1)S(1)} %pad_maximum_fusion.8), channel_id=1, source_target_pairs={{0,12},{1,13},{2,14},{3,15},{4,8},{5,9},{6,10},{7,11},{8,4},{9,5},... | collective-permute-start | bytes 135176 | tf_op jit(solution)/shard_map/ppermute | solution.py:532
  39.0 1.1 %collective-permute-start.7 = (bf16[176,128]{1,0:T(8,128)(2,1)S(1)}, bf16[176,128]{1,0:T(8,128)(2,1)S(1)}, u32[]{:S(2)}, u32[]{:S(2)}) collective-permute-start(bf16[176,128]{1,0:T(8,128)(2,1)S(1)} %pad_maximum_fusion.7), channel_id=1, source_target_pairs={{0,8},{1,9},{2,10},{3,11},{4,12},{5,13},{6,14},{7,15},{8,0},{9,1},... | collective-permute-start | bytes 135176 | tf_op jit(solution)/shard_map/ppermute | solution.py:532
  40.1 0.5 collective-permute-start.6
  40.7 0.3 collective-permute-done.8
  41.0 3.4 %collective-permute-done.7 = bf16[176,128]{1,0:T(8,128)(2,1)S(1)} collective-permute-done((bf16[176,128]{1,0:T(8,128)(2,1)S(1)}, bf16[176,128]{1,0:T(8,128)(2,1)S(1)}, u32[]{:S(2)}, u32[]{:S(2)}) %collective-permute-start.7) | collective-permute-done | bytes 45088 | tf_op jit(solution)/shard_map/ppermute | solution.py:532
  44.4 0.2 collective-permute-done.6
  44.7 3.1 %collective-permute-start.11 = (bf16[176,128]{1,0:T(8,128)(2,1)S(1)}, bf16[176,128]{1,0:T(8,128)(2,1)S(1)}, u32[]{:S(2)}, u32[]{:S(2)}) collective-permute-start(bf16[176,128]{1,0:T(8,128)(2,1)S(1)} %get-tuple-element.62), channel_id=1, source_target_pairs={{0,12},{1,13},{2,14},{3,15},{4,8},{5,9},{6,10},{7,11},{8,4},{9,5},... | collective-permute-start | bytes 135176 | tf_op jit(solution)/shard_map/ppermute | solution.py:532
  47.8 0.0 collective-permute-start.10
  47.8 1.3 %collective-permute-start.9 = (bf16[176,128]{1,0:T(8,128)(2,1)S(1)}, bf16[176,128]{1,0:T(8,128)(2,1)S(1)}, u32[]{:S(2)}, u32[]{:S(2)}) collective-permute-start(bf16[176,128]{1,0:T(8,128)(2,1)S(1)} %get-tuple-element.62), channel_id=1, source_target_pairs={{0,4},{1,5},{2,6},{3,7},{4,0},{5,1},{6,2},{7,3},{8,12},{9,13},{10,... | collective-permute-start | bytes 135176 | tf_op jit(solution)/shard_map/ppermute | solution.py:532
  49.1 1.5 %collective-permute-done.11 = bf16[176,128]{1,0:T(8,128)(2,1)S(1)} collective-permute-done((bf16[176,128]{1,0:T(8,128)(2,1)S(1)}, bf16[176,128]{1,0:T(8,128)(2,1)S(1)}, u32[]{:S(2)}, u32[]{:S(2)}) %collective-permute-start.11) | collective-permute-done | bytes 45088 | tf_op jit(solution)/shard_map/ppermute | solution.py:532
  50.6 2.1 %collective-permute-done.10 = bf16[176,128]{1,0:T(8,128)(2,1)S(1)} collective-permute-done((bf16[176,128]{1,0:T(8,128)(2,1)S(1)}, bf16[176,128]{1,0:T(8,128)(2,1)S(1)}, u32[]{:S(2)}, u32[]{:S(2)}) %collective-permute-start.10) | collective-permute-done | bytes 45088 | tf_op jit(solution)/shard_map/ppermute | solution.py:532
  52.8 0.0 collective-permute-done.9
  52.8 0.2 collective-permute-start.12
  53.0 5.3 %collective-permute-done.12 = bf16[4,176,128]{2,1,0:T(8,128)(2,1)S(1)} collective-permute-done((bf16[4,176,128]{2,1,0:T(8,128)(2,1)S(1)}, bf16[4,176,128]{2,1,0:T(8,128)(2,1)S(1)}, u32[]{:S(2)}, u32[]{:S(2)}) %collective-permute-start.12) | collective-permute-done | bytes 180256 | tf_op jit(solution)/shard_map/ppermute | solution.py:532
  58.5 0.1 collective-permute-start.13
  58.6 1.6 %collective-permute-done.13 = bf16[1216,128]{1,0:T(8,128)(2,1)S(1)} collective-permute-done((bf16[1216,128]{1,0:T(8,128)(2,1)S(1)}, bf16[1216,128]{1,0:T(8,128)(2,1)S(1)}, u32[]{:S(2)}, u32[]{:S(2)}) %collective-permute-start.13) | collective-permute-done | bytes 311328 | tf_op jit(solution)/shard_map/ppermute | solution.py:532
  60.1 0.1 pad_maximum_fusion.pieces_ref
  60.2 1.6 %shard_map.147 = (f32[75,128]{1,0:T(8,128)}, f32[49,2,128]{2,1,0:T(2,128)}, f32[2,128]{1,0:T(2,128)}, f32[2,128,512]{2,1,0:T(8,128)}, f32[2,512,128]{2,1,0:T(8,128)}, /*index=5*/f32[2,128]{1,0:T(2,128)}) custom-call(s32[20]{0:T(128)S(1)} %fusion.order_ref, bf16[16,128,128]{2,1,0:T(8,128)(2,1)S(1)} %pad_maximum_fusion.pieces_ref, ...), custom_call_target="tpu_custom_call" | custom-call | tf_op jit(solution)/shard_map/pallas_call | solution.py:734
  (25 shorter events, 0.4 us)
Async XLA Ops:
  0.7 0.7 %copy-start.6 = (s32[1,512]{1,0:T(1,128)S(1)}, s32[1,512]{1,0:T(1,128)}, u32[]{:S(2)}) copy-start(s32[1,512]{1,0:T(1,128)} %ocean_ref.1) | copy-start | bytes 6148
  1.3 0.9 %copy-start.3 = (bf16[1,75,512]{2,1,0:T(8,128)(2,1)S(1)}, bf16[1,75,512]{2,1,0:T(8,128)(2,1)}, u32[]{:S(2)}) copy-start(bf16[1,75,512]{2,1,0:T(8,128)(2,1)} %param.9) | copy-start | bytes 230404
  2.2 11.8 %copy-start.4 = (f32[2,49,128]{2,0,1:T(2,128)S(1)}, f32[2,49,128]{2,0,1:T(2,128)}, u32[]{:S(2)}) copy-start(f32[2,49,128]{2,0,1:T(2,128)} %param.12) | copy-start | bytes 150532
  2.6 6.7 %collective-permute-start = (bf16[6,32,128]{2,1,0:T(8,128)(2,1)S(1)}, bf16[6,32,128]{2,1,0:T(8,128)(2,1)S(1)}, u32[]{:S(2)}, u32[]{:S(2)}) collective-permute-start(bf16[6,32,128]{2,1,0:T(8,128)(2,1)S(1)} %get-tuple-element.28), channel_id=1, source_target_pairs={{0,8},{1,9},{2,10},{3,11},{4,12},{5,13},{6,14},{7,15},{8,0},{9,1},... | collective-permute-start | bytes 147464 | tf_op jit(solution)/shard_map/ppermute | solution.py:532
  6.7 2.6 %collective-permute-start.1 = (bf16[6,32,128]{2,1,0:T(8,128)(2,1)S(1)}, bf16[6,32,128]{2,1,0:T(8,128)(2,1)S(1)}, u32[]{:S(2)}, u32[]{:S(2)}) collective-permute-start(bf16[6,32,128]{2,1,0:T(8,128)(2,1)S(1)} %get-tuple-element.29), channel_id=1, source_target_pairs={{8,15},{9,14},{10,13},{11,12},{12,11},{13,10},{14,9},{15,8},{24,31... | collective-permute-start | bytes 147464 | tf_op jit(solution)/shard_map/ppermute | solution.py:532
  7.4 6.6 %copy-start.2 = (bf16[1,512,128]{2,1,0:T(8,128)(2,1)S(1)}, bf16[1,512,128]{2,1,0:T(8,128)(2,1)}, u32[]{:S(2)}) copy-start(bf16[1,512,128]{2,1,0:T(8,128)(2,1)} %param.17) | copy-start | bytes 393220
  7.4 6.6 %copy-start = (bf16[2,128,512]{2,1,0:T(8,128)(2,1)S(1)}, bf16[2,128,512]{2,1,0:T(8,128)(2,1)}, u32[]{:S(2)}) copy-start(bf16[2,128,512]{2,1,0:T(8,128)(2,1)} %win_hbm.1) | copy-start | bytes 786436
  7.4 6.6 %copy-start.1 = (bf16[2,512,128]{2,1,0:T(8,128)(2,1)S(1)}, bf16[2,512,128]{2,1,0:T(8,128)(2,1)}, u32[]{:S(2)}) copy-start(bf16[2,512,128]{2,1,0:T(8,128)(2,1)} %wout_hbm.1) | copy-start | bytes 786436
  9.4 4.6 %collective-permute-start.2 = (bf16[28,8,128]{2,1,0:T(8,128)(2,1)S(1)}, bf16[28,8,128]{2,1,0:T(8,128)(2,1)S(1)}, u32[]{:S(2)}, u32[]{:S(2)}) collective-permute-start(bf16[28,8,128]{2,1,0:T(8,128)(2,1)S(1)} %pad_maximum_fusion.4), channel_id=1, source_target_pairs={{0,1},{1,2},{2,3},{3,4},{4,5},{5,6},{6,7},{7,0},{8,9},{9,10},{10,1... | collective-permute-start | bytes 172040 | tf_op jit(solution)/shard_map/ppermute | solution.py:532
  9.5 4.6 %copy-start.5 = (bf16[75,128]{1,0:T(8,128)(2,1)S(1)}, bf16[75,128]{1,0:T(8,128)(2,1)}, u32[]{:S(2)}) copy-start(bf16[75,128]{1,0:T(8,128)(2,1)} %stem_hbm.1) | copy-start | bytes 57604
  9.5 4.6 %copy-start.8 = (f32[2,128]{1,0:T(2,128)S(1)}, f32[2,128]{1,0:T(2,128)}, u32[]{:S(2)}) copy-start(f32[2,128]{1,0:T(2,128)} %scale_hbm.1) | copy-start | bytes 3076
  9.5 4.5 %collective-permute-start.3 = (bf16[28,8,128]{2,1,0:T(8,128)(2,1)S(1)}, bf16[28,8,128]{2,1,0:T(8,128)(2,1)S(1)}, u32[]{:S(2)}, u32[]{:S(2)}) collective-permute-start(bf16[28,8,128]{2,1,0:T(8,128)(2,1)S(1)} %pad_maximum_fusion.5), channel_id=1, source_target_pairs={{0,7},{1,0},{2,1},{3,2},{4,3},{5,4},{6,5},{7,6},{8,15},{9,8},{10,9... | collective-permute-start | bytes 172040 | tf_op jit(solution)/shard_map/ppermute | solution.py:532
  14.0 0.7 %copy-start.7 = (f32[2,128]{1,0:T(2,128)S(1)}, f32[2,128]{1,0:T(2,128)}, u32[]{:S(2)}) copy-start(f32[2,128]{1,0:T(2,128)} %gain_hbm.1) | copy-start | bytes 3076
  24.7 2.2 %collective-permute-start.4 = (bf16[1024,128]{1,0:T(8,128)(2,1)S(1)}, bf16[1024,128]{1,0:T(8,128)(2,1)S(1)}, u32[]{:S(2)}, u32[]{:S(2)}) collective-permute-start(bf16[1024,128]{1,0:T(8,128)(2,1)S(1)} %broadcast_select_fusion), channel_id=1, source_target_pairs={{0,1},{1,0},{2,3},{3,2},{4,5},{5,4},{6,7},{7,6},{8,9},{9,8},{10,11... | collective-permute-start | bytes 786440 | tf_op jit(solution)/shard_map/ppermute | solution.py:532
  27.0 7.9 %collective-permute-start.5 = (bf16[512,128]{1,0:T(8,128)(2,1)S(1)}, bf16[512,128]{1,0:T(8,128)(2,1)S(1)}, u32[]{:S(2)}, u32[]{:S(2)}) collective-permute-start(bf16[512,128]{1,0:T(8,128)(2,1)S(1)} %select_convert_fusion), channel_id=1, source_target_pairs={{0,2},{1,3},{2,0},{3,1},{4,6},{5,7},{6,4},{7,5},{8,10},{9,11},{10,... | collective-permute-start | bytes 393224 | tf_op jit(solution)/shard_map/ppermute | solution.py:532
  35.0 6.0 %collective-permute-start.8 = (bf16[176,128]{1,0:T(8,128)(2,1)S(1)}, bf16[176,128]{1,0:T(8,128)(2,1)S(1)}, u32[]{:S(2)}, u32[]{:S(2)}) collective-permute-start(bf16[176,128]{1,0:T(8,128)(2,1)S(1)} %pad_maximum_fusion.8), channel_id=1, source_target_pairs={{0,12},{1,13},{2,14},{3,15},{4,8},{5,9},{6,10},{7,11},{8,4},{9,5},... | collective-permute-start | bytes 135176 | tf_op jit(solution)/shard_map/ppermute | solution.py:532
  39.0 5.4 %collective-permute-start.7 = (bf16[176,128]{1,0:T(8,128)(2,1)S(1)}, bf16[176,128]{1,0:T(8,128)(2,1)S(1)}, u32[]{:S(2)}, u32[]{:S(2)}) collective-permute-start(bf16[176,128]{1,0:T(8,128)(2,1)S(1)} %pad_maximum_fusion.7), channel_id=1, source_target_pairs={{0,8},{1,9},{2,10},{3,11},{4,12},{5,13},{6,14},{7,15},{8,0},{9,1},... | collective-permute-start | bytes 135176 | tf_op jit(solution)/shard_map/ppermute | solution.py:532
  40.1 4.5 %collective-permute-start.6 = (bf16[176,128]{1,0:T(8,128)(2,1)S(1)}, bf16[176,128]{1,0:T(8,128)(2,1)S(1)}, u32[]{:S(2)}, u32[]{:S(2)}) collective-permute-start(bf16[176,128]{1,0:T(8,128)(2,1)S(1)} %pad_maximum_fusion.6), channel_id=1, source_target_pairs={{0,4},{1,5},{2,6},{3,7},{4,0},{5,1},{6,2},{7,3},{8,12},{9,13},{10,... | collective-permute-start | bytes 135176 | tf_op jit(solution)/shard_map/ppermute | solution.py:532
  44.7 5.9 %collective-permute-start.11 = (bf16[176,128]{1,0:T(8,128)(2,1)S(1)}, bf16[176,128]{1,0:T(8,128)(2,1)S(1)}, u32[]{:S(2)}, u32[]{:S(2)}) collective-permute-start(bf16[176,128]{1,0:T(8,128)(2,1)S(1)} %get-tuple-element.62), channel_id=1, source_target_pairs={{0,12},{1,13},{2,14},{3,15},{4,8},{5,9},{6,10},{7,11},{8,4},{9,5},... | collective-permute-start | bytes 135176 | tf_op jit(solution)/shard_map/ppermute | solution.py:532
  47.8 4.9 %collective-permute-start.10 = (bf16[176,128]{1,0:T(8,128)(2,1)S(1)}, bf16[176,128]{1,0:T(8,128)(2,1)S(1)}, u32[]{:S(2)}, u32[]{:S(2)}) collective-permute-start(bf16[176,128]{1,0:T(8,128)(2,1)S(1)} %get-tuple-element.62), channel_id=1, source_target_pairs={{0,8},{1,9},{2,10},{3,11},{4,12},{5,13},{6,14},{7,15},{8,0},{9,1},... | collective-permute-start | bytes 135176 | tf_op jit(solution)/shard_map/ppermute | solution.py:532
  47.8 4.9 %collective-permute-start.9 = (bf16[176,128]{1,0:T(8,128)(2,1)S(1)}, bf16[176,128]{1,0:T(8,128)(2,1)S(1)}, u32[]{:S(2)}, u32[]{:S(2)}) collective-permute-start(bf16[176,128]{1,0:T(8,128)(2,1)S(1)} %get-tuple-element.62), channel_id=1, source_target_pairs={{0,4},{1,5},{2,6},{3,7},{4,0},{5,1},{6,2},{7,3},{8,12},{9,13},{10,... | collective-permute-start | bytes 135176 | tf_op jit(solution)/shard_map/ppermute | solution.py:532
  52.8 5.6 %collective-permute-start.12 = (bf16[4,176,128]{2,1,0:T(8,128)(2,1)S(1)}, bf16[4,176,128]{2,1,0:T(8,128)(2,1)S(1)}, u32[]{:S(2)}, u32[]{:S(2)}) collective-permute-start(bf16[4,176,128]{2,1,0:T(8,128)(2,1)S(1)} %pad_maximum_fusion.3), channel_id=1, source_target_pairs={{0,2},{1,3},{2,0},{3,1},{4,6},{5,7},{6,4},{7,5},{8,10},{9,11},{10,... | collective-permute-start | bytes 540680 | tf_op jit(solution)/shard_map/ppermute | solution.py:532
  58.5 1.7 %collective-permute-start.13 = (bf16[1216,128]{1,0:T(8,128)(2,1)S(1)}, bf16[1216,128]{1,0:T(8,128)(2,1)S(1)}, u32[]{:S(2)}, u32[]{:S(2)}) collective-permute-start(bf16[1216,128]{1,0:T(8,128)(2,1)S(1)} %pad_maximum_fusion.1), channel_id=1, source_target_pairs={{0,1},{1,0},{2,3},{3,2},{4,5},{5,4},{6,7},{7,6},{8,9},{9,8},{10,11... | collective-permute-start | bytes 933896 | tf_op jit(solution)/shard_map/ppermute | solution.py:532

commit v4 on v3

--- a/solution.py
+++ b/solution.py
@@ -18,6 +18,7 @@
 EH, EW = TH + 2 * RIM, TW + 2 * PADC
 RH, RW = TH + 6, 40
 RING_COL = 5
+MID, MID_ROWS = 6, 10
 
 C0 = 0.7978845608028654
 C1 = 0.7978845608028654 * 0.044715
@@ -27,6 +28,8 @@
 STEM_AT, KERNEL_AT, GAIN_AT, SCALE_AT = 0, (75, 124), 173, 175
 SMALL = 192
 
+STEPS = (3, 2, 1)
+
 BF = jnp.bfloat16
 F32 = jnp.float32
 
@@ -47,23 +50,35 @@
     return lax.dot_general(left, right, (((1,), (1,)), ((), ())), preferred_element_type=F32)
 
 
-def prepare_kernel(top_ref, levels_ref, ocean_ref, tile_ref, strip_ref, fold_ref, stage):
+def prepare_kernel(levels_hbm, ocean_hbm, tile_ref, west_ref, east_ref, fold_ref, stage, levels_ref, ocean_ref, arrived):
     count, cells = levels_ref.shape
+    loads = [
+        pltpu.make_async_copy(levels_hbm, levels_ref, arrived.at[0]),
+        pltpu.make_async_copy(ocean_hbm, ocean_ref, arrived.at[1]),
+    ]
+    for load in loads:
+        load.start()
     stage[...] = jnp.zeros_like(stage)
+    for load in loads:
+        load.wait()
     stage[0:count, :] = levels_ref[...].astype(F32)
     stage[count : count + 1, :] = ocean_ref[...].astype(F32)
     rows = lax.broadcasted_iota(jnp.int32, (LANES, LANES), 0)
     cols = lax.broadcasted_iota(jnp.int32, (LANES, LANES), 1)
     eye = (rows == cols).astype(BF)
     turned = contract_rows(stage[...].astype(BF), eye)
-    tile_ref[...] = turned.reshape(TH, TW, LANES).astype(BF)
     side = RIM * TW
-    lower, upper = turned[0:side], turned[cells - side :]
-    strip_ref[...] = jnp.where(top_ref[0] == 1, lower, upper).reshape(RIM, TW, LANES).astype(BF)
     rows = lax.broadcasted_iota(jnp.int32, (side, side), 0)
     cols = lax.broadcasted_iota(jnp.int32, (side, side), 1)
     swap = (rows + cols == side - 1).astype(BF)
-    fold_ref[...] = jnp.dot(swap, upper.astype(BF), preferred_element_type=F32).reshape(RIM, TW, LANES).astype(BF)
+    fold = jnp.dot(swap, turned[cells - side :].astype(BF), preferred_element_type=F32).reshape(RIM, TW, LANES)
+    tile = turned.reshape(TH, TW, LANES)
+    tile_ref[...] = tile.astype(BF)
+    fold_ref[...] = fold.astype(BF)
+    west_ref[0:TH] = tile[:, 0:PADC].astype(BF)
+    west_ref[TH:] = fold[:, TW - PADC :].astype(BF)
+    east_ref[0:TH] = tile[:, TW - PADC :].astype(BF)
+    east_ref[TH:] = fold[:, 0:PADC].astype(BF)
 
 
 def load_column(ref, row, start):
@@ -89,6 +104,110 @@
     return totals
 
 
+def chunks(spans, body):
+    def run(carry):
+        for at in spans:
+            carry = body(at.start // (at.stop - at.start), at, carry)
+        return carry
+
+    return run
+
+
+def spans_of(count, size):
+    return [slice(at, at + size) for at in range(0, count, size)]
+
+
+def norm_rows(conv, xhat, rinv, normed, gain, spans):
+    for at in spans:
+        values = conv[at, :]
+        average = jnp.mean(values, axis=-1, keepdims=True)
+        centered = values - average
+        inverse = lax.rsqrt(jnp.mean(centered * centered, axis=-1, keepdims=True) + NORM_STABILIZER)
+        scaled = centered * inverse
+        xhat[at, :] = scaled
+        rinv[at, :] = jnp.broadcast_to(inverse, values.shape)
+        normed[at, :] = (scaled * gain).astype(BF)
+
+
+def gelu_rows(pre, act, slope, spans):
+    for at in spans:
+        for start in range(at.start, at.stop, 16):
+            here = slice(start, start + 16)
+            v = pre[here, :]
+            square = v * v
+            inner = v * (C0 + C1 * square)
+            half = 0.5 * jnp.tanh(inner) + 0.5
+            active = v * half
+            act[here, :] = active.astype(BF)
+            slope[here, :] = half + active * (1.0 - half) * (2.0 * C0 + (6.0 * C1) * square)
+
+
+def joint_weights(stem_ref, weights):
+    count = stem_ref.shape[0]
+    weights[...] = jnp.zeros_like(weights)
+    weights[0:count, 0:LANES] = stem_ref[...].astype(F32)
+    weights[count : count + 1, LANES:] = jnp.ones((1, LANES), F32)
+    return weights[...].astype(BF)
+
+
+def middle_kernel(
+    tile_ref,
+    west_ref,
+    east_ref,
+    table_ref,
+    stem_ref,
+    win_ref,
+    wout_ref,
+    flat,
+    xhat,
+    rinv,
+    normed,
+    act,
+    slope,
+    branch,
+    ext,
+    x0,
+    m6,
+    weights,
+    taps,
+    conv,
+    wide,
+):
+    joint = joint_weights(stem_ref, weights)
+    spread_taps(table_ref, 0, taps)
+    ext[:, 0:PADC] = west_ref[0:TH].astype(F32)
+    ext[:, PADC : PADC + TW] = tile_ref[...].astype(F32)
+    ext[:, PADC + TW :] = east_ref[0:TH].astype(F32)
+    for row in range(0, TH, 4):
+        at = slice(row, row + 4)
+        both = jnp.dot(ext[at].reshape(4 * EW, LANES).astype(BF), joint, preferred_element_type=F32)
+        mask = both[:, LANES:]
+        m6[at] = mask.reshape(4, EW, LANES)
+        x0[at] = (mask * both[:, :LANES]).astype(BF).astype(F32).reshape(4, EW, LANES)
+
+    def conv_columns(block, _):
+        start = pl.multiple_of(block * 8, 8)
+        rows = range(MID, MID + MID_ROWS)
+        totals = conv_block(x0, (taps,), start + 2, rows, range(RIM, RIM + TH), lambda o, r, a, d: (0, a * 7 + d))
+        for o in rows:
+            conv[pl.ds(pl.multiple_of((o - MID) * RW + start, 8), 8), :] = totals[o]
+        return 0
+
+    lax.fori_loop(0, RW // 8, conv_columns, 0)
+    count = MID_ROWS * RW
+    spans = spans_of(count, 2 * RW)
+    norm_rows(conv, xhat, rinv, normed, table_ref[49, 0:1, :], spans)
+    wide[...] = jnp.dot(normed[...], win_ref[0], preferred_element_type=F32)
+    gelu_rows(wide, act, slope, spans)
+    branch[...] = jnp.dot(act[...], wout_ref[0], preferred_element_type=F32)
+    for index, at in enumerate(spans):
+        rows = slice(index * 2 + MID + 3 - RIM, index * 2 + MID + 5 - RIM)
+        mask = m6[rows, RING_COL : RING_COL + RW, :]
+        held = x0[rows, RING_COL : RING_COL + RW, :]
+        value = mask * (held + table_ref[50, 0:1, :] * branch[at, :].reshape(2, RW, LANES))
+        flat[at, :] = value.reshape(2 * RW, LANES).astype(BF)
+
+
 def spread_taps(dw_ref, layer, taps, top=None):
     for t in range(49):
         row = dw_ref[t, layer : layer + 1, :]
@@ -114,13 +233,18 @@
     east_ref,
     south_ref,
     north_ref,
-    stem_hbm,
-    dw_hbm,
-    gain_hbm,
-    win_hbm,
-    wout_hbm,
-    scale_hbm,
-    up_hbm,
+    table_ref,
+    stem_ref,
+    win_ref,
+    wout_ref,
+    up_ref,
+    mid_flat,
+    mid_xhat,
+    mid_rinv,
+    mid_normed,
+    mid_act,
+    mid_slope,
+    mid_branch,
     out_ref,
     packed_ref,
     sums,
@@ -157,47 +281,29 @@
     wide,
     thin,
     gpre,
-    stem_ref,
-    dw_ref,
-    gain_ref,
-    win_ref,
-    wout_ref,
-    scale_ref,
-    up_ref,
-    arrived,
 ):
     top = top_ref[0] == 1
-    levels_count = stem_ref.shape[0]
     count0, count1 = RH * RW, TH * TW
-
-    loads = [
-        pltpu.make_async_copy(source, target, arrived.at[index])
-        for index, (source, target) in enumerate(
-            (
-                (stem_hbm, stem_ref),
-                (dw_hbm, dw_ref),
-                (gain_hbm, gain_ref),
-                (win_hbm, win_ref),
-                (wout_hbm, wout_ref),
-                (scale_hbm, scale_ref),
-                (up_hbm, up_ref),
-            )
-        )
-    ]
-    for load in loads:
-        load.start()
-
-    ext[0:RIM, PADC : PADC + TW] = south_ref[...].astype(F32)
+    all0, all1 = spans_of(count0, 2 * RW), spans_of(count1, 2 * TW)
+    middle = slice(MID * RW, (MID + MID_ROWS) * RW)
+    rims = [slice(0, middle.start), slice(middle.stop, count0)]
+    rim0 = [at for at in all0 if at.stop <= middle.start or at.start >= middle.stop]
+
+    def from_middle(at):
+        return middle.start <= at.start < middle.stop
+
+    def pick(mid, ref, at):
+        if from_middle(at):
+            return mid[at.start - middle.start : at.stop - middle.start, :]
+        return ref[at, :]
+
+    ext[0:RIM] = south_ref[...].astype(F32)
     ext[RIM : RIM + TH, PADC : PADC + TW] = tile_ref[...].astype(F32)
-    ext[RIM + TH :, PADC : PADC + TW] = north_ref[...].astype(F32)
-    ext[:, 0:PADC] = west_ref[...].astype(F32)
-    ext[:, PADC + TW :] = east_ref[...].astype(F32)
-
-    weights[...] = jnp.zeros_like(weights)
-    loads[0].wait()
-    weights[0:levels_count, 0:LANES] = stem_ref[...].astype(F32)
-    weights[levels_count : levels_count + 1, LANES:] = jnp.ones((1, LANES), F32)
-    joint = weights[...].astype(BF)
+    ext[RIM : RIM + TH, 0:PADC] = west_ref[0:TH].astype(F32)
+    ext[RIM : RIM + TH, PADC + TW :] = east_ref[0:TH].astype(F32)
+    ext[RIM + TH :] = north_ref[...].astype(F32)
+
+    joint = joint_weights(stem_ref, weights)
 
     for index in range(EH // 4):
         at = slice(index * 4, index * 4 + 4)
@@ -210,17 +316,15 @@
         flat0[index * 4 * EW : (index + 1) * 4 * EW, :] = value
         x0[at] = value.astype(F32).reshape(4, EW, LANES)
 
-    for load in loads[1:]:
-        load.wait()
-    spread_taps(dw_ref, 0, taps0)
-    spread_taps(dw_ref, 0, taps0n, top)
-    spread_taps(dw_ref, 1, taps1)
+    spread_taps(table_ref, 0, taps0)
+    spread_taps(table_ref, 0, taps0n, top)
+    spread_taps(table_ref, 1, taps1)
 
     north_at = 3 + TH
 
     def conv0_block(block, _):
         start = pl.multiple_of(block * 8, 8)
-        for rows in (range(0, 19), range(19, 22)):
+        for rows in (range(0, MID), range(MID + MID_ROWS, north_at), range(north_at, RH)):
             totals = conv_block(
                 x0,
                 (taps0, taps0n),
@@ -235,59 +339,24 @@
 
     lax.fori_loop(0, RW // 8, conv0_block, 0)
 
-    def chunks(count, size, body):
-        def run(carry):
-            for index in range(count // size):
-                carry = body(index, slice(index * size, index * size + size), carry)
-            return carry
-
-        return run
-
-    def norm_rows(conv, xhat, rinv, normed, gain, count, size):
-        def step(index, at, _):
-            values = conv[at, :]
-            average = jnp.mean(values, axis=-1, keepdims=True)
-            centered = values - average
-            inverse = lax.rsqrt(jnp.mean(centered * centered, axis=-1, keepdims=True) + NORM_STABILIZER)
-            scaled = centered * inverse
-            xhat[at, :] = scaled
-            rinv[at, :] = jnp.broadcast_to(inverse, (size, LANES))
-            normed[at, :] = (scaled * gain).astype(BF)
-            return 0
-
-        chunks(count, size, step)(0)
-
-    def gelu_rows(pre, act, slope, count, size):
-        def step(index, at, _):
-            for part in range(size // 16):
-                here = slice(index * size + part * 16, index * size + part * 16 + 16)
-                v = pre[here, :]
-                square = v * v
-                inner = v * (C0 + C1 * square)
-                half = 0.5 * jnp.tanh(inner) + 0.5
-                active = v * half
-                act[here, :] = active.astype(BF)
-                slope[here, :] = half + active * (1.0 - half) * (2.0 * C0 + (6.0 * C1) * square)
-            return 0
-
-        chunks(count, size, step)(0)
-
-    norm_rows(conv0, xhat0, rinv0, normed0, gain_ref[0:1, :], count0, 80)
-    wide[0:count0] = jnp.dot(normed0[...], win_ref[0], preferred_element_type=F32)
-    gelu_rows(wide, act0, slope0, count0, 80)
-    branch0[...] = jnp.dot(act0[...], wout_ref[0], preferred_element_type=F32)
-
-    def next0(index, at, _):
-        rows = pl.ds(index * 2 + 3, 2)
-        mask = m6[rows, RING_COL : RING_COL + RW, :]
-        held = x0[rows, RING_COL : RING_COL + RW, :]
-        branch = branch0[at, :].reshape(2, RW, LANES)
-        value = (mask * (held + scale_ref[0:1, :] * branch)).astype(BF)
-        flat1[at, :] = value.reshape(2 * RW, LANES)
-        x1[pl.ds(index * 2, 2)] = value.astype(F32)
-        return 0
-
-    chunks(count0, 2 * RW, next0)(0)
+    norm_rows(conv0, xhat0, rinv0, normed0, table_ref[49, 0:1, :], rim0)
+    normed0[middle] = mid_normed[...]
+    act0[middle] = mid_act[...]
+    for at in rims:
+        wide[at] = jnp.dot(normed0[at], win_ref[0], preferred_element_type=F32)
+    gelu_rows(wide, act0, slope0, rim0)
+    for at in rims:
+        branch0[at] = jnp.dot(act0[at], wout_ref[0], preferred_element_type=F32)
+
+    flat1[middle] = mid_flat[...]
+    for index, at in enumerate(all0):
+        if not from_middle(at):
+            rows = slice(index * 2 + 3, index * 2 + 5)
+            mask = m6[rows, RING_COL : RING_COL + RW, :]
+            held = x0[rows, RING_COL : RING_COL + RW, :]
+            value = mask * (held + table_ref[50, 0:1, :] * branch0[at, :].reshape(2, RW, LANES))
+            flat1[at, :] = value.reshape(2 * RW, LANES).astype(BF)
+        x1[index * 2 : index * 2 + 2] = flat1[at, :].astype(F32).reshape(2, RW, LANES)
 
     def conv1_block(block, _):
         start = pl.multiple_of(block * 8, 8)
@@ -300,9 +369,9 @@
         return 0
 
     lax.fori_loop(0, TW // 8, conv1_block, 0)
-    norm_rows(conv1, xhat1, rinv1, normed1, gain_ref[1:2, :], count1, 64)
+    norm_rows(conv1, xhat1, rinv1, normed1, table_ref[49, 1:2, :], all1)
     wide[0:count1] = jnp.dot(normed1[...], win_ref[1], preferred_element_type=F32)
-    gelu_rows(wide, act1, slope1, count1, 64)
+    gelu_rows(wide, act1, slope1, all1)
     branch1[...] = jnp.dot(act1[...], wout_ref[1], preferred_element_type=F32)
 
     sums[...] = jnp.zeros_like(sums)
@@ -316,13 +385,13 @@
         mask = m6[pl.ds(index * rows + RIM, rows), PADC : PADC + TW, :]
         held = x1[pl.ds(index * rows + 3, rows), 3 : 3 + TW, :]
         branch = branch1[at, :].reshape(rows, TW, LANES)
-        out_ref[at, :] = (mask * (held + scale_ref[1:2, :] * branch)).astype(BF).reshape(rows * TW, LANES)
+        out_ref[at, :] = (mask * (held + table_ref[50, 1:2, :] * branch)).astype(BF).reshape(rows * TW, LANES)
         masked = mask * (up_ref[at, :].astype(F32) * rescale).reshape(rows, TW, LANES)
         g1[pl.ds(index * rows + 3, rows), 3 : 3 + TW, :] = masked
-        thin[at, :] = (masked * scale_ref[1:2, :]).reshape(rows * TW, LANES).astype(BF)
+        thin[at, :] = (masked * table_ref[50, 1:2, :]).reshape(rows * TW, LANES).astype(BF)
         return total + folded(masked * branch)
 
-    total = chunks(count1, 2 * TW, next1)(jnp.zeros((8, LANES), F32))
+    total = chunks(all1, next1)(jnp.zeros((8, LANES), F32))
     sums[3:4, :] = jnp.sum(total, axis=0, keepdims=True)
 
     def grad_wout(layer, count, act):
@@ -330,16 +399,11 @@
             act[...], thin[0:count]
         ).astype(BF)
 
-    def grad_pre(layer, count, size, slope):
+    def grad_pre(layer, count, slope):
         wide[0:count] = contract_cols(thin[0:count], wout_ref[layer])
 
-        def step(index, at, _):
-            for part in range(size // 16):
-                here = slice(index * size + part * 16, index * size + part * 16 + 16)
-                gpre[here, :] = (wide[here, :] * slope[here, :]).astype(BF)
-            return 0
-
-        chunks(count, size, step)(0)
+        for at in spans_of(count, 16):
+            gpre[at, :] = (wide[at, :] * slope(at)).astype(BF)
 
     def grad_win(layer, count, normed):
         gp = gpre[0:count]
@@ -350,24 +414,24 @@
         wide[0:count, 0:LANES] = contract_cols(gp, win_ref[layer])
 
     def grad_conv(layer, count, size, xhat, rinv, grad):
-        gain = gain_ref[layer : layer + 1, :]
+        gain = table_ref[49, layer : layer + 1, :]
 
         def step(index, at, total):
             gn = wide[at, 0:LANES]
-            scaled = xhat[at, :]
+            scaled = xhat(at)
             gx = gn * gain
             first = jnp.mean(gx, axis=-1, keepdims=True)
             second = jnp.mean(gx * scaled, axis=-1, keepdims=True)
-            grad[at, :] = (rinv[at, :] * (gx - first - scaled * second)).astype(BF)
+            grad[at, :] = (rinv(at) * (gx - first - scaled * second)).astype(BF)
             return total + folded(gn * scaled)
 
-        total = chunks(count, size, step)(jnp.zeros((8, LANES), F32))
+        total = chunks(spans_of(count, size), step)(jnp.zeros((8, LANES), F32))
         sums[layer : layer + 1, :] = jnp.sum(total, axis=0, keepdims=True)
 
     grad_wout(1, count1, act1)
-    grad_pre(1, count1, 64, slope1)
+    grad_pre(1, count1, lambda at: slope1[at, :])
     grad_win(1, count1, normed1)
-    grad_conv(1, count1, 2 * TW, xhat1, rinv1, grad1)
+    grad_conv(1, count1, 2 * TW, lambda at: xhat1[at, :], lambda at: rinv1[at, :], grad1)
     padded(grad1, pad1, TW)
 
     def back1_block(block, _):
@@ -387,53 +451,28 @@
         masked = m6[pl.ds(index * 2 + 3, 2), RING_COL : RING_COL + RW, :] * g1[rows]
         flat = masked.reshape(2 * RW, LANES)
         carry0[at, :] = flat
-        thin[at, :] = (flat * scale_ref[0:1, :]).astype(BF)
-        return total + folded(flat * branch0[at, :])
-
-    total = chunks(count0, 2 * RW, masked0)(jnp.zeros((8, LANES), F32))
+        thin[at, :] = (flat * table_ref[50, 0:1, :]).astype(BF)
+        return total + folded(flat * pick(mid_branch, branch0, at))
+
+    total = chunks(all0, masked0)(jnp.zeros((8, LANES), F32))
     sums[2:3, :] = jnp.sum(total, axis=0, keepdims=True)
     grad_wout(0, count0, act0)
-    grad_pre(0, count0, 80, slope0)
+    grad_pre(0, count0, lambda at: pick(mid_slope, slope0, at))
     grad_win(0, count0, normed0)
-    grad_conv(0, count0, 2 * RW, xhat0, rinv0, grad0)
-
-
-def rest_kernel(
-    top_ref,
-    dw_ref,
-    sums,
-    cells,
-    flat0,
-    flat1,
-    grad0,
-    grad1,
-    carry0,
-    small_ref,
-    small,
-    x0,
-    x1,
-    pad0,
-    pad1,
-    taps0,
-    taps0n,
-    h0,
-    gk0,
-    gk0n,
-    gk1,
-):
-    top = top_ref[0] == 1
-    north_at = 3 + TH
-    levels_count = KERNEL_AT[0] - STEM_AT
-
-    for row in range(0, EH, 4):
-        x0[row : row + 4] = flat0[row * EW : (row + 4) * EW, :].astype(F32).reshape(4, EW, LANES)
+    grad_conv(
+        0,
+        count0,
+        2 * RW,
+        lambda at: pick(mid_xhat, xhat0, at),
+        lambda at: pick(mid_rinv, rinv0, at),
+        grad0,
+    )
+
+
+def taps1_kernel(flat1, grad1, gk1, x1, pad1):
     for row in range(0, RH, 2):
         x1[row : row + 2] = flat1[row * RW : (row + 2) * RW, :].astype(F32).reshape(2, RW, LANES)
-    padded(grad0, pad0, RW)
     padded(grad1, pad1, TW)
-    spread_taps(dw_ref, 0, taps0)
-    spread_taps(dw_ref, 0, taps0n, top)
-
     gk1[...] = jnp.zeros_like(gk1)
 
     def kernel1_block(block, _):
@@ -449,6 +488,36 @@
         return 0
 
     lax.fori_loop(0, TW // 8, kernel1_block, 0)
+
+
+def rest_kernel(
+    top_ref,
+    dw_ref,
+    sums,
+    cells,
+    flat0,
+    grad0,
+    carry0,
+    gk1,
+    small_ref,
+    small,
+    x0,
+    pad0,
+    taps0,
+    taps0n,
+    h0,
+    gk0,
+    gk0n,
+):
+    top = top_ref[0] == 1
+    north_at = 3 + TH
+    levels_count = KERNEL_AT[0] - STEM_AT
+
+    for row in range(0, EH, 4):
+        x0[row : row + 4] = flat0[row * EW : (row + 4) * EW, :].astype(F32).reshape(4, EW, LANES)
+    padded(grad0, pad0, RW)
+    spread_taps(dw_ref, 0, taps0)
+    spread_taps(dw_ref, 0, taps0n, top)
 
     gk0[...] = jnp.zeros_like(gk0)
     gk0n[...] = jnp.zeros_like(gk0n)
@@ -506,26 +575,62 @@
 
 
 def unpack_kernel(
-    order_ref, pieces_ref, mine_ref, other_ref, stem_ref, kernel_ref, gain_ref, win_ref, wout_ref, scale_ref, rows, small
+    order_ref,
+    pieces_ref,
+    mine_ref,
+    other_ref,
+    stem_out,
+    kernel_out,
+    gain_out,
+    win_out,
+    wout_out,
+    scale_out,
+    stem_ref,
+    kernel_ref,
+    gain_ref,
+    win_ref,
+    wout_ref,
+    scale_ref,
+    small,
+    sent,
 ):
     count, size = pieces_ref.shape[0], pieces_ref.shape[1]
-    for index in range(count):
-        rows[index * size : (index + 1) * size, :] = pieces_ref[order_ref[index]].astype(F32)
-    count, size = mine_ref.shape[0], mine_ref.shape[1]
-    for index in range(count):
-        at = order_ref[pieces_ref.shape[0] + index]
+    stores = [
+        pltpu.make_async_copy(source, target, sent.at[index])
+        for index, (source, target) in enumerate(
+            [(win_ref.at[layer], win_out.at[layer]) for layer in range(2)]
+            + [(wout_ref.at[layer], wout_out.at[layer]) for layer in range(2)]
+            + [(stem_ref, stem_out), (kernel_ref, kernel_out), (gain_ref, gain_out), (scale_ref, scale_out)]
+        )
+    ]
+
+    def rows(at, length):
+        return [
+            pieces_ref[order_ref[index]].astype(F32) if count > 1 else pieces_ref[0, index * 128 : index * 128 + 128].astype(F32)
+            for index in range(at // 128, (at + length) // 128)
+        ]
+
+    for layer in range(2):
+        for part, block in enumerate(rows(WIN_ROW + 512 * layer, 512)):
+            win_ref[layer, :, 128 * part : 128 * part + 128] = block
+        stores[layer].start()
+    for layer in range(2):
+        for part, block in enumerate(rows(WOUT_ROW + 512 * layer, 512)):
+            wout_ref[layer, 128 * part : 128 * part + 128, :] = block
+        stores[2 + layer].start()
+    places, size = mine_ref.shape[0], mine_ref.shape[1]
+    for index in range(places):
+        at = order_ref[count + index]
         small[index * size : (index + 1) * size, :] = mine_ref[at].astype(F32) + other_ref[at].astype(F32)
     for layer in range(2):
-        for part in range(4):
-            at = WIN_ROW + 512 * layer + 128 * part
-            win_ref[layer, :, 128 * part : 128 * part + 128] = rows[at : at + 128, :]
-        at = WOUT_ROW + 512 * layer
-        wout_ref[layer] = rows[at : at + 512, :]
-        at = KERNEL_AT[layer]
-        kernel_ref[:, layer, :] = small[at : at + 49, :]
+        kernel_ref[:, layer, :] = small[KERNEL_AT[layer] : KERNEL_AT[layer] + 49, :]
     stem_ref[...] = small[STEM_AT : STEM_AT + stem_ref.shape[0], :]
     gain_ref[...] = small[GAIN_AT : GAIN_AT + 2, :]
     scale_ref[...] = small[SCALE_AT : SCALE_AT + 2, :]
+    for store in stores[4:]:
+        store.start()
+    for store in stores:
+        store.wait()
 
 
 def permuted(value, pairs):
@@ -569,14 +674,14 @@
             axis=0,
         )
 
-    arrived = [crossed(shard(step), 4 * step) for step in (1, 2, 3)]
+    arrived = [crossed(shard(step), 4 * step) for step in STEPS]
     bulk = lax.dynamic_slice_in_dim(total, deep * quarter, quarter, 0)
     rest_sum = lax.dynamic_slice_in_dim(small, deep * part, part, 0).astype(F32)
     for other in arrived:
         bulk = bulk + other[:quarter].astype(F32)
         rest_sum = rest_sum + other[quarter:].astype(F32)
     mine = jnp.concatenate([bulk.astype(BF), rest_sum.astype(BF)], axis=0)
-    pieces = jnp.stack([mine] + [crossed(mine, 4 * step) for step in (1, 2, 3)])
+    pieces = jnp.stack([mine] + [crossed(mine, 4 * step) for step in STEPS][::-1])
     came = crossed(pieces, 2)
     bulk = jnp.concatenate([pieces[:, :quarter], came[:, :quarter]], axis=0)
     small = (pieces[:, quarter:].astype(F32) + came[:, quarter:].astype(F32)).astype(BF)
@@ -597,42 +702,79 @@
     is_top = me // TX == rows - 1
     count = levels.shape[2]
     top = is_top.astype(jnp.int32)[None]
-    taps = dw_kernel.transpose(1, 0, 2)
-    tile, strip, folded = pl.pallas_call(
+    table = jnp.concatenate([dw_kernel.transpose(1, 0, 2), ln_gain[None], layer_scale[None]])
+    tile, to_west, to_east, folded = pl.pallas_call(
         prepare_kernel,
         out_shape=[
             jax.ShapeDtypeStruct((TH, TW, LANES), BF),
-            jax.ShapeDtypeStruct((RIM, TW, LANES), BF),
+            jax.ShapeDtypeStruct((TH + RIM, PADC, LANES), BF),
+            jax.ShapeDtypeStruct((TH + RIM, PADC, LANES), BF),
             jax.ShapeDtypeStruct((RIM, TW, LANES), BF),
         ],
-        in_specs=[smem()] + vmem(2),
-        out_specs=vmem(3),
-        scratch_shapes=[pltpu.VMEM((LANES, count), F32)],
+        in_specs=[pl.BlockSpec(memory_space=pltpu.HBM)] * 2,
+        out_specs=vmem(4),
+        scratch_shapes=[
+            pltpu.VMEM((LANES, count), F32),
+            pltpu.VMEM(levels.shape[1:], BF),
+            pltpu.VMEM(ocean.shape, jnp.int32),
+            pltpu.SemaphoreType.DMA((2,)),
+        ],
         compiler_params=pltpu.CompilerParams(vmem_limit_bytes=4 << 20),
-    )(top, levels[0], ocean)
-    if rows == 2:
-        south = north = permuted(strip, [(i, (i + TX) % size) for i in range(size)])
-        south = jnp.where(is_top, south, jnp.zeros_like(south))
-    else:
-        south = permuted(tile[-RIM:], [(i, i + TX) for i in range(size - TX)])
-        north = permuted(tile[:RIM], [(i + TX, i) for i in range(size - TX)])
-    folded = permuted(folded, [(i, i // TX * TX + TX - 1 - i % TX) for i in range(size - TX, size)])
-    north = jnp.where(is_top, folded, north)
-
-    def columns(at):
-        return jnp.concatenate([south[:, at], tile[:, at], north[:, at]], axis=0)
+    )(levels[0], ocean)
 
     def column_pairs(step):
         return [(i, i // TX * TX + (i % TX + step) % TX) for i in range(size)]
 
-    west = permuted(columns(slice(TW - PADC, TW)), column_pairs(1))
-    east = permuted(columns(slice(0, PADC)), column_pairs(-1))
+    west = permuted(to_east, column_pairs(1))
+    east = permuted(to_west, column_pairs(-1))
+
+    def wide_rows(at):
+        return jnp.concatenate([west[at], tile[at], east[at]], axis=1)
+
+    lower, upper = wide_rows(slice(0, RIM)), wide_rows(slice(TH - RIM, TH))
+    folded = jnp.concatenate([east[TH:], folded, west[TH:]], axis=1)
+    folded = permuted(folded, [(i, i // TX * TX + TX - 1 - i % TX) for i in range(size - TX, size)])
+    if rows == 2:
+        north = permuted(jnp.where(is_top, lower, upper), [(i, (i + TX) % size) for i in range(size)])
+        south = jnp.where(is_top, north, jnp.zeros_like(north))
+    else:
+        south = permuted(upper, [(i, i + TX) for i in range(size - TX)])
+        north = permuted(lower, [(i + TX, i) for i in range(size - TX)])
+    north = jnp.where(is_top, folded, north)
 
     def scratch(*shape, dtype=F32):
         return pltpu.VMEM(shape, dtype)
 
     count0 = RH * RW
     hidden = w_in.shape[2]
+    count_mid = MID_ROWS * RW
+    mid_shapes = [
+        jax.ShapeDtypeStruct((count_mid, LANES), BF),
+        jax.ShapeDtypeStruct((count_mid, LANES), F32),
+        jax.ShapeDtypeStruct((count_mid, LANES), F32),
+        jax.ShapeDtypeStruct((count_mid, LANES), BF),
+        jax.ShapeDtypeStruct((count_mid, hidden), BF),
+        jax.ShapeDtypeStruct((count_mid, hidden), F32),
+        jax.ShapeDtypeStruct((count_mid, LANES), F32),
+    ]
+    middle = pl.pallas_call(
+        middle_kernel,
+        out_shape=mid_shapes,
+        in_specs=vmem(7),
+        out_specs=vmem(7),
+        scratch_shapes=[
+            scratch(TH, EW, LANES),
+            scratch(TH, EW, LANES),
+            scratch(TH, EW, LANES),
+            scratch(LANES, 2 * LANES),
+            scratch(49, 8, LANES),
+            scratch(count_mid, LANES),
+            scratch(count_mid, hidden),
+        ],
+        compiler_params=pltpu.CompilerParams(vmem_limit_bytes=10 << 20),
+        cost_estimate=pl.CostEstimate(flops=4_000_000_000, bytes_accessed=3_000_000, transcendentals=0),
+    )(tile, west, east, table, stem, w_in, w_out)
+
     ring_shapes = [
         jax.ShapeDtypeStruct((8, LANES), F32),
         jax.ShapeDtypeStruct((EH * EW, LANES), BF),
@@ -649,7 +791,7 @@
             jax.ShapeDtypeStruct((BULK, LANES), BF),
         ]
         + ring_shapes,
-        in_specs=[smem()] + vmem(5) + [pl.BlockSpec(memory_space=pltpu.HBM)] * 7,
+        in_specs=[smem()] + vmem(17),
         out_specs=vmem(9),
         scratch_shapes=[
             scratch(EH, EW, LANES),
@@ -679,14 +821,6 @@
             scratch(count0, hidden),
             scratch(count0, LANES, dtype=BF),
             scratch(count0, hidden, dtype=BF),
-            pltpu.VMEM(stem.shape, BF),
-            scratch(dw_kernel.shape[1], dw_kernel.shape[0], LANES),
-            scratch(*ln_gain.shape),
-            scratch(*w_in.shape, dtype=BF),
-            scratch(*w_out.shape, dtype=BF),
-            scratch(*layer_scale.shape),
-            scratch(count, LANES, dtype=BF),
-            pltpu.SemaphoreType.DMA((7,)),
         ],
         compiler_params=pltpu.CompilerParams(vmem_limit_bytes=20 << 20),
     )(
@@ -696,37 +830,44 @@
         east,
         south,
         north,
+        table,
         stem,
-        taps,
-        ln_gain,
         w_in,
         w_out,
-        layer_scale,
         upstream[0],
+        *middle,
     )
+
+    sums, cells, flat0, flat1, grad0, grad1, carry0 = ring
+    grad_taps1 = pl.pallas_call(
+        taps1_kernel,
+        out_shape=jax.ShapeDtypeStruct((49, 8, LANES), F32),
+        in_specs=vmem(2),
+        out_specs=vmem(1)[0],
+        scratch_shapes=[scratch(RH, RW, LANES), scratch(TH, EW, LANES)],
+        compiler_params=pltpu.CompilerParams(vmem_limit_bytes=6 << 20),
+        cost_estimate=pl.CostEstimate(flops=2_000_000_000, bytes_accessed=500_000, transcendentals=0),
+    )(flat1, grad1)
 
     def rest(top):
         return pl.pallas_call(
             rest_kernel,
             out_shape=jax.ShapeDtypeStruct((SMALL, LANES), BF),
-            in_specs=[smem()] + vmem(8),
+            in_specs=[smem()] + vmem(7),
             out_specs=vmem(1)[0],
             scratch_shapes=[
                 scratch(SMALL, LANES),
                 scratch(EH, EW, LANES),
-                scratch(RH, RW, LANES),
                 scratch(RH, EW + 8, LANES),
-                scratch(TH, EW, LANES),
                 scratch(49, 8, LANES),
                 scratch(49, 8, LANES),
                 scratch(EH, EW, LANES),
                 scratch(49, 8, LANES),
                 scratch(49, 8, LANES),
-                scratch(49, 8, LANES),
             ],
             compiler_params=pltpu.CompilerParams(vmem_limit_bytes=10 << 20),
             cost_estimate=pl.CostEstimate(flops=10_000_000_000, bytes_accessed=4_000_000, transcendentals=0),
-        )(top, taps, *ring)
+        )(top, table, sums, cells, flat0, grad0, carry0, grad_taps1)
 
     pieces, mine, other, order = summed_pieces(packed, top, rest)
     shapes = [array.shape for array in (stem, dw_kernel, ln_gain, w_in, w_out, layer_scale)]
@@ -735,8 +876,9 @@
         unpack_kernel,
         out_shape=[jax.ShapeDtypeStruct(shape, F32) for shape in shapes],
         in_specs=[smem()] + vmem(3),
-        out_specs=vmem(6),
-        scratch_shapes=[scratch(BULK, LANES), scratch(SMALL, LANES)],
+        out_specs=[pl.BlockSpec(memory_space=pltpu.HBM)] * 6,
+        scratch_shapes=[scratch(*shape) for shape in shapes]
+        + [scratch(SMALL, LANES), pltpu.SemaphoreType.DMA((8,))],
         compiler_params=pltpu.CompilerParams(vmem_limit_bytes=8 << 20),
     )(order, pieces, mine, other)
     grads = list(grads)

time: 62 us -> 58.5 us (0.944)
  starting transfers between devices: 21 us -> 17.1 us
  waiting for transfers between devices: 19.3 us -> 18.5 us
    ppermute x14, starting transfers between devices: 21 us -> 17.1 us  [permuted(): return lax.ppermute(value, 'gy', pairs)]
    pallas_call x0 -> x2, Pallas kernels: none -> 3.07 us  [the longest x1 2.09 us: shards(): pl.pallas_call(middle_kernel, out_shape=mid_shapes, in_specs=vmem(7), out...]
    pallas_call x1, Pallas kernels: 9.97 us -> 8.44 us  [shards(): pl.pallas_call(functools.partial(main_kernel, 1.0 / math.sqrt(size * coun...]
    pallas_call x1, Pallas kernels: 5.77 us -> 4.73 us  [rest(): pl.pallas_call(rest_kernel, out_shape=jax.ShapeDtypeStruct((SMALL, LANES)...]
    ppermute x14, waiting for transfers between devices: 19.3 us -> 18.5 us  [permuted(): return lax.ppermute(value, 'gy', pairs)]
  transfers between devices with their start and end apart: 14 -> 14, of which waited for: 10 -> 12; matrix products, arithmetic and copies ran while one was open for 0% -> 0% of each run, Pallas kernels for 9% -> 13%
where the time goes in v4:
time: 58.5 us; the launch traced here: 58.3 us
  waiting for transfers between devices  18.5 us (32%)
  Pallas kernels  18.4 us (31%)
  starting transfers between devices  17.1 us (29%)
  local copies, waits for them, and re-layouts  2.82 us (5%)
  between operations  1.01 us (2%)
    ppermute x14, waiting for transfers between devices, permuted(): return lax.ppermute(value, 'gy', pairs)  18.5 us
    ppermute x14, starting transfers between devices, permuted(): return lax.ppermute(value, 'gy', pairs)  17.1 us
    pallas_call x1, Pallas kernels, shards(): pl.pallas_call(functools.partial(main_kernel, 1.0 / math.sqrt(size * coun...  8.44 us
    pallas_call x1, Pallas kernels, rest(): pl.pallas_call(rest_kernel, out_shape=jax.ShapeDtypeStruct((SMALL, LANES)...  4.73 us
    unnamed x18, local copies, waits for them, and re-layouts  2.72 us
    pallas_call x1, Pallas kernels, shards(): pl.pallas_call(middle_kernel, out_shape=mid_shapes, in_specs=vmem(7), out...  2.09 us
    pallas_call x1, Pallas kernels, shards(): pl.pallas_call(unpack_kernel, out_shape=[jax.ShapeDtypeStruct(shape, F32)...  1.63 us
  transfers between devices with their start and end apart: 14, of which 12 were waited for; matrix products, arithmetic and copies ran while one was open for 0% of the time, Pallas kernels for 13%

profile of v4, /device:TPU:0, one launch (start us, length us, event | category | flops | bytes accessed | tf_op | source)
XLA Modules:
  0.0 58.3 jit_solution(542481849284574693)
XLA Ops:
  0.6 0.0 copy-start.3
  0.6 0.9 %copy-done.3 = bf16[1,75,512]{2,1,0:T(8,128)(2,1)S(1)} copy-done((bf16[1,75,512]{2,1,0:T(8,128)(2,1)S(1)}, bf16[1,75,512]{2,1,0:T(8,128)(2,1)}, u32[]{:S(2)}) %copy-start.3) | copy-done | bytes 76824
  1.5 0.0 copy-start.5
  1.5 0.7 %copy-done.5 = s32[1,512]{1,0:T(1,128)S(1)} copy-done((s32[1,512]{1,0:T(1,128)S(1)}, s32[1,512]{1,0:T(1,128)}, u32[]{:S(2)}) %copy-start.5) | copy-done | bytes 2072
  2.2 0.5 shard_map.144
  2.7 3.4 %collective-permute-start.1 = (bf16[22,8,128]{2,1,0:T(8,128)(2,1)S(1)}, bf16[22,8,128]{2,1,0:T(8,128)(2,1)S(1)}, u32[]{:S(2)}, u32[]{:S(2)}) collective-permute-start(bf16[22,8,128]{2,1,0:T(8,128)(2,1)S(1)} %get-tuple-element.37), channel_id=1, source_target_pairs={{0,7},{1,0},{2,1},{3,2},{4,3},{5,4},{6,5},{7,6},{8,15},{9,8},{10,9... | collective-permute-start | bytes 135176 | tf_op jit(solution)/shard_map/ppermute | solution.py:637
  6.2 0.0 collective-permute-start
  6.2 0.0 copy-start.6
  6.2 0.0 copy-start.8
  6.2 0.0 copy-start.7
  6.2 0.8 %copy-done.6 = f32[2,49,128]{2,0,1:T(2,128)S(1)} copy-done((f32[2,49,128]{2,0,1:T(2,128)S(1)}, f32[2,49,128]{2,0,1:T(2,128)}, u32[]{:S(2)}) %copy-start.6) | copy-done | bytes 50200
  7.0 0.0 copy-done.8
  7.0 0.0 copy-done.7
  7.0 0.0 copy-start.4
  7.0 0.0 copy-start
  7.0 0.0 copy-start.1
  7.1 0.8 %collective-permute-done.1.east_ref = bf16[22,8,128]{2,1,0:T(8,128)(2,1)S(1)} collective-permute-done((bf16[22,8,128]{2,1,0:T(8,128)(2,1)S(1)}, bf16[22,8,128]{2,1,0:T(8,128)(2,1)S(1)}, u32[]{:S(2)}, u32[]{:S(2)}) %collective-permute-start.1) | collective-permute-done | bytes 45088 | tf_op jit(solution)/shard_map/ppermute | solution.py:637
  7.9 2.7 %collective-permute-done.west_ref = bf16[22,8,128]{2,1,0:T(8,128)(2,1)S(1)} collective-permute-done((bf16[22,8,128]{2,1,0:T(8,128)(2,1)S(1)}, bf16[22,8,128]{2,1,0:T(8,128)(2,1)S(1)}, u32[]{:S(2)}, u32[]{:S(2)}) %collective-permute-start) | collective-permute-done | bytes 45088 | tf_op jit(solution)/shard_map/ppermute | solution.py:637
  10.6 2.7 %collective-permute-start.2 = (bf16[6,48,128]{2,1,0:T(8,128)(2,1)S(1)}, bf16[6,48,128]{2,1,0:T(8,128)(2,1)S(1)}, u32[]{:S(2)}, u32[]{:S(2)}) collective-permute-start(bf16[6,48,128]{2,1,0:T(8,128)(2,1)S(1)} %maximum_select_fusion), channel_id=1, source_target_pairs={{0,8},{1,9},{2,10},{3,11},{4,12},{5,13},{6,14},{7,15},{8,0},{9,1},... | collective-permute-start | bytes 221192 | tf_op jit(solution)/shard_map/ppermute | solution.py:637
  13.2 0.7 %collective-permute-start.3 = (bf16[6,48,128]{2,1,0:T(8,128)(2,1)S(1)}, bf16[6,48,128]{2,1,0:T(8,128)(2,1)S(1)}, u32[]{:S(2)}, u32[]{:S(2)}) collective-permute-start(bf16[6,48,128]{2,1,0:T(8,128)(2,1)S(1)} %pad_maximum_fusion.4), channel_id=1, source_target_pairs={{8,15},{9,14},{10,13},{11,12},{12,11},{13,10},{14,9},{15,8},{24,31... | collective-permute-start | bytes 221192 | tf_op jit(solution)/shard_map/ppermute | solution.py:637
  13.9 0.0 copy-done.4
  13.9 0.0 copy-done
  13.9 0.0 copy-done.1
  13.9 2.1 %shard_map.145 = (bf16[400,128]{1,0:T(8,128)(2,1)S(1)}, f32[400,128]{1,0:T(8,128)S(1)}, f32[400,128]{1,0:T(8,128)S(1)}, bf16[400,128]{1,0:T(8,128)(2,1)S(1)}, bf...) custom-call(bf16[16,32,128]{2,1,0:T(8,128)(2,1)S(1)} %get-tuple-element.35.tile_ref, ...), custom_call_target="tpu_custom_call" | custom-call | flops 4000000000 | bytes 3000000 | tf_op jit(solution)/shard_map/pallas_call | solution.py:760
  16.0 0.0 copy-start.2
  16.0 0.5 collective-permute-done.2
  16.6 0.0 collective-permute-done.3
  16.6 0.4 copy-done.2
  16.9 8.4 %shard_map.146 = (bf16[512,128]{1,0:T(8,128)(2,1)}, bf16[2048,128]{1,0:T(8,128)(2,1)S(1)}, f32[8,128]{1,0:T(8,128)S(1)}, bf16[1344,128]{1,0:T(8,128)(2,1)S(1)}, ...) custom-call(s32[1]{0:T(128)} %bitcast.top_ref, ...), custom_call_target="tpu_custom_call" | custom-call | tf_op jit(solution)/shard_map/pallas_call | solution.py:787
  25.4 0.1 collective-permute-start.4
  25.5 1.0 %shard_map.147.gk1 = f32[49,8,128]{2,1,0:T(8,128)S(1)} custom-call(bf16[880,128]{1,0:T(8,128)(2,1)S(1)} %get-tuple-element.55.flat1, bf16[512,128]{1,0:T(8,128)(2,1)S(1)} %get-tuple-element.56.grad1), custom_call_target="tpu_custom_call" | custom-call | flops 2000000000 | bytes 500000 | tf_op jit(solution)/shard_map/pallas_call | solution.py:842
  26.5 0.5 collective-permute-done.4
  27.0 0.1 convert_add_fusion
  27.2 0.1 collective-permute-start.5
  27.2 4.7 %shard_map.148 = bf16[192,128]{1,0:T(8,128)(2,1)S(1)} custom-call(s32[1]{0:T(128)} %bitcast.top_ref, f32[51,2,128]{2,1,0:T(2,128)S(1)} %pad_maximum_fusion.5.table_ref.dw_ref, f32[8,128]{1,0:T(8,128)S(1)} %get-tuple-element.50.sums, bf16[1344,128]{1,0:T(8,128)(2,1)S(1)} %get-tuple-element.51.cells, bf16[1344,128]{1,0:T(8,128)(2,1)S(1)} %get-tuple-element.52.flat0, ...), custom_call_target="tpu_custom_call" | custom-call | flops 10000000000 | bytes 4000000 | tf_op jit(solution)/shard_map/pallas_call | solution.py:853
  32.0 0.8 %collective-permute-done.5 = bf16[512,128]{1,0:T(8,128)(2,1)S(1)} collective-permute-done((bf16[512,128]{1,0:T(8,128)(2,1)S(1)}, bf16[512,128]{1,0:T(8,128)(2,1)S(1)}, u32[]{:S(2)}, u32[]{:S(2)}) %collective-permute-start.5) | collective-permute-done | bytes 131104 | tf_op jit(solution)/shard_map/ppermute | solution.py:637
  32.9 3.7 %collective-permute-start.6 = (bf16[176,128]{1,0:T(8,128)(2,1)S(1)}, bf16[176,128]{1,0:T(8,128)(2,1)S(1)}, u32[]{:S(2)}, u32[]{:S(2)}) collective-permute-start(bf16[176,128]{1,0:T(8,128)(2,1)S(1)} %pad_maximum_fusion.6), channel_id=1, source_target_pairs={{0,12},{1,13},{2,14},{3,15},{4,8},{5,9},{6,10},{7,11},{8,4},{9,5},... | collective-permute-start | bytes 135176 | tf_op jit(solution)/shard_map/ppermute | solution.py:637
  36.6 0.0 collective-permute-start.7
  36.6 0.8 %collective-permute-start.8 = (bf16[176,128]{1,0:T(8,128)(2,1)S(1)}, bf16[176,128]{1,0:T(8,128)(2,1)S(1)}, u32[]{:S(2)}, u32[]{:S(2)}) collective-permute-start(bf16[176,128]{1,0:T(8,128)(2,1)S(1)} %pad_maximum_fusion.8), channel_id=1, source_target_pairs={{0,4},{1,5},{2,6},{3,7},{4,0},{5,1},{6,2},{7,3},{8,12},{9,13},{10,... | collective-permute-start | bytes 135176 | tf_op jit(solution)/shard_map/ppermute | solution.py:637
  37.3 1.5 %collective-permute-done.6 = bf16[176,128]{1,0:T(8,128)(2,1)S(1)} collective-permute-done((bf16[176,128]{1,0:T(8,128)(2,1)S(1)}, bf16[176,128]{1,0:T(8,128)(2,1)S(1)}, u32[]{:S(2)}, u32[]{:S(2)}) %collective-permute-start.6) | collective-permute-done | bytes 45088 | tf_op jit(solution)/shard_map/ppermute | solution.py:637
  38.8 2.9 %collective-permute-done.7 = bf16[176,128]{1,0:T(8,128)(2,1)S(1)} collective-permute-done((bf16[176,128]{1,0:T(8,128)(2,1)S(1)}, bf16[176,128]{1,0:T(8,128)(2,1)S(1)}, u32[]{:S(2)}, u32[]{:S(2)}) %collective-permute-start.7) | collective-permute-done | bytes 45088 | tf_op jit(solution)/shard_map/ppermute | solution.py:637
  41.7 0.0 collective-permute-done.8
  41.7 1.9 %collective-permute-start.11 = (bf16[176,128]{1,0:T(8,128)(2,1)S(1)}, bf16[176,128]{1,0:T(8,128)(2,1)S(1)}, u32[]{:S(2)}, u32[]{:S(2)}) collective-permute-start(bf16[176,128]{1,0:T(8,128)(2,1)S(1)} %get-tuple-element.74), channel_id=1, source_target_pairs={{0,12},{1,13},{2,14},{3,15},{4,8},{5,9},{6,10},{7,11},{8,4},{9,5},... | collective-permute-start | bytes 135176 | tf_op jit(solution)/shard_map/ppermute | solution.py:637
  43.7 0.6 collective-permute-start.9
  44.2 2.0 %collective-permute-start.10 = (bf16[176,128]{1,0:T(8,128)(2,1)S(1)}, bf16[176,128]{1,0:T(8,128)(2,1)S(1)}, u32[]{:S(2)}, u32[]{:S(2)}) collective-permute-start(bf16[176,128]{1,0:T(8,128)(2,1)S(1)} %get-tuple-element.74), channel_id=1, source_target_pairs={{0,8},{1,9},{2,10},{3,11},{4,12},{5,13},{6,14},{7,15},{8,0},{9,1},... | collective-permute-start | bytes 135176 | tf_op jit(solution)/shard_map/ppermute | solution.py:637
  46.2 1.5 %collective-permute-done.11 = bf16[176,128]{1,0:T(8,128)(2,1)S(1)} collective-permute-done((bf16[176,128]{1,0:T(8,128)(2,1)S(1)}, bf16[176,128]{1,0:T(8,128)(2,1)S(1)}, u32[]{:S(2)}, u32[]{:S(2)}) %collective-permute-start.11) | collective-permute-done | bytes 45088 | tf_op jit(solution)/shard_map/ppermute | solution.py:637
  47.7 0.4 collective-permute-done.9
  48.1 1.0 %collective-permute-done.10 = bf16[176,128]{1,0:T(8,128)(2,1)S(1)} collective-permute-done((bf16[176,128]{1,0:T(8,128)(2,1)S(1)}, bf16[176,128]{1,0:T(8,128)(2,1)S(1)}, u32[]{:S(2)}, u32[]{:S(2)}) %collective-permute-start.10) | collective-permute-done | bytes 45088 | tf_op jit(solution)/shard_map/ppermute | solution.py:637
  49.2 1.2 %collective-permute-start.12 = (bf16[4,176,128]{2,1,0:T(8,128)(2,1)S(1)}, bf16[4,176,128]{2,1,0:T(8,128)(2,1)S(1)}, u32[]{:S(2)}, u32[]{:S(2)}) collective-permute-start(bf16[4,176,128]{2,1,0:T(8,128)(2,1)S(1)} %pad_maximum_fusion.3), channel_id=1, source_target_pairs={{0,2},{1,3},{2,0},{3,1},{4,6},{5,7},{6,4},{7,5},{8,10},{9,11},{10,... | collective-permute-start | bytes 540680 | tf_op jit(solution)/shard_map/ppermute | solution.py:637
  50.4 4.3 %collective-permute-done.12 = bf16[4,176,128]{2,1,0:T(8,128)(2,1)S(1)} collective-permute-done((bf16[4,176,128]{2,1,0:T(8,128)(2,1)S(1)}, bf16[4,176,128]{2,1,0:T(8,128)(2,1)S(1)}, u32[]{:S(2)}, u32[]{:S(2)}) %collective-permute-start.12) | collective-permute-done | bytes 180256 | tf_op jit(solution)/shard_map/ppermute | solution.py:637
  54.9 0.1 collective-permute-start.13
  55.0 1.6 %collective-permute-done.13 = bf16[1216,128]{1,0:T(8,128)(2,1)S(1)} collective-permute-done((bf16[1216,128]{1,0:T(8,128)(2,1)S(1)}, bf16[1216,128]{1,0:T(8,128)(2,1)S(1)}, u32[]{:S(2)}, u32[]{:S(2)}) %collective-permute-start.13) | collective-permute-done | bytes 311328 | tf_op jit(solution)/shard_map/ppermute | solution.py:637
  56.6 0.1 pad_maximum_fusion.pieces_ref
  56.6 1.6 %shard_map.149 = (f32[75,128]{1,0:T(8,128)}, f32[49,2,128]{2,1,0:T(2,128)}, f32[2,128]{1,0:T(2,128)}, f32[2,128,512]{2,1,0:T(8,128)}, f32[2,512,128]{2,1,0:T(8,128)}, /*index=5*/f32[2,128]{1,0:T(2,128)}) custom-call(s32[20]{0:T(128)S(1)} %fusion.order_ref, bf16[16,128,128]{2,1,0:T(8,128)(2,1)S(1)} %pad_maximum_fusion.pieces_ref, ...), custom_call_target="tpu_custom_call" | custom-call | tf_op jit(solution)/shard_map/pallas_call | solution.py:875
  (27 shorter events, 0.4 us)
Async XLA Ops:
  0.6 0.9 %copy-start.3 = (bf16[1,75,512]{2,1,0:T(8,128)(2,1)S(1)}, bf16[1,75,512]{2,1,0:T(8,128)(2,1)}, u32[]{:S(2)}) copy-start(bf16[1,75,512]{2,1,0:T(8,128)(2,1)} %param.9) | copy-start | bytes 230404
  1.5 0.7 %copy-start.5 = (s32[1,512]{1,0:T(1,128)S(1)}, s32[1,512]{1,0:T(1,128)}, u32[]{:S(2)}) copy-start(s32[1,512]{1,0:T(1,128)} %ocean_hbm.1) | copy-start | bytes 6148
  2.7 5.2 %collective-permute-start.1 = (bf16[22,8,128]{2,1,0:T(8,128)(2,1)S(1)}, bf16[22,8,128]{2,1,0:T(8,128)(2,1)S(1)}, u32[]{:S(2)}, u32[]{:S(2)}) collective-permute-start(bf16[22,8,128]{2,1,0:T(8,128)(2,1)S(1)} %get-tuple-element.37), channel_id=1, source_target_pairs={{0,7},{1,0},{2,1},{3,2},{4,3},{5,4},{6,5},{7,6},{8,15},{9,8},{10,9... | collective-permute-start | bytes 135176 | tf_op jit(solution)/shard_map/ppermute | solution.py:637
  6.2 4.4 %collective-permute-start = (bf16[22,8,128]{2,1,0:T(8,128)(2,1)S(1)}, bf16[22,8,128]{2,1,0:T(8,128)(2,1)S(1)}, u32[]{:S(2)}, u32[]{:S(2)}) collective-permute-start(bf16[22,8,128]{2,1,0:T(8,128)(2,1)S(1)} %get-tuple-element.36), channel_id=1, source_target_pairs={{0,1},{1,2},{2,3},{3,4},{4,5},{5,6},{6,7},{7,0},{8,9},{9,10},{10,1... | collective-permute-start | bytes 135176 | tf_op jit(solution)/shard_map/ppermute | solution.py:637
  6.2 0.8 %copy-start.6 = (f32[2,49,128]{2,0,1:T(2,128)S(1)}, f32[2,49,128]{2,0,1:T(2,128)}, u32[]{:S(2)}) copy-start(f32[2,49,128]{2,0,1:T(2,128)} %param.12) | copy-start | bytes 150532
  6.2 0.8 %copy-start.8 = (f32[2,128]{1,0:T(2,128)S(1)}, f32[2,128]{1,0:T(2,128)}, u32[]{:S(2)}) copy-start(f32[2,128]{1,0:T(2,128)} %param.13) | copy-start | bytes 3076
  6.2 0.8 %copy-start.7 = (f32[2,128]{1,0:T(2,128)S(1)}, f32[2,128]{1,0:T(2,128)}, u32[]{:S(2)}) copy-start(f32[2,128]{1,0:T(2,128)} %param.16) | copy-start | bytes 3076
  7.0 6.9 %copy-start.4 = (bf16[75,128]{1,0:T(8,128)(2,1)S(1)}, bf16[75,128]{1,0:T(8,128)(2,1)}, u32[]{:S(2)}) copy-start(bf16[75,128]{1,0:T(8,128)(2,1)} %stem_ref.3) | copy-start | bytes 57604
  7.0 6.9 %copy-start = (bf16[2,128,512]{2,1,0:T(8,128)(2,1)S(1)}, bf16[2,128,512]{2,1,0:T(8,128)(2,1)}, u32[]{:S(2)}) copy-start(bf16[2,128,512]{2,1,0:T(8,128)(2,1)} %win_ref.3) | copy-start | bytes 786436
  7.0 6.9 %copy-start.1 = (bf16[2,512,128]{2,1,0:T(8,128)(2,1)S(1)}, bf16[2,512,128]{2,1,0:T(8,128)(2,1)}, u32[]{:S(2)}) copy-start(bf16[2,512,128]{2,1,0:T(8,128)(2,1)} %wout_ref.3) | copy-start | bytes 786436
  10.6 6.0 %collective-permute-start.2 = (bf16[6,48,128]{2,1,0:T(8,128)(2,1)S(1)}, bf16[6,48,128]{2,1,0:T(8,128)(2,1)S(1)}, u32[]{:S(2)}, u32[]{:S(2)}) collective-permute-start(bf16[6,48,128]{2,1,0:T(8,128)(2,1)S(1)} %maximum_select_fusion), channel_id=1, source_target_pairs={{0,8},{1,9},{2,10},{3,11},{4,12},{5,13},{6,14},{7,15},{8,0},{9,1},... | collective-permute-start | bytes 221192 | tf_op jit(solution)/shard_map/ppermute | solution.py:637
  13.2 3.3 %collective-permute-start.3 = (bf16[6,48,128]{2,1,0:T(8,128)(2,1)S(1)}, bf16[6,48,128]{2,1,0:T(8,128)(2,1)S(1)}, u32[]{:S(2)}, u32[]{:S(2)}) collective-permute-start(bf16[6,48,128]{2,1,0:T(8,128)(2,1)S(1)} %pad_maximum_fusion.4), channel_id=1, source_target_pairs={{8,15},{9,14},{10,13},{11,12},{12,11},{13,10},{14,9},{15,8},{24,31... | collective-permute-start | bytes 221192 | tf_op jit(solution)/shard_map/ppermute | solution.py:637
  16.0 0.9 %copy-start.2 = (bf16[1,512,128]{2,1,0:T(8,128)(2,1)S(1)}, bf16[1,512,128]{2,1,0:T(8,128)(2,1)}, u32[]{:S(2)}) copy-start(bf16[1,512,128]{2,1,0:T(8,128)(2,1)} %param.17) | copy-start | bytes 393220
  25.4 1.6 %collective-permute-start.4 = (bf16[1024,128]{1,0:T(8,128)(2,1)S(1)}, bf16[1024,128]{1,0:T(8,128)(2,1)S(1)}, u32[]{:S(2)}, u32[]{:S(2)}) collective-permute-start(bf16[1024,128]{1,0:T(8,128)(2,1)S(1)} %broadcast_select_fusion), channel_id=1, source_target_pairs={{0,1},{1,0},{2,3},{3,2},{4,5},{5,4},{6,7},{7,6},{8,9},{9,8},{10,11... | collective-permute-start | bytes 786440 | tf_op jit(solution)/shard_map/ppermute | solution.py:637
  27.2 5.6 %collective-permute-start.5 = (bf16[512,128]{1,0:T(8,128)(2,1)S(1)}, bf16[512,128]{1,0:T(8,128)(2,1)S(1)}, u32[]{:S(2)}, u32[]{:S(2)}) collective-permute-start(bf16[512,128]{1,0:T(8,128)(2,1)S(1)} %select_convert_fusion), channel_id=1, source_target_pairs={{0,2},{1,3},{2,0},{3,1},{4,6},{5,7},{6,4},{7,5},{8,10},{9,11},{10,... | collective-permute-start | bytes 393224 | tf_op jit(solution)/shard_map/ppermute | solution.py:637
  32.9 5.9 %collective-permute-start.6 = (bf16[176,128]{1,0:T(8,128)(2,1)S(1)}, bf16[176,128]{1,0:T(8,128)(2,1)S(1)}, u32[]{:S(2)}, u32[]{:S(2)}) collective-permute-start(bf16[176,128]{1,0:T(8,128)(2,1)S(1)} %pad_maximum_fusion.6), channel_id=1, source_target_pairs={{0,12},{1,13},{2,14},{3,15},{4,8},{5,9},{6,10},{7,11},{8,4},{9,5},... | collective-permute-start | bytes 135176 | tf_op jit(solution)/shard_map/ppermute | solution.py:637
  36.6 5.1 %collective-permute-start.7 = (bf16[176,128]{1,0:T(8,128)(2,1)S(1)}, bf16[176,128]{1,0:T(8,128)(2,1)S(1)}, u32[]{:S(2)}, u32[]{:S(2)}) collective-permute-start(bf16[176,128]{1,0:T(8,128)(2,1)S(1)} %pad_maximum_fusion.7), channel_id=1, source_target_pairs={{0,8},{1,9},{2,10},{3,11},{4,12},{5,13},{6,14},{7,15},{8,0},{9,1},... | collective-permute-start | bytes 135176 | tf_op jit(solution)/shard_map/ppermute | solution.py:637
  36.6 5.1 %collective-permute-start.8 = (bf16[176,128]{1,0:T(8,128)(2,1)S(1)}, bf16[176,128]{1,0:T(8,128)(2,1)S(1)}, u32[]{:S(2)}, u32[]{:S(2)}) collective-permute-start(bf16[176,128]{1,0:T(8,128)(2,1)S(1)} %pad_maximum_fusion.8), channel_id=1, source_target_pairs={{0,4},{1,5},{2,6},{3,7},{4,0},{5,1},{6,2},{7,3},{8,12},{9,13},{10,... | collective-permute-start | bytes 135176 | tf_op jit(solution)/shard_map/ppermute | solution.py:637
  41.7 6.0 %collective-permute-start.11 = (bf16[176,128]{1,0:T(8,128)(2,1)S(1)}, bf16[176,128]{1,0:T(8,128)(2,1)S(1)}, u32[]{:S(2)}, u32[]{:S(2)}) collective-permute-start(bf16[176,128]{1,0:T(8,128)(2,1)S(1)} %get-tuple-element.74), channel_id=1, source_target_pairs={{0,12},{1,13},{2,14},{3,15},{4,8},{5,9},{6,10},{7,11},{8,4},{9,5},... | collective-permute-start | bytes 135176 | tf_op jit(solution)/shard_map/ppermute | solution.py:637
  43.7 4.5 %collective-permute-start.9 = (bf16[176,128]{1,0:T(8,128)(2,1)S(1)}, bf16[176,128]{1,0:T(8,128)(2,1)S(1)}, u32[]{:S(2)}, u32[]{:S(2)}) collective-permute-start(bf16[176,128]{1,0:T(8,128)(2,1)S(1)} %get-tuple-element.74), channel_id=1, source_target_pairs={{0,4},{1,5},{2,6},{3,7},{4,0},{5,1},{6,2},{7,3},{8,12},{9,13},{10,... | collective-permute-start | bytes 135176 | tf_op jit(solution)/shard_map/ppermute | solution.py:637
  44.2 4.9 %collective-permute-start.10 = (bf16[176,128]{1,0:T(8,128)(2,1)S(1)}, bf16[176,128]{1,0:T(8,128)(2,1)S(1)}, u32[]{:S(2)}, u32[]{:S(2)}) collective-permute-start(bf16[176,128]{1,0:T(8,128)(2,1)S(1)} %get-tuple-element.74), channel_id=1, source_target_pairs={{0,8},{1,9},{2,10},{3,11},{4,12},{5,13},{6,14},{7,15},{8,0},{9,1},... | collective-permute-start | bytes 135176 | tf_op jit(solution)/shard_map/ppermute | solution.py:637
  49.2 5.6 %collective-permute-start.12 = (bf16[4,176,128]{2,1,0:T(8,128)(2,1)S(1)}, bf16[4,176,128]{2,1,0:T(8,128)(2,1)S(1)}, u32[]{:S(2)}, u32[]{:S(2)}) collective-permute-start(bf16[4,176,128]{2,1,0:T(8,128)(2,1)S(1)} %pad_maximum_fusion.3), channel_id=1, source_target_pairs={{0,2},{1,3},{2,0},{3,1},{4,6},{5,7},{6,4},{7,5},{8,10},{9,11},{10,... | collective-permute-start | bytes 540680 | tf_op jit(solution)/shard_map/ppermute | solution.py:637
  54.9 1.7 %collective-permute-start.13 = (bf16[1216,128]{1,0:T(8,128)(2,1)S(1)}, bf16[1216,128]{1,0:T(8,128)(2,1)S(1)}, u32[]{:S(2)}, u32[]{:S(2)}) collective-permute-start(bf16[1216,128]{1,0:T(8,128)(2,1)S(1)} %pad_maximum_fusion.1), channel_id=1, source_target_pairs={{0,1},{1,0},{2,3},{3,2},{4,5},{5,4},{6,7},{7,6},{8,9},{9,8},{10,11... | collective-permute-start | bytes 933896 | tf_op jit(solution)/shard_map/ppermute | solution.py:637

commit v5 on v4

--- a/solution.py
+++ b/solution.py
@@ -50,19 +50,11 @@
     return lax.dot_general(left, right, (((1,), (1,)), ((), ())), preferred_element_type=F32)
 
 
-def prepare_kernel(levels_hbm, ocean_hbm, tile_ref, west_ref, east_ref, fold_ref, stage, levels_ref, ocean_ref, arrived):
+def prepare_kernel(levels_ref, ocean_ref, tile_ref, west_ref, east_ref, fold_ref, stage):
     count, cells = levels_ref.shape
-    loads = [
-        pltpu.make_async_copy(levels_hbm, levels_ref, arrived.at[0]),
-        pltpu.make_async_copy(ocean_hbm, ocean_ref, arrived.at[1]),
-    ]
-    for load in loads:
-        load.start()
     stage[...] = jnp.zeros_like(stage)
-    for load in loads:
-        load.wait()
     stage[0:count, :] = levels_ref[...].astype(F32)
-    stage[count : count + 1, :] = ocean_ref[...].astype(F32)
+    stage[count : count + 1, :] = ocean_ref[...]
     rows = lax.broadcasted_iota(jnp.int32, (LANES, LANES), 0)
     cols = lax.broadcasted_iota(jnp.int32, (LANES, LANES), 1)
     eye = (rows == cols).astype(BF)
@@ -79,6 +71,48 @@
     west_ref[TH:] = fold[:, TW - PADC :].astype(BF)
     east_ref[0:TH] = tile[:, TW - PADC :].astype(BF)
     east_ref[TH:] = fold[:, 0:PADC].astype(BF)
+
+
+def pack_kernel(used, tile_ref, west_ref, east_ref, fold_ref, lower_ref, upper_ref, folded_ref):
+    spare, halo = LANES - used, RIM * PADC
+    over = used - spare
+
+    def kept(value, low, high):
+        lane = lax.broadcasted_iota(jnp.int32, value.shape, 1)
+        return jnp.where((lane >= low) & (lane < high), value, 0.0)
+
+    def store(ref, own, first, last):
+        own = own.astype(F32).reshape(RIM * TW, LANES)
+        first, last = [value.astype(F32).reshape(halo, LANES) for value in (first, last)]
+        extra = [
+            kept(pltpu.roll(first, used, 1), used, LANES),
+            kept(pltpu.roll(last, used, 1), used, LANES),
+            kept(pltpu.roll(first, used - spare, 1), used, used + over)
+            + kept(pltpu.roll(last, used - spare + over, 1), used + over, used + 2 * over),
+        ]
+        for index, value in enumerate(extra):
+            at = slice(index * halo, (index + 1) * halo)
+            ref[at] = (own[at] + value).astype(BF)
+        ref[3 * halo :] = own[3 * halo :].astype(BF)
+
+    for ref, at in ((lower_ref, slice(0, RIM)), (upper_ref, slice(TH - RIM, TH))):
+        store(ref, tile_ref[at], west_ref[at], east_ref[at])
+    store(folded_ref, fold_ref[...], east_ref[TH:], west_ref[TH:])
+
+
+def unpack_rows(used, packed_ref, ext, at):
+    spare, halo = LANES - used, RIM * PADC
+    over = used - spare
+    rows = packed_ref[...].astype(F32)
+    lane = lax.broadcasted_iota(jnp.int32, (halo, LANES), 1)
+    own = jnp.where(lax.broadcasted_iota(jnp.int32, rows.shape, 1) < used, rows, 0.0)
+    ext[at : at + RIM, PADC : PADC + TW] = own.reshape(RIM, TW, LANES)
+    tail = rows[2 * halo : 3 * halo]
+    for index, (start, shift) in enumerate(((0, used - spare), (PADC + TW, used - spare + over))):
+        front = pltpu.roll(rows[index * halo : (index + 1) * halo], LANES - used, 1)
+        back = pltpu.roll(tail, LANES - shift, 1)
+        value = jnp.where(lane < spare, front, jnp.where(lane < used, back, 0.0))
+        ext[at : at + RIM, start : start + PADC] = value.reshape(RIM, PADC, LANES)
 
 
 def load_column(ref, row, start):
@@ -297,11 +331,11 @@
             return mid[at.start - middle.start : at.stop - middle.start, :]
         return ref[at, :]
 
-    ext[0:RIM] = south_ref[...].astype(F32)
+    unpack_rows(stem_ref.shape[0] + 1, south_ref, ext, 0)
+    unpack_rows(stem_ref.shape[0] + 1, north_ref, ext, RIM + TH)
     ext[RIM : RIM + TH, PADC : PADC + TW] = tile_ref[...].astype(F32)
     ext[RIM : RIM + TH, 0:PADC] = west_ref[0:TH].astype(F32)
     ext[RIM : RIM + TH, PADC + TW :] = east_ref[0:TH].astype(F32)
-    ext[RIM + TH :] = north_ref[...].astype(F32)
 
     joint = joint_weights(stem_ref, weights)
 
@@ -711,16 +745,11 @@
             jax.ShapeDtypeStruct((TH + RIM, PADC, LANES), BF),
             jax.ShapeDtypeStruct((RIM, TW, LANES), BF),
         ],
-        in_specs=[pl.BlockSpec(memory_space=pltpu.HBM)] * 2,
+        in_specs=vmem(2),
         out_specs=vmem(4),
-        scratch_shapes=[
-            pltpu.VMEM((LANES, count), F32),
-            pltpu.VMEM(levels.shape[1:], BF),
-            pltpu.VMEM(ocean.shape, jnp.int32),
-            pltpu.SemaphoreType.DMA((2,)),
-        ],
+        scratch_shapes=[pltpu.VMEM((LANES, count), F32)],
         compiler_params=pltpu.CompilerParams(vmem_limit_bytes=4 << 20),
-    )(levels[0], ocean)
+    )(levels[0], ocean.astype(F32))
 
     def column_pairs(step):
         return [(i, i // TX * TX + (i % TX + step) % TX) for i in range(size)]
@@ -728,11 +757,13 @@
     west = permuted(to_east, column_pairs(1))
     east = permuted(to_west, column_pairs(-1))
 
-    def wide_rows(at):
-        return jnp.concatenate([west[at], tile[at], east[at]], axis=1)
-
-    lower, upper = wide_rows(slice(0, RIM)), wide_rows(slice(TH - RIM, TH))
-    folded = jnp.concatenate([east[TH:], folded, west[TH:]], axis=1)
+    lower, upper, folded = pl.pallas_call(
+        functools.partial(pack_kernel, stem.shape[0] + 1),
+        out_shape=[jax.ShapeDtypeStruct((RIM * TW, LANES), BF)] * 3,
+        in_specs=vmem(4),
+        out_specs=vmem(3),
+        compiler_params=pltpu.CompilerParams(vmem_limit_bytes=4 << 20),
+    )(tile, west, east, folded)
     folded = permuted(folded, [(i, i // TX * TX + TX - 1 - i % TX) for i in range(size - TX, size)])
     if rows == 2:
         north = permuted(jnp.where(is_top, lower, upper), [(i, (i + TX) % size) for i in range(size)])

time: 58.5 us -> 57.9 us (0.990)
  waiting for transfers between devices: 18.5 us -> 13.9 us
  starting transfers between devices: 17.1 us -> 20.8 us
  other arithmetic: 0.5 us -> 1.15 us
    ppermute x14, waiting for transfers between devices: 18.5 us -> 13.9 us  [permuted(): return lax.ppermute(value, 'gy', pairs)]
    ppermute x14, starting transfers between devices: 17.1 us -> 20.8 us  [permuted(): return lax.ppermute(value, 'gy', pairs)]
    convert_element_type x0 -> x1, other arithmetic: none -> 0.69 us  [shards(): ocean.astype(F32)]
    unnamed x18 -> x16, local copies, waits for them, and re-layouts: 2.72 us -> 2.45 us
  transfers between devices with their start and end apart: 14 -> 14, of which waited for: 12 -> 9; matrix products, arithmetic and copies ran while one was open for 0% -> 0% of each run, Pallas kernels for 13% -> 14%
where the time goes in v5:
time: 57.9 us; the launch traced here: 57.7 us
  starting transfers between devices  20.8 us (36%)
  Pallas kernels  18.4 us (32%)
  waiting for transfers between devices  13.9 us (24%)
  local copies, waits for them, and re-layouts  2.53 us (4%)
  other arithmetic  1.15 us (2%)
  between operations  0.94 us (2%)
    ppermute x14, starting transfers between devices, permuted(): return lax.ppermute(value, 'gy', pairs)  20.8 us
    ppermute x14, waiting for transfers between devices, permuted(): return lax.ppermute(value, 'gy', pairs)  13.9 us
    pallas_call x1, Pallas kernels, shards(): pl.pallas_call(functools.partial(main_kernel, 1.0 / math.sqrt(size * coun...  8.52 us
    pallas_call x1, Pallas kernels, rest(): pl.pallas_call(rest_kernel, out_shape=jax.ShapeDtypeStruct((SMALL, LANES)...  4.72 us
    unnamed x16, local copies, waits for them, and re-layouts  2.45 us
    pallas_call x1, Pallas kernels, shards(): pl.pallas_call(middle_kernel, out_shape=mid_shapes, in_specs=vmem(7), out...  2.09 us
    pallas_call x1, Pallas kernels, shards(): pl.pallas_call(unpack_kernel, out_shape=[jax.ShapeDtypeStruct(shape, F32)...  1.63 us
  transfers between devices with their start and end apart: 14, of which 9 were waited for; matrix products, arithmetic and copies ran while one was open for 0% of the time, Pallas kernels for 14%

profile of v5, /device:TPU:0, one launch (start us, length us, event | category | flops | bytes accessed | tf_op | source)
XLA Modules:
  0.0 57.7 jit_solution(2591010994238990568)
XLA Ops:
  0.6 0.7 %convert_element_type.61.ocean_ref = f32[1,512]{1,0:T(1,128)S(1)} convert(s32[1,512]{1,0:T(1,128)} %param.10) | non-fusion elementwise | flops 512 | bytes 4096 | tf_op jit(solution)/shard_map/convert_element_type | solution.py:752
  1.3 0.0 copy-start.3
  1.3 0.9 %copy-done.3 = bf16[1,75,512]{2,1,0:T(8,128)(2,1)S(1)} copy-done((bf16[1,75,512]{2,1,0:T(8,128)(2,1)S(1)}, bf16[1,75,512]{2,1,0:T(8,128)(2,1)}, u32[]{:S(2)}) %copy-start.3) | copy-done | bytes 76824
  2.2 0.0 copy-start.5
  2.2 0.4 shard_map.144
  2.6 0.5 collective-permute-start
  3.1 3.0 %collective-permute-start.1 = (bf16[22,8,128]{2,1,0:T(8,128)(2,1)S(1)}, bf16[22,8,128]{2,1,0:T(8,128)(2,1)S(1)}, u32[]{:S(2)}, u32[]{:S(2)}) collective-permute-start(bf16[22,8,128]{2,1,0:T(8,128)(2,1)S(1)} %get-tuple-element.40), channel_id=1, source_target_pairs={{0,7},{1,0},{2,1},{3,2},{4,3},{5,4},{6,5},{7,6},{8,15},{9,8},{10,9... | collective-permute-start | bytes 135176 | tf_op jit(solution)/shard_map/ppermute | solution.py:671
  6.1 0.0 copy-start.7
  6.1 0.0 copy-start.6
  6.1 0.0 copy-done.5
  6.1 0.7 %copy-done.7 = f32[2,128]{1,0:T(2,128)S(1)} copy-done((f32[2,128]{1,0:T(2,128)S(1)}, f32[2,128]{1,0:T(2,128)}, u32[]{:S(2)}) %copy-start.7) | copy-done | bytes 1048
  6.8 0.0 copy-done.6
  6.8 0.0 copy-start
  6.8 0.0 copy-start.1
  6.9 0.9 %collective-permute-done.west_ref = bf16[22,8,128]{2,1,0:T(8,128)(2,1)S(1)} collective-permute-done((bf16[22,8,128]{2,1,0:T(8,128)(2,1)S(1)}, bf16[22,8,128]{2,1,0:T(8,128)(2,1)S(1)}, u32[]{:S(2)}, u32[]{:S(2)}) %collective-permute-start) | collective-permute-done | bytes 45088 | tf_op jit(solution)/shard_map/ppermute | solution.py:671
  7.8 0.0 collective-permute-done.1.east_ref
  7.8 0.1 shard_map.145
  8.0 0.0 copy-start.4
  8.0 3.3 %collective-permute-start.2 = (bf16[192,128]{1,0:T(8,128)(2,1)S(1)}, bf16[192,128]{1,0:T(8,128)(2,1)S(1)}, u32[]{:S(2)}, u32[]{:S(2)}) collective-permute-start(bf16[192,128]{1,0:T(8,128)(2,1)S(1)} %broadcast_select_fusion.3), channel_id=1, source_target_pairs={{0,8},{1,9},{2,10},{3,11},{4,12},{5,13},{6,14},{7,15},{8,0},{9,1},... | collective-permute-start | bytes 147464 | tf_op jit(solution)/shard_map/ppermute | solution.py:671
  11.3 0.7 %collective-permute-start.3 = (bf16[192,128]{1,0:T(8,128)(2,1)S(1)}, bf16[192,128]{1,0:T(8,128)(2,1)S(1)}, u32[]{:S(2)}, u32[]{:S(2)}) collective-permute-start(bf16[192,128]{1,0:T(8,128)(2,1)S(1)} %get-tuple-element.44), channel_id=1, source_target_pairs={{8,15},{9,14},{10,13},{11,12},{12,11},{13,10},{14,9},{15,8},{24,31... | collective-permute-start | bytes 147464 | tf_op jit(solution)/shard_map/ppermute | solution.py:671
  11.9 0.0 copy-done
  12.0 0.0 copy-done.1
  12.0 0.0 copy-done.4
  12.0 2.1 %shard_map.146 = (bf16[400,128]{1,0:T(8,128)(2,1)S(1)}, f32[400,128]{1,0:T(8,128)S(1)}, f32[400,128]{1,0:T(8,128)S(1)}, bf16[400,128]{1,0:T(8,128)(2,1)S(1)}, bf...) custom-call(bf16[16,32,128]{2,1,0:T(8,128)(2,1)S(1)} %get-tuple-element.38.tile_ref, ...), custom_call_target="tpu_custom_call" | custom-call | flops 4000000000 | bytes 3000000 | tf_op jit(solution)/shard_map/pallas_call | solution.py:791
  14.1 0.0 copy-start.2
  14.1 0.0 collective-permute-done.2
  14.1 0.0 collective-permute-done.3
  14.1 0.9 %copy-done.2 = bf16[1,512,128]{2,1,0:T(8,128)(2,1)S(1)} copy-done((bf16[1,512,128]{2,1,0:T(8,128)(2,1)S(1)}, bf16[1,512,128]{2,1,0:T(8,128)(2,1)}, u32[]{:S(2)}) %copy-start.2) | copy-done | bytes 131096
  15.0 8.5 %shard_map.147 = (bf16[512,128]{1,0:T(8,128)(2,1)}, bf16[2048,128]{1,0:T(8,128)(2,1)S(1)}, f32[8,128]{1,0:T(8,128)S(1)}, bf16[1344,128]{1,0:T(8,128)(2,1)S(1)}, ...) custom-call(s32[1]{0:T(128)} %bitcast.top_ref, ...), custom_call_target="tpu_custom_call" | custom-call | tf_op jit(solution)/shard_map/pallas_call | solution.py:818
  23.5 0.5 collective-permute-start.4
  24.0 1.0 %shard_map.148.gk1 = f32[49,8,128]{2,1,0:T(8,128)S(1)} custom-call(bf16[880,128]{1,0:T(8,128)(2,1)S(1)} %get-tuple-element.61.flat1, bf16[512,128]{1,0:T(8,128)(2,1)S(1)} %get-tuple-element.62.grad1), custom_call_target="tpu_custom_call" | custom-call | flops 2000000000 | bytes 500000 | tf_op jit(solution)/shard_map/pallas_call | solution.py:873
  25.0 0.2 collective-permute-done.4
  25.2 0.1 convert_add_fusion
  25.3 2.5 %collective-permute-start.5 = (bf16[512,128]{1,0:T(8,128)(2,1)S(1)}, bf16[512,128]{1,0:T(8,128)(2,1)S(1)}, u32[]{:S(2)}, u32[]{:S(2)}) collective-permute-start(bf16[512,128]{1,0:T(8,128)(2,1)S(1)} %select_convert_fusion), channel_id=1, source_target_pairs={{0,2},{1,3},{2,0},{3,1},{4,6},{5,7},{6,4},{7,5},{8,10},{9,11},{10,... | collective-permute-start | bytes 393224 | tf_op jit(solution)/shard_map/ppermute | solution.py:671
  27.9 4.7 %shard_map.149 = bf16[192,128]{1,0:T(8,128)(2,1)S(1)} custom-call(s32[1]{0:T(128)} %bitcast.top_ref, f32[51,2,128]{2,1,0:T(2,128)S(1)} %pad_maximum_fusion.4.table_ref.dw_ref, f32[8,128]{1,0:T(8,128)S(1)} %get-tuple-element.56.sums, bf16[1344,128]{1,0:T(8,128)(2,1)S(1)} %get-tuple-element.57.cells, bf16[1344,128]{1,0:T(8,128)(2,1)S(1)} %get-tuple-element.58.flat0, ...), custom_call_target="tpu_custom_call" | custom-call | flops 10000000000 | bytes 4000000 | tf_op jit(solution)/shard_map/pallas_call | solution.py:884
  32.6 0.0 collective-permute-done.5
  32.7 3.3 %collective-permute-start.6 = (bf16[176,128]{1,0:T(8,128)(2,1)S(1)}, bf16[176,128]{1,0:T(8,128)(2,1)S(1)}, u32[]{:S(2)}, u32[]{:S(2)}) collective-permute-start(bf16[176,128]{1,0:T(8,128)(2,1)S(1)} %pad_maximum_fusion.5), channel_id=1, source_target_pairs={{0,12},{1,13},{2,14},{3,15},{4,8},{5,9},{6,10},{7,11},{8,4},{9,5},... | collective-permute-start | bytes 135176 | tf_op jit(solution)/shard_map/ppermute | solution.py:671
  36.0 0.0 collective-permute-start.7
  36.0 1.2 %collective-permute-start.8 = (bf16[176,128]{1,0:T(8,128)(2,1)S(1)}, bf16[176,128]{1,0:T(8,128)(2,1)S(1)}, u32[]{:S(2)}, u32[]{:S(2)}) collective-permute-start(bf16[176,128]{1,0:T(8,128)(2,1)S(1)} %pad_maximum_fusion.7), channel_id=1, source_target_pairs={{0,4},{1,5},{2,6},{3,7},{4,0},{5,1},{6,2},{7,3},{8,12},{9,13},{10,... | collective-permute-start | bytes 135176 | tf_op jit(solution)/shard_map/ppermute | solution.py:671
  37.2 1.5 %collective-permute-done.6 = bf16[176,128]{1,0:T(8,128)(2,1)S(1)} collective-permute-done((bf16[176,128]{1,0:T(8,128)(2,1)S(1)}, bf16[176,128]{1,0:T(8,128)(2,1)S(1)}, u32[]{:S(2)}, u32[]{:S(2)}) %collective-permute-start.6) | collective-permute-done | bytes 45088 | tf_op jit(solution)/shard_map/ppermute | solution.py:671
  38.7 2.6 %collective-permute-done.7 = bf16[176,128]{1,0:T(8,128)(2,1)S(1)} collective-permute-done((bf16[176,128]{1,0:T(8,128)(2,1)S(1)}, bf16[176,128]{1,0:T(8,128)(2,1)S(1)}, u32[]{:S(2)}, u32[]{:S(2)}) %collective-permute-start.7) | collective-permute-done | bytes 45088 | tf_op jit(solution)/shard_map/ppermute | solution.py:671
  41.3 0.0 collective-permute-done.8
  41.4 2.1 %collective-permute-start.11 = (bf16[176,128]{1,0:T(8,128)(2,1)S(1)}, bf16[176,128]{1,0:T(8,128)(2,1)S(1)}, u32[]{:S(2)}, u32[]{:S(2)}) collective-permute-start(bf16[176,128]{1,0:T(8,128)(2,1)S(1)} %get-tuple-element.78), channel_id=1, source_target_pairs={{0,12},{1,13},{2,14},{3,15},{4,8},{5,9},{6,10},{7,11},{8,4},{9,5},... | collective-permute-start | bytes 135176 | tf_op jit(solution)/shard_map/ppermute | solution.py:671
  43.4 0.3 collective-permute-start.9
  43.7 2.1 %collective-permute-start.10 = (bf16[176,128]{1,0:T(8,128)(2,1)S(1)}, bf16[176,128]{1,0:T(8,128)(2,1)S(1)}, u32[]{:S(2)}, u32[]{:S(2)}) collective-permute-start(bf16[176,128]{1,0:T(8,128)(2,1)S(1)} %get-tuple-element.78), channel_id=1, source_target_pairs={{0,8},{1,9},{2,10},{3,11},{4,12},{5,13},{6,14},{7,15},{8,0},{9,1},... | collective-permute-start | bytes 135176 | tf_op jit(solution)/shard_map/ppermute | solution.py:671
  45.8 1.5 %collective-permute-done.11 = bf16[176,128]{1,0:T(8,128)(2,1)S(1)} collective-permute-done((bf16[176,128]{1,0:T(8,128)(2,1)S(1)}, bf16[176,128]{1,0:T(8,128)(2,1)S(1)}, u32[]{:S(2)}, u32[]{:S(2)}) %collective-permute-start.11) | collective-permute-done | bytes 45088 | tf_op jit(solution)/shard_map/ppermute | solution.py:671
  47.3 0.5 collective-permute-done.9
  47.7 0.9 %collective-permute-done.10 = bf16[176,128]{1,0:T(8,128)(2,1)S(1)} collective-permute-done((bf16[176,128]{1,0:T(8,128)(2,1)S(1)}, bf16[176,128]{1,0:T(8,128)(2,1)S(1)}, u32[]{:S(2)}, u32[]{:S(2)}) %collective-permute-start.10) | collective-permute-done | bytes 45088 | tf_op jit(solution)/shard_map/ppermute | solution.py:671
  48.7 1.3 %collective-permute-start.12 = (bf16[4,176,128]{2,1,0:T(8,128)(2,1)S(1)}, bf16[4,176,128]{2,1,0:T(8,128)(2,1)S(1)}, u32[]{:S(2)}, u32[]{:S(2)}) collective-permute-start(bf16[4,176,128]{2,1,0:T(8,128)(2,1)S(1)} %pad_maximum_fusion.3), channel_id=1, source_target_pairs={{0,2},{1,3},{2,0},{3,1},{4,6},{5,7},{6,4},{7,5},{8,10},{9,11},{10,... | collective-permute-start | bytes 540680 | tf_op jit(solution)/shard_map/ppermute | solution.py:671
  50.0 4.2 %collective-permute-done.12 = bf16[4,176,128]{2,1,0:T(8,128)(2,1)S(1)} collective-permute-done((bf16[4,176,128]{2,1,0:T(8,128)(2,1)S(1)}, bf16[4,176,128]{2,1,0:T(8,128)(2,1)S(1)}, u32[]{:S(2)}, u32[]{:S(2)}) %collective-permute-start.12) | collective-permute-done | bytes 180256 | tf_op jit(solution)/shard_map/ppermute | solution.py:671
  54.3 0.1 collective-permute-start.13
  54.4 1.6 %collective-permute-done.13 = bf16[1216,128]{1,0:T(8,128)(2,1)S(1)} collective-permute-done((bf16[1216,128]{1,0:T(8,128)(2,1)S(1)}, bf16[1216,128]{1,0:T(8,128)(2,1)S(1)}, u32[]{:S(2)}, u32[]{:S(2)}) %collective-permute-start.13) | collective-permute-done | bytes 311328 | tf_op jit(solution)/shard_map/ppermute | solution.py:671
  56.0 0.1 pad_maximum_fusion.pieces_ref
  56.1 1.6 %shard_map.150 = (f32[75,128]{1,0:T(8,128)}, f32[49,2,128]{2,1,0:T(2,128)}, f32[2,128]{1,0:T(2,128)}, f32[2,128,512]{2,1,0:T(8,128)}, f32[2,512,128]{2,1,0:T(8,128)}, /*index=5*/f32[2,128]{1,0:T(2,128)}) custom-call(s32[20]{0:T(128)S(1)} %fusion.order_ref, bf16[16,128,128]{2,1,0:T(8,128)(2,1)S(1)} %pad_maximum_fusion.pieces_ref, ...), custom_call_target="tpu_custom_call" | custom-call | tf_op jit(solution)/shard_map/pallas_call | solution.py:906
  (23 shorter events, 0.4 us)
Async XLA Ops:
  1.3 0.9 %copy-start.3 = (bf16[1,75,512]{2,1,0:T(8,128)(2,1)S(1)}, bf16[1,75,512]{2,1,0:T(8,128)(2,1)}, u32[]{:S(2)}) copy-start(bf16[1,75,512]{2,1,0:T(8,128)(2,1)} %param.9) | copy-start | bytes 230404
  2.2 3.9 %copy-start.5 = (f32[2,49,128]{2,0,1:T(2,128)S(1)}, f32[2,49,128]{2,0,1:T(2,128)}, u32[]{:S(2)}) copy-start(f32[2,49,128]{2,0,1:T(2,128)} %param.12) | copy-start | bytes 150532
  2.6 5.2 %collective-permute-start = (bf16[22,8,128]{2,1,0:T(8,128)(2,1)S(1)}, bf16[22,8,128]{2,1,0:T(8,128)(2,1)S(1)}, u32[]{:S(2)}, u32[]{:S(2)}) collective-permute-start(bf16[22,8,128]{2,1,0:T(8,128)(2,1)S(1)} %get-tuple-element.39), channel_id=1, source_target_pairs={{0,1},{1,2},{2,3},{3,4},{4,5},{5,6},{6,7},{7,0},{8,9},{9,10},{10,1... | collective-permute-start | bytes 135176 | tf_op jit(solution)/shard_map/ppermute | solution.py:671
  3.1 4.7 %collective-permute-start.1 = (bf16[22,8,128]{2,1,0:T(8,128)(2,1)S(1)}, bf16[22,8,128]{2,1,0:T(8,128)(2,1)S(1)}, u32[]{:S(2)}, u32[]{:S(2)}) collective-permute-start(bf16[22,8,128]{2,1,0:T(8,128)(2,1)S(1)} %get-tuple-element.40), channel_id=1, source_target_pairs={{0,7},{1,0},{2,1},{3,2},{4,3},{5,4},{6,5},{7,6},{8,15},{9,8},{10,9... | collective-permute-start | bytes 135176 | tf_op jit(solution)/shard_map/ppermute | solution.py:671
  6.1 0.7 %copy-start.7 = (f32[2,128]{1,0:T(2,128)S(1)}, f32[2,128]{1,0:T(2,128)}, u32[]{:S(2)}) copy-start(f32[2,128]{1,0:T(2,128)} %param.13) | copy-start | bytes 3076
  6.1 0.7 %copy-start.6 = (f32[2,128]{1,0:T(2,128)S(1)}, f32[2,128]{1,0:T(2,128)}, u32[]{:S(2)}) copy-start(f32[2,128]{1,0:T(2,128)} %param.16) | copy-start | bytes 3076
  6.8 5.1 %copy-start = (bf16[2,128,512]{2,1,0:T(8,128)(2,1)S(1)}, bf16[2,128,512]{2,1,0:T(8,128)(2,1)}, u32[]{:S(2)}) copy-start(bf16[2,128,512]{2,1,0:T(8,128)(2,1)} %win_ref.3) | copy-start | bytes 786436
  6.8 5.1 %copy-start.1 = (bf16[2,512,128]{2,1,0:T(8,128)(2,1)S(1)}, bf16[2,512,128]{2,1,0:T(8,128)(2,1)}, u32[]{:S(2)}) copy-start(bf16[2,512,128]{2,1,0:T(8,128)(2,1)} %wout_ref.3) | copy-start | bytes 786436
  8.0 4.0 %copy-start.4 = (bf16[75,128]{1,0:T(8,128)(2,1)S(1)}, bf16[75,128]{1,0:T(8,128)(2,1)}, u32[]{:S(2)}) copy-start(bf16[75,128]{1,0:T(8,128)(2,1)} %stem_ref.3) | copy-start | bytes 57604
  8.0 6.1 %collective-permute-start.2 = (bf16[192,128]{1,0:T(8,128)(2,1)S(1)}, bf16[192,128]{1,0:T(8,128)(2,1)S(1)}, u32[]{:S(2)}, u32[]{:S(2)}) collective-permute-start(bf16[192,128]{1,0:T(8,128)(2,1)S(1)} %broadcast_select_fusion.3), channel_id=1, source_target_pairs={{0,8},{1,9},{2,10},{3,11},{4,12},{5,13},{6,14},{7,15},{8,0},{9,1},... | collective-permute-start | bytes 147464 | tf_op jit(solution)/shard_map/ppermute | solution.py:671
  11.3 2.8 %collective-permute-start.3 = (bf16[192,128]{1,0:T(8,128)(2,1)S(1)}, bf16[192,128]{1,0:T(8,128)(2,1)S(1)}, u32[]{:S(2)}, u32[]{:S(2)}) collective-permute-start(bf16[192,128]{1,0:T(8,128)(2,1)S(1)} %get-tuple-element.44), channel_id=1, source_target_pairs={{8,15},{9,14},{10,13},{11,12},{12,11},{13,10},{14,9},{15,8},{24,31... | collective-permute-start | bytes 147464 | tf_op jit(solution)/shard_map/ppermute | solution.py:671
  14.1 0.9 %copy-start.2 = (bf16[1,512,128]{2,1,0:T(8,128)(2,1)S(1)}, bf16[1,512,128]{2,1,0:T(8,128)(2,1)}, u32[]{:S(2)}) copy-start(bf16[1,512,128]{2,1,0:T(8,128)(2,1)} %param.17) | copy-start | bytes 393220
  23.5 1.7 %collective-permute-start.4 = (bf16[1024,128]{1,0:T(8,128)(2,1)S(1)}, bf16[1024,128]{1,0:T(8,128)(2,1)S(1)}, u32[]{:S(2)}, u32[]{:S(2)}) collective-permute-start(bf16[1024,128]{1,0:T(8,128)(2,1)S(1)} %broadcast_select_fusion), channel_id=1, source_target_pairs={{0,1},{1,0},{2,3},{3,2},{4,5},{5,4},{6,7},{7,6},{8,9},{9,8},{10,11... | collective-permute-start | bytes 786440 | tf_op jit(solution)/shard_map/ppermute | solution.py:671
  25.3 7.3 %collective-permute-start.5 = (bf16[512,128]{1,0:T(8,128)(2,1)S(1)}, bf16[512,128]{1,0:T(8,128)(2,1)S(1)}, u32[]{:S(2)}, u32[]{:S(2)}) collective-permute-start(bf16[512,128]{1,0:T(8,128)(2,1)S(1)} %select_convert_fusion), channel_id=1, source_target_pairs={{0,2},{1,3},{2,0},{3,1},{4,6},{5,7},{6,4},{7,5},{8,10},{9,11},{10,... | collective-permute-start | bytes 393224 | tf_op jit(solution)/shard_map/ppermute | solution.py:671
  32.7 6.0 %collective-permute-start.6 = (bf16[176,128]{1,0:T(8,128)(2,1)S(1)}, bf16[176,128]{1,0:T(8,128)(2,1)S(1)}, u32[]{:S(2)}, u32[]{:S(2)}) collective-permute-start(bf16[176,128]{1,0:T(8,128)(2,1)S(1)} %pad_maximum_fusion.5), channel_id=1, source_target_pairs={{0,12},{1,13},{2,14},{3,15},{4,8},{5,9},{6,10},{7,11},{8,4},{9,5},... | collective-permute-start | bytes 135176 | tf_op jit(solution)/shard_map/ppermute | solution.py:671
  36.0 5.3 %collective-permute-start.7 = (bf16[176,128]{1,0:T(8,128)(2,1)S(1)}, bf16[176,128]{1,0:T(8,128)(2,1)S(1)}, u32[]{:S(2)}, u32[]{:S(2)}) collective-permute-start(bf16[176,128]{1,0:T(8,128)(2,1)S(1)} %pad_maximum_fusion.6), channel_id=1, source_target_pairs={{0,8},{1,9},{2,10},{3,11},{4,12},{5,13},{6,14},{7,15},{8,0},{9,1},... | collective-permute-start | bytes 135176 | tf_op jit(solution)/shard_map/ppermute | solution.py:671
  36.0 5.3 %collective-permute-start.8 = (bf16[176,128]{1,0:T(8,128)(2,1)S(1)}, bf16[176,128]{1,0:T(8,128)(2,1)S(1)}, u32[]{:S(2)}, u32[]{:S(2)}) collective-permute-start(bf16[176,128]{1,0:T(8,128)(2,1)S(1)} %pad_maximum_fusion.7), channel_id=1, source_target_pairs={{0,4},{1,5},{2,6},{3,7},{4,0},{5,1},{6,2},{7,3},{8,12},{9,13},{10,... | collective-permute-start | bytes 135176 | tf_op jit(solution)/shard_map/ppermute | solution.py:671
  41.4 5.9 %collective-permute-start.11 = (bf16[176,128]{1,0:T(8,128)(2,1)S(1)}, bf16[176,128]{1,0:T(8,128)(2,1)S(1)}, u32[]{:S(2)}, u32[]{:S(2)}) collective-permute-start(bf16[176,128]{1,0:T(8,128)(2,1)S(1)} %get-tuple-element.78), channel_id=1, source_target_pairs={{0,12},{1,13},{2,14},{3,15},{4,8},{5,9},{6,10},{7,11},{8,4},{9,5},... | collective-permute-start | bytes 135176 | tf_op jit(solution)/shard_map/ppermute | solution.py:671
  43.4 4.3 %collective-permute-start.9 = (bf16[176,128]{1,0:T(8,128)(2,1)S(1)}, bf16[176,128]{1,0:T(8,128)(2,1)S(1)}, u32[]{:S(2)}, u32[]{:S(2)}) collective-permute-start(bf16[176,128]{1,0:T(8,128)(2,1)S(1)} %get-tuple-element.78), channel_id=1, source_target_pairs={{0,4},{1,5},{2,6},{3,7},{4,0},{5,1},{6,2},{7,3},{8,12},{9,13},{10,... | collective-permute-start | bytes 135176 | tf_op jit(solution)/shard_map/ppermute | solution.py:671
  43.7 4.9 %collective-permute-start.10 = (bf16[176,128]{1,0:T(8,128)(2,1)S(1)}, bf16[176,128]{1,0:T(8,128)(2,1)S(1)}, u32[]{:S(2)}, u32[]{:S(2)}) collective-permute-start(bf16[176,128]{1,0:T(8,128)(2,1)S(1)} %get-tuple-element.78), channel_id=1, source_target_pairs={{0,8},{1,9},{2,10},{3,11},{4,12},{5,13},{6,14},{7,15},{8,0},{9,1},... | collective-permute-start | bytes 135176 | tf_op jit(solution)/shard_map/ppermute | solution.py:671
  48.7 5.6 %collective-permute-start.12 = (bf16[4,176,128]{2,1,0:T(8,128)(2,1)S(1)}, bf16[4,176,128]{2,1,0:T(8,128)(2,1)S(1)}, u32[]{:S(2)}, u32[]{:S(2)}) collective-permute-start(bf16[4,176,128]{2,1,0:T(8,128)(2,1)S(1)} %pad_maximum_fusion.3), channel_id=1, source_target_pairs={{0,2},{1,3},{2,0},{3,1},{4,6},{5,7},{6,4},{7,5},{8,10},{9,11},{10,... | collective-permute-start | bytes 540680 | tf_op jit(solution)/shard_map/ppermute | solution.py:671
  54.3 1.7 %collective-permute-start.13 = (bf16[1216,128]{1,0:T(8,128)(2,1)S(1)}, bf16[1216,128]{1,0:T(8,128)(2,1)S(1)}, u32[]{:S(2)}, u32[]{:S(2)}) collective-permute-start(bf16[1216,128]{1,0:T(8,128)(2,1)S(1)} %pad_maximum_fusion.1), channel_id=1, source_target_pairs={{0,1},{1,0},{2,3},{3,2},{4,5},{5,4},{6,7},{7,6},{8,9},{9,8},{10,11... | collective-permute-start | bytes 933896 | tf_op jit(solution)/shard_map/ppermute | solution.py:671

commit v6 on v5

--- a/solution.py
+++ b/solution.py
@@ -220,14 +220,15 @@
         x0[at] = (mask * both[:, :LANES]).astype(BF).astype(F32).reshape(4, EW, LANES)
 
     def conv_columns(block, _):
-        start = pl.multiple_of(block * 8, 8)
+        start = block * 8
         rows = range(MID, MID + MID_ROWS)
         totals = conv_block(x0, (taps,), start + 2, rows, range(RIM, RIM + TH), lambda o, r, a, d: (0, a * 7 + d))
         for o in rows:
-            conv[pl.ds(pl.multiple_of((o - MID) * RW + start, 8), 8), :] = totals[o]
+            conv[pl.ds((o - MID) * RW + start, 8), :] = totals[o]
         return 0
 
-    lax.fori_loop(0, RW // 8, conv_columns, 0)
+    for block in range(RW // 8):
+        conv_columns(block, 0)
     count = MID_ROWS * RW
     spans = spans_of(count, 2 * RW)
     norm_rows(conv, xhat, rinv, normed, table_ref[49, 0:1, :], spans)
@@ -357,7 +358,7 @@
     north_at = 3 + TH
 
     def conv0_block(block, _):
-        start = pl.multiple_of(block * 8, 8)
+        start = block * 8
         for rows in (range(0, MID), range(MID + MID_ROWS, north_at), range(north_at, RH)):
             totals = conv_block(
                 x0,
@@ -368,10 +369,11 @@
                 lambda o, r, a, d: (1 if o >= north_at else 0, a * 7 + d),
             )
             for o in rows:
-                conv0[pl.ds(pl.multiple_of(o * RW + start, 8), 8), :] = totals[o]
+                conv0[pl.ds(o * RW + start, 8), :] = totals[o]
         return 0
 
-    lax.fori_loop(0, RW // 8, conv0_block, 0)
+    for block in range(RW // 8):
+        conv0_block(block, 0)
 
     norm_rows(conv0, xhat0, rinv0, normed0, table_ref[49, 0:1, :], rim0)
     normed0[middle] = mid_normed[...]
@@ -393,16 +395,17 @@
         x1[index * 2 : index * 2 + 2] = flat1[at, :].astype(F32).reshape(2, RW, LANES)
 
     def conv1_block(block, _):
-        start = pl.multiple_of(block * 8, 8)
+        start = block * 8
         for rows in (range(0, 16),):
             totals = conv_block(
                 x1, (taps1,), start, rows, range(0, RH), lambda o, r, a, d: (0, a * 7 + d)
             )
             for o in rows:
-                conv1[pl.ds(pl.multiple_of(o * TW + start, 8), 8), :] = totals[o]
+                conv1[pl.ds(o * TW + start, 8), :] = totals[o]
         return 0
 
-    lax.fori_loop(0, TW // 8, conv1_block, 0)
+    for block in range(TW // 8):
+        conv1_block(block, 0)
     norm_rows(conv1, xhat1, rinv1, normed1, table_ref[49, 1:2, :], all1)
     wide[0:count1] = jnp.dot(normed1[...], win_ref[1], preferred_element_type=F32)
     gelu_rows(wide, act1, slope1, all1)
@@ -469,7 +472,7 @@
     padded(grad1, pad1, TW)
 
     def back1_block(block, _):
-        start = pl.multiple_of(block * 8, 8)
+        start = block * 8
         for rows in (range(0, 22),):
             totals = conv_block(
                 pad1, (taps1,), start + 2, rows, range(6, 6 + TH), lambda o, r, a, d: (0, 48 - (a * 7 + d))
@@ -478,7 +481,8 @@
                 g1[o, pl.ds(start, 8), :] += totals[o]
         return 0
 
-    lax.fori_loop(0, RW // 8, back1_block, 0)
+    for block in range(RW // 8):
+        back1_block(block, 0)
 
     def masked0(index, at, total):
         rows = pl.ds(index * 2, 2)
@@ -510,7 +514,7 @@
     gk1[...] = jnp.zeros_like(gk1)
 
     def kernel1_block(block, _):
-        start = pl.multiple_of(block * 8, 8)
+        start = block * 8
         grads = [pad1[j, pl.ds(start + PADC, 8), :] for j in range(TH)]
         for d in range(7):
             column = [load_column(x1, r, start + d) for r in range(RH)]
@@ -521,7 +525,8 @@
                 gk1[a * 7 + d] = total
         return 0
 
-    lax.fori_loop(0, TW // 8, kernel1_block, 0)
+    for block in range(TW // 8):
+        kernel1_block(block, 0)
 
 
 def rest_kernel(

time: 57.9 us -> 56.7 us (0.979)
  Pallas kernels: 18.4 us -> 16.7 us
  waiting for transfers between devices: 13.9 us -> 14.9 us
    pallas_call x1, Pallas kernels: 8.52 us -> 7.25 us  [shards(): pl.pallas_call(functools.partial(main_kernel, 1.0 / math.sqrt(size * coun...]
    ppermute x14, waiting for transfers between devices: 13.9 us -> 14.9 us  [permuted(): return lax.ppermute(value, 'gy', pairs)]
  transfers between devices with their start and end apart: 14 -> 14, of which waited for: 9 -> 10; matrix products, arithmetic and copies ran while one was open for 0% -> 0% of each run, Pallas kernels for 14% -> 13%
where the time goes in v6:
time: 56.7 us; the launch traced here: 56.4 us
  starting transfers between devices  20.3 us (36%)
  Pallas kernels  16.7 us (29%)
  waiting for transfers between devices  14.9 us (26%)
  local copies, waits for them, and re-layouts  2.43 us (4%)
  other arithmetic  1.15 us (2%)
  between operations  0.92 us (2%)
    ppermute x14, starting transfers between devices, permuted(): return lax.ppermute(value, 'gy', pairs)  20.3 us
    ppermute x14, waiting for transfers between devices, permuted(): return lax.ppermute(value, 'gy', pairs)  14.9 us
    pallas_call x1, Pallas kernels, shards(): pl.pallas_call(functools.partial(main_kernel, 1.0 / math.sqrt(size * coun...  7.25 us
    pallas_call x1, Pallas kernels, rest(): pl.pallas_call(rest_kernel, out_shape=jax.ShapeDtypeStruct((SMALL, LANES)...  4.72 us
    unnamed x16, local copies, waits for them, and re-layouts  2.35 us
    pallas_call x1, Pallas kernels, shards(): pl.pallas_call(middle_kernel, out_shape=mid_shapes, in_specs=vmem(7), out...  1.7 us
    pallas_call x1, Pallas kernels, shards(): pl.pallas_call(unpack_kernel, out_shape=[jax.ShapeDtypeStruct(shape, F32)...  1.63 us
  transfers between devices with their start and end apart: 14, of which 10 were waited for; matrix products, arithmetic and copies ran while one was open for 0% of the time, Pallas kernels for 13%

profile of v6, /device:TPU:0, one launch (start us, length us, event | category | flops | bytes accessed | tf_op | source)
XLA Modules:
  0.0 56.4 jit_solution(12123260402064330213)
XLA Ops:
  0.6 0.7 %convert_element_type.61.ocean_ref = f32[1,512]{1,0:T(1,128)S(1)} convert(s32[1,512]{1,0:T(1,128)} %param.10) | non-fusion elementwise | flops 512 | bytes 4096 | tf_op jit(solution)/shard_map/convert_element_type | solution.py:757
  1.3 0.0 copy-start.3
  1.3 0.9 %copy-done.3 = bf16[1,75,512]{2,1,0:T(8,128)(2,1)S(1)} copy-done((bf16[1,75,512]{2,1,0:T(8,128)(2,1)S(1)}, bf16[1,75,512]{2,1,0:T(8,128)(2,1)}, u32[]{:S(2)}) %copy-start.3) | copy-done | bytes 76824
  2.2 0.0 copy-start.5
  2.2 0.4 shard_map.144
  2.6 0.5 collective-permute-start
  3.1 3.0 %collective-permute-start.1 = (bf16[22,8,128]{2,1,0:T(8,128)(2,1)S(1)}, bf16[22,8,128]{2,1,0:T(8,128)(2,1)S(1)}, u32[]{:S(2)}, u32[]{:S(2)}) collective-permute-start(bf16[22,8,128]{2,1,0:T(8,128)(2,1)S(1)} %get-tuple-element.40), channel_id=1, source_target_pairs={{0,7},{1,0},{2,1},{3,2},{4,3},{5,4},{6,5},{7,6},{8,15},{9,8},{10,9... | collective-permute-start | bytes 135176 | tf_op jit(solution)/shard_map/ppermute | solution.py:676
  6.1 0.0 copy-start.7
  6.1 0.0 copy-start.6
  6.1 0.0 copy-done.5
  6.1 0.7 %copy-done.7 = f32[2,128]{1,0:T(2,128)S(1)} copy-done((f32[2,128]{1,0:T(2,128)S(1)}, f32[2,128]{1,0:T(2,128)}, u32[]{:S(2)}) %copy-start.7) | copy-done | bytes 1048
  6.8 0.0 copy-done.6
  6.8 0.0 copy-start
  6.8 0.0 copy-start.1
  6.9 0.9 %collective-permute-done.west_ref = bf16[22,8,128]{2,1,0:T(8,128)(2,1)S(1)} collective-permute-done((bf16[22,8,128]{2,1,0:T(8,128)(2,1)S(1)}, bf16[22,8,128]{2,1,0:T(8,128)(2,1)S(1)}, u32[]{:S(2)}, u32[]{:S(2)}) %collective-permute-start) | collective-permute-done | bytes 45088 | tf_op jit(solution)/shard_map/ppermute | solution.py:676
  7.8 0.0 collective-permute-done.1.east_ref
  7.8 0.1 shard_map.145
  8.0 0.0 copy-start.4
  8.0 3.3 %collective-permute-start.2 = (bf16[192,128]{1,0:T(8,128)(2,1)S(1)}, bf16[192,128]{1,0:T(8,128)(2,1)S(1)}, u32[]{:S(2)}, u32[]{:S(2)}) collective-permute-start(bf16[192,128]{1,0:T(8,128)(2,1)S(1)} %broadcast_select_fusion.3), channel_id=1, source_target_pairs={{0,8},{1,9},{2,10},{3,11},{4,12},{5,13},{6,14},{7,15},{8,0},{9,1},... | collective-permute-start | bytes 147464 | tf_op jit(solution)/shard_map/ppermute | solution.py:676
  11.3 0.7 %collective-permute-start.3 = (bf16[192,128]{1,0:T(8,128)(2,1)S(1)}, bf16[192,128]{1,0:T(8,128)(2,1)S(1)}, u32[]{:S(2)}, u32[]{:S(2)}) collective-permute-start(bf16[192,128]{1,0:T(8,128)(2,1)S(1)} %get-tuple-element.44), channel_id=1, source_target_pairs={{8,15},{9,14},{10,13},{11,12},{12,11},{13,10},{14,9},{15,8},{24,31... | collective-permute-start | bytes 147464 | tf_op jit(solution)/shard_map/ppermute | solution.py:676
  11.9 0.0 copy-done
  12.0 0.0 copy-done.1
  12.0 0.0 copy-done.4
  12.0 1.7 %shard_map.146 = (bf16[400,128]{1,0:T(8,128)(2,1)S(1)}, f32[400,128]{1,0:T(8,128)S(1)}, f32[400,128]{1,0:T(8,128)S(1)}, bf16[400,128]{1,0:T(8,128)(2,1)S(1)}, bf...) custom-call(bf16[16,32,128]{2,1,0:T(8,128)(2,1)S(1)} %get-tuple-element.38.tile_ref, ...), custom_call_target="tpu_custom_call" | custom-call | flops 4000000000 | bytes 3000000 | tf_op jit(solution)/shard_map/pallas_call | solution.py:796
  13.7 0.0 copy-start.2
  13.7 0.1 collective-permute-done.2
  13.8 0.0 collective-permute-done.3
  13.8 0.8 %copy-done.2 = bf16[1,512,128]{2,1,0:T(8,128)(2,1)S(1)} copy-done((bf16[1,512,128]{2,1,0:T(8,128)(2,1)S(1)}, bf16[1,512,128]{2,1,0:T(8,128)(2,1)}, u32[]{:S(2)}) %copy-start.2) | copy-done | bytes 131096
  14.6 7.3 %shard_map.147 = (bf16[512,128]{1,0:T(8,128)(2,1)}, bf16[2048,128]{1,0:T(8,128)(2,1)S(1)}, f32[8,128]{1,0:T(8,128)S(1)}, bf16[1344,128]{1,0:T(8,128)(2,1)S(1)}, ...) custom-call(s32[1]{0:T(128)} %bitcast.top_ref, ...), custom_call_target="tpu_custom_call" | custom-call | tf_op jit(solution)/shard_map/pallas_call | solution.py:823
  21.9 0.5 collective-permute-start.4
  22.4 0.9 %shard_map.148.gk1 = f32[49,8,128]{2,1,0:T(8,128)S(1)} custom-call(bf16[880,128]{1,0:T(8,128)(2,1)S(1)} %get-tuple-element.61.flat1, bf16[512,128]{1,0:T(8,128)(2,1)S(1)} %get-tuple-element.62.grad1), custom_call_target="tpu_custom_call" | custom-call | flops 2000000000 | bytes 500000 | tf_op jit(solution)/shard_map/pallas_call | solution.py:878
  23.2 0.3 collective-permute-done.4
  23.5 0.1 convert_add_fusion
  23.7 2.5 %collective-permute-start.5 = (bf16[512,128]{1,0:T(8,128)(2,1)S(1)}, bf16[512,128]{1,0:T(8,128)(2,1)S(1)}, u32[]{:S(2)}, u32[]{:S(2)}) collective-permute-start(bf16[512,128]{1,0:T(8,128)(2,1)S(1)} %select_convert_fusion), channel_id=1, source_target_pairs={{0,2},{1,3},{2,0},{3,1},{4,6},{5,7},{6,4},{7,5},{8,10},{9,11},{10,... | collective-permute-start | bytes 393224 | tf_op jit(solution)/shard_map/ppermute | solution.py:676
  26.2 4.7 %shard_map.149 = bf16[192,128]{1,0:T(8,128)(2,1)S(1)} custom-call(s32[1]{0:T(128)} %bitcast.top_ref, f32[51,2,128]{2,1,0:T(2,128)S(1)} %pad_maximum_fusion.4.table_ref.dw_ref, f32[8,128]{1,0:T(8,128)S(1)} %get-tuple-element.56.sums, bf16[1344,128]{1,0:T(8,128)(2,1)S(1)} %get-tuple-element.57.cells, bf16[1344,128]{1,0:T(8,128)(2,1)S(1)} %get-tuple-element.58.flat0, ...), custom_call_target="tpu_custom_call" | custom-call | flops 10000000000 | bytes 4000000 | tf_op jit(solution)/shard_map/pallas_call | solution.py:889
  30.9 0.0 collective-permute-done.5
  31.0 3.7 %collective-permute-start.6 = (bf16[176,128]{1,0:T(8,128)(2,1)S(1)}, bf16[176,128]{1,0:T(8,128)(2,1)S(1)}, u32[]{:S(2)}, u32[]{:S(2)}) collective-permute-start(bf16[176,128]{1,0:T(8,128)(2,1)S(1)} %pad_maximum_fusion.5), channel_id=1, source_target_pairs={{0,12},{1,13},{2,14},{3,15},{4,8},{5,9},{6,10},{7,11},{8,4},{9,5},... | collective-permute-start | bytes 135176 | tf_op jit(solution)/shard_map/ppermute | solution.py:676
  34.7 0.0 collective-permute-start.7
  34.7 0.8 %collective-permute-start.8 = (bf16[176,128]{1,0:T(8,128)(2,1)S(1)}, bf16[176,128]{1,0:T(8,128)(2,1)S(1)}, u32[]{:S(2)}, u32[]{:S(2)}) collective-permute-start(bf16[176,128]{1,0:T(8,128)(2,1)S(1)} %pad_maximum_fusion.7), channel_id=1, source_target_pairs={{0,4},{1,5},{2,6},{3,7},{4,0},{5,1},{6,2},{7,3},{8,12},{9,13},{10,... | collective-permute-start | bytes 135176 | tf_op jit(solution)/shard_map/ppermute | solution.py:676
  35.5 1.5 %collective-permute-done.6 = bf16[176,128]{1,0:T(8,128)(2,1)S(1)} collective-permute-done((bf16[176,128]{1,0:T(8,128)(2,1)S(1)}, bf16[176,128]{1,0:T(8,128)(2,1)S(1)}, u32[]{:S(2)}, u32[]{:S(2)}) %collective-permute-start.6) | collective-permute-done | bytes 45088 | tf_op jit(solution)/shard_map/ppermute | solution.py:676
  37.0 3.0 %collective-permute-done.7 = bf16[176,128]{1,0:T(8,128)(2,1)S(1)} collective-permute-done((bf16[176,128]{1,0:T(8,128)(2,1)S(1)}, bf16[176,128]{1,0:T(8,128)(2,1)S(1)}, u32[]{:S(2)}, u32[]{:S(2)}) %collective-permute-start.7) | collective-permute-done | bytes 45088 | tf_op jit(solution)/shard_map/ppermute | solution.py:676
  40.0 0.0 collective-permute-done.8
  40.1 2.0 %collective-permute-start.11 = (bf16[176,128]{1,0:T(8,128)(2,1)S(1)}, bf16[176,128]{1,0:T(8,128)(2,1)S(1)}, u32[]{:S(2)}, u32[]{:S(2)}) collective-permute-start(bf16[176,128]{1,0:T(8,128)(2,1)S(1)} %get-tuple-element.78), channel_id=1, source_target_pairs={{0,12},{1,13},{2,14},{3,15},{4,8},{5,9},{6,10},{7,11},{8,4},{9,5},... | collective-permute-start | bytes 135176 | tf_op jit(solution)/shard_map/ppermute | solution.py:676
  42.1 0.3 collective-permute-start.9
  42.4 2.1 %collective-permute-start.10 = (bf16[176,128]{1,0:T(8,128)(2,1)S(1)}, bf16[176,128]{1,0:T(8,128)(2,1)S(1)}, u32[]{:S(2)}, u32[]{:S(2)}) collective-permute-start(bf16[176,128]{1,0:T(8,128)(2,1)S(1)} %get-tuple-element.78), channel_id=1, source_target_pairs={{0,8},{1,9},{2,10},{3,11},{4,12},{5,13},{6,14},{7,15},{8,0},{9,1},... | collective-permute-start | bytes 135176 | tf_op jit(solution)/shard_map/ppermute | solution.py:676
  44.5 1.5 %collective-permute-done.11 = bf16[176,128]{1,0:T(8,128)(2,1)S(1)} collective-permute-done((bf16[176,128]{1,0:T(8,128)(2,1)S(1)}, bf16[176,128]{1,0:T(8,128)(2,1)S(1)}, u32[]{:S(2)}, u32[]{:S(2)}) %collective-permute-start.11) | collective-permute-done | bytes 45088 | tf_op jit(solution)/shard_map/ppermute | solution.py:676
  46.0 0.4 collective-permute-done.9
  46.5 0.9 %collective-permute-done.10 = bf16[176,128]{1,0:T(8,128)(2,1)S(1)} collective-permute-done((bf16[176,128]{1,0:T(8,128)(2,1)S(1)}, bf16[176,128]{1,0:T(8,128)(2,1)S(1)}, u32[]{:S(2)}, u32[]{:S(2)}) %collective-permute-start.10) | collective-permute-done | bytes 45088 | tf_op jit(solution)/shard_map/ppermute | solution.py:676
  47.4 0.9 %collective-permute-start.12 = (bf16[4,176,128]{2,1,0:T(8,128)(2,1)S(1)}, bf16[4,176,128]{2,1,0:T(8,128)(2,1)S(1)}, u32[]{:S(2)}, u32[]{:S(2)}) collective-permute-start(bf16[4,176,128]{2,1,0:T(8,128)(2,1)S(1)} %pad_maximum_fusion.3), channel_id=1, source_target_pairs={{0,2},{1,3},{2,0},{3,1},{4,6},{5,7},{6,4},{7,5},{8,10},{9,11},{10,... | collective-permute-start | bytes 540680 | tf_op jit(solution)/shard_map/ppermute | solution.py:676
  48.3 4.6 %collective-permute-done.12 = bf16[4,176,128]{2,1,0:T(8,128)(2,1)S(1)} collective-permute-done((bf16[4,176,128]{2,1,0:T(8,128)(2,1)S(1)}, bf16[4,176,128]{2,1,0:T(8,128)(2,1)S(1)}, u32[]{:S(2)}, u32[]{:S(2)}) %collective-permute-start.12) | collective-permute-done | bytes 180256 | tf_op jit(solution)/shard_map/ppermute | solution.py:676
  53.0 0.1 collective-permute-start.13
  53.1 1.6 %collective-permute-done.13 = bf16[1216,128]{1,0:T(8,128)(2,1)S(1)} collective-permute-done((bf16[1216,128]{1,0:T(8,128)(2,1)S(1)}, bf16[1216,128]{1,0:T(8,128)(2,1)S(1)}, u32[]{:S(2)}, u32[]{:S(2)}) %collective-permute-start.13) | collective-permute-done | bytes 311328 | tf_op jit(solution)/shard_map/ppermute | solution.py:676
  54.7 0.1 pad_maximum_fusion.pieces_ref
  54.8 1.6 %shard_map.150 = (f32[75,128]{1,0:T(8,128)}, f32[49,2,128]{2,1,0:T(2,128)}, f32[2,128]{1,0:T(2,128)}, f32[2,128,512]{2,1,0:T(8,128)}, f32[2,512,128]{2,1,0:T(8,128)}, /*index=5*/f32[2,128]{1,0:T(2,128)}) custom-call(s32[20]{0:T(128)S(1)} %fusion.order_ref, bf16[16,128,128]{2,1,0:T(8,128)(2,1)S(1)} %pad_maximum_fusion.pieces_ref, ...), custom_call_target="tpu_custom_call" | custom-call | tf_op jit(solution)/shard_map/pallas_call | solution.py:911
  (23 shorter events, 0.4 us)
Async XLA Ops:
  1.3 0.9 %copy-start.3 = (bf16[1,75,512]{2,1,0:T(8,128)(2,1)S(1)}, bf16[1,75,512]{2,1,0:T(8,128)(2,1)}, u32[]{:S(2)}) copy-start(bf16[1,75,512]{2,1,0:T(8,128)(2,1)} %param.9) | copy-start | bytes 230404
  2.2 3.9 %copy-start.5 = (f32[2,49,128]{2,0,1:T(2,128)S(1)}, f32[2,49,128]{2,0,1:T(2,128)}, u32[]{:S(2)}) copy-start(f32[2,49,128]{2,0,1:T(2,128)} %param.12) | copy-start | bytes 150532
  2.6 5.2 %collective-permute-start = (bf16[22,8,128]{2,1,0:T(8,128)(2,1)S(1)}, bf16[22,8,128]{2,1,0:T(8,128)(2,1)S(1)}, u32[]{:S(2)}, u32[]{:S(2)}) collective-permute-start(bf16[22,8,128]{2,1,0:T(8,128)(2,1)S(1)} %get-tuple-element.39), channel_id=1, source_target_pairs={{0,1},{1,2},{2,3},{3,4},{4,5},{5,6},{6,7},{7,0},{8,9},{9,10},{10,1... | collective-permute-start | bytes 135176 | tf_op jit(solution)/shard_map/ppermute | solution.py:676
  3.1 4.7 %collective-permute-start.1 = (bf16[22,8,128]{2,1,0:T(8,128)(2,1)S(1)}, bf16[22,8,128]{2,1,0:T(8,128)(2,1)S(1)}, u32[]{:S(2)}, u32[]{:S(2)}) collective-permute-start(bf16[22,8,128]{2,1,0:T(8,128)(2,1)S(1)} %get-tuple-element.40), channel_id=1, source_target_pairs={{0,7},{1,0},{2,1},{3,2},{4,3},{5,4},{6,5},{7,6},{8,15},{9,8},{10,9... | collective-permute-start | bytes 135176 | tf_op jit(solution)/shard_map/ppermute | solution.py:676
  6.1 0.7 %copy-start.7 = (f32[2,128]{1,0:T(2,128)S(1)}, f32[2,128]{1,0:T(2,128)}, u32[]{:S(2)}) copy-start(f32[2,128]{1,0:T(2,128)} %param.13) | copy-start | bytes 3076
  6.1 0.7 %copy-start.6 = (f32[2,128]{1,0:T(2,128)S(1)}, f32[2,128]{1,0:T(2,128)}, u32[]{:S(2)}) copy-start(f32[2,128]{1,0:T(2,128)} %param.16) | copy-start | bytes 3076
  6.8 5.1 %copy-start = (bf16[2,128,512]{2,1,0:T(8,128)(2,1)S(1)}, bf16[2,128,512]{2,1,0:T(8,128)(2,1)}, u32[]{:S(2)}) copy-start(bf16[2,128,512]{2,1,0:T(8,128)(2,1)} %win_ref.3) | copy-start | bytes 786436
  6.8 5.1 %copy-start.1 = (bf16[2,512,128]{2,1,0:T(8,128)(2,1)S(1)}, bf16[2,512,128]{2,1,0:T(8,128)(2,1)}, u32[]{:S(2)}) copy-start(bf16[2,512,128]{2,1,0:T(8,128)(2,1)} %wout_ref.3) | copy-start | bytes 786436
  8.0 4.0 %copy-start.4 = (bf16[75,128]{1,0:T(8,128)(2,1)S(1)}, bf16[75,128]{1,0:T(8,128)(2,1)}, u32[]{:S(2)}) copy-start(bf16[75,128]{1,0:T(8,128)(2,1)} %stem_ref.3) | copy-start | bytes 57604
  8.0 5.8 %collective-permute-start.2 = (bf16[192,128]{1,0:T(8,128)(2,1)S(1)}, bf16[192,128]{1,0:T(8,128)(2,1)S(1)}, u32[]{:S(2)}, u32[]{:S(2)}) collective-permute-start(bf16[192,128]{1,0:T(8,128)(2,1)S(1)} %broadcast_select_fusion.3), channel_id=1, source_target_pairs={{0,8},{1,9},{2,10},{3,11},{4,12},{5,13},{6,14},{7,15},{8,0},{9,1},... | collective-permute-start | bytes 147464 | tf_op jit(solution)/shard_map/ppermute | solution.py:676
  11.3 2.5 %collective-permute-start.3 = (bf16[192,128]{1,0:T(8,128)(2,1)S(1)}, bf16[192,128]{1,0:T(8,128)(2,1)S(1)}, u32[]{:S(2)}, u32[]{:S(2)}) collective-permute-start(bf16[192,128]{1,0:T(8,128)(2,1)S(1)} %get-tuple-element.44), channel_id=1, source_target_pairs={{8,15},{9,14},{10,13},{11,12},{12,11},{13,10},{14,9},{15,8},{24,31... | collective-permute-start | bytes 147464 | tf_op jit(solution)/shard_map/ppermute | solution.py:676
  13.7 0.9 %copy-start.2 = (bf16[1,512,128]{2,1,0:T(8,128)(2,1)S(1)}, bf16[1,512,128]{2,1,0:T(8,128)(2,1)}, u32[]{:S(2)}) copy-start(bf16[1,512,128]{2,1,0:T(8,128)(2,1)} %param.17) | copy-start | bytes 393220
  21.9 1.7 %collective-permute-start.4 = (bf16[1024,128]{1,0:T(8,128)(2,1)S(1)}, bf16[1024,128]{1,0:T(8,128)(2,1)S(1)}, u32[]{:S(2)}, u32[]{:S(2)}) collective-permute-start(bf16[1024,128]{1,0:T(8,128)(2,1)S(1)} %broadcast_select_fusion), channel_id=1, source_target_pairs={{0,1},{1,0},{2,3},{3,2},{4,5},{5,4},{6,7},{7,6},{8,9},{9,8},{10,11... | collective-permute-start | bytes 786440 | tf_op jit(solution)/shard_map/ppermute | solution.py:676
  23.7 7.3 %collective-permute-start.5 = (bf16[512,128]{1,0:T(8,128)(2,1)S(1)}, bf16[512,128]{1,0:T(8,128)(2,1)S(1)}, u32[]{:S(2)}, u32[]{:S(2)}) collective-permute-start(bf16[512,128]{1,0:T(8,128)(2,1)S(1)} %select_convert_fusion), channel_id=1, source_target_pairs={{0,2},{1,3},{2,0},{3,1},{4,6},{5,7},{6,4},{7,5},{8,10},{9,11},{10,... | collective-permute-start | bytes 393224 | tf_op jit(solution)/shard_map/ppermute | solution.py:676
  31.0 6.0 %collective-permute-start.6 = (bf16[176,128]{1,0:T(8,128)(2,1)S(1)}, bf16[176,128]{1,0:T(8,128)(2,1)S(1)}, u32[]{:S(2)}, u32[]{:S(2)}) collective-permute-start(bf16[176,128]{1,0:T(8,128)(2,1)S(1)} %pad_maximum_fusion.5), channel_id=1, source_target_pairs={{0,12},{1,13},{2,14},{3,15},{4,8},{5,9},{6,10},{7,11},{8,4},{9,5},... | collective-permute-start | bytes 135176 | tf_op jit(solution)/shard_map/ppermute | solution.py:676
  34.7 5.3 %collective-permute-start.7 = (bf16[176,128]{1,0:T(8,128)(2,1)S(1)}, bf16[176,128]{1,0:T(8,128)(2,1)S(1)}, u32[]{:S(2)}, u32[]{:S(2)}) collective-permute-start(bf16[176,128]{1,0:T(8,128)(2,1)S(1)} %pad_maximum_fusion.6), channel_id=1, source_target_pairs={{0,8},{1,9},{2,10},{3,11},{4,12},{5,13},{6,14},{7,15},{8,0},{9,1},... | collective-permute-start | bytes 135176 | tf_op jit(solution)/shard_map/ppermute | solution.py:676
  34.7 5.3 %collective-permute-start.8 = (bf16[176,128]{1,0:T(8,128)(2,1)S(1)}, bf16[176,128]{1,0:T(8,128)(2,1)S(1)}, u32[]{:S(2)}, u32[]{:S(2)}) collective-permute-start(bf16[176,128]{1,0:T(8,128)(2,1)S(1)} %pad_maximum_fusion.7), channel_id=1, source_target_pairs={{0,4},{1,5},{2,6},{3,7},{4,0},{5,1},{6,2},{7,3},{8,12},{9,13},{10,... | collective-permute-start | bytes 135176 | tf_op jit(solution)/shard_map/ppermute | solution.py:676
  40.1 5.9 %collective-permute-start.11 = (bf16[176,128]{1,0:T(8,128)(2,1)S(1)}, bf16[176,128]{1,0:T(8,128)(2,1)S(1)}, u32[]{:S(2)}, u32[]{:S(2)}) collective-permute-start(bf16[176,128]{1,0:T(8,128)(2,1)S(1)} %get-tuple-element.78), channel_id=1, source_target_pairs={{0,12},{1,13},{2,14},{3,15},{4,8},{5,9},{6,10},{7,11},{8,4},{9,5},... | collective-permute-start | bytes 135176 | tf_op jit(solution)/shard_map/ppermute | solution.py:676
  42.1 4.4 %collective-permute-start.9 = (bf16[176,128]{1,0:T(8,128)(2,1)S(1)}, bf16[176,128]{1,0:T(8,128)(2,1)S(1)}, u32[]{:S(2)}, u32[]{:S(2)}) collective-permute-start(bf16[176,128]{1,0:T(8,128)(2,1)S(1)} %get-tuple-element.78), channel_id=1, source_target_pairs={{0,4},{1,5},{2,6},{3,7},{4,0},{5,1},{6,2},{7,3},{8,12},{9,13},{10,... | collective-permute-start | bytes 135176 | tf_op jit(solution)/shard_map/ppermute | solution.py:676
  42.4 4.9 %collective-permute-start.10 = (bf16[176,128]{1,0:T(8,128)(2,1)S(1)}, bf16[176,128]{1,0:T(8,128)(2,1)S(1)}, u32[]{:S(2)}, u32[]{:S(2)}) collective-permute-start(bf16[176,128]{1,0:T(8,128)(2,1)S(1)} %get-tuple-element.78), channel_id=1, source_target_pairs={{0,8},{1,9},{2,10},{3,11},{4,12},{5,13},{6,14},{7,15},{8,0},{9,1},... | collective-permute-start | bytes 135176 | tf_op jit(solution)/shard_map/ppermute | solution.py:676
  47.4 5.6 %collective-permute-start.12 = (bf16[4,176,128]{2,1,0:T(8,128)(2,1)S(1)}, bf16[4,176,128]{2,1,0:T(8,128)(2,1)S(1)}, u32[]{:S(2)}, u32[]{:S(2)}) collective-permute-start(bf16[4,176,128]{2,1,0:T(8,128)(2,1)S(1)} %pad_maximum_fusion.3), channel_id=1, source_target_pairs={{0,2},{1,3},{2,0},{3,1},{4,6},{5,7},{6,4},{7,5},{8,10},{9,11},{10,... | collective-permute-start | bytes 540680 | tf_op jit(solution)/shard_map/ppermute | solution.py:676
  53.0 1.7 %collective-permute-start.13 = (bf16[1216,128]{1,0:T(8,128)(2,1)S(1)}, bf16[1216,128]{1,0:T(8,128)(2,1)S(1)}, u32[]{:S(2)}, u32[]{:S(2)}) collective-permute-start(bf16[1216,128]{1,0:T(8,128)(2,1)S(1)} %pad_maximum_fusion.1), channel_id=1, source_target_pairs={{0,1},{1,0},{2,3},{3,2},{4,5},{5,4},{6,7},{7,6},{8,9},{9,8},{10,11... | collective-permute-start | bytes 933896 | tf_op jit(solution)/shard_map/ppermute | solution.py:676

commit v7 on v6

--- a/solution.py
+++ b/solution.py
@@ -562,7 +562,7 @@
     gk0n[...] = jnp.zeros_like(gk0n)
 
     def kernel0_block(block, _):
-        start = pl.multiple_of(block * 8, 8)
+        start = block * 8
         grads = [pad0[j, pl.ds(start + PADC, 8), :] for j in range(RH)]
         for d in range(7):
             column = [load_column(x0, r, start + 2 + d) for r in range(EH)]
@@ -577,7 +577,8 @@
                 gk0n[a * 7 + d] = total
         return 0
 
-    lax.fori_loop(0, RW // 8, kernel0_block, 0)
+    for block in range(RW // 8):
+        kernel0_block(block, 0)
     for t in range(49):
         north = jnp.where(top, gk0n[48 - t], gk0n[t])
         small[KERNEL_AT[0] + t : KERNEL_AT[0] + t + 1, :] = jnp.sum(gk0[t] + north, axis=0, keepdims=True)

time: 56.7 us -> 57.3 us (1.011)
  Pallas kernels: 16.7 us -> 17.3 us
    pallas_call x1, Pallas kernels: 4.72 us -> 5.39 us  [rest(): pl.pallas_call(rest_kernel, out_shape=jax.ShapeDtypeStruct((SMALL, LANES)...]
  transfers between devices with their start and end apart: 14 -> 14, of which waited for: 10 -> 10; matrix products, arithmetic and copies ran while one was open for 0% -> 0% of each run, Pallas kernels for 13% -> 14%
where the time goes in v7:
time: 57.3 us; the launch traced here: 57.1 us
  starting transfers between devices  20.3 us (35%)
  Pallas kernels  17.3 us (30%)
  waiting for transfers between devices  14.9 us (26%)
  local copies, waits for them, and re-layouts  2.43 us (4%)
  other arithmetic  1.15 us (2%)
  between operations  0.92 us (2%)
    ppermute x14, starting transfers between devices, permuted(): return lax.ppermute(value, 'gy', pairs)  20.3 us
    ppermute x14, waiting for transfers between devices, permuted(): return lax.ppermute(value, 'gy', pairs)  14.9 us
    pallas_call x1, Pallas kernels, shards(): pl.pallas_call(functools.partial(main_kernel, 1.0 / math.sqrt(size * coun...  7.25 us
    pallas_call x1, Pallas kernels, rest(): pl.pallas_call(rest_kernel, out_shape=jax.ShapeDtypeStruct((SMALL, LANES)...  5.39 us
    unnamed x16, local copies, waits for them, and re-layouts  2.35 us
    pallas_call x1, Pallas kernels, shards(): pl.pallas_call(middle_kernel, out_shape=mid_shapes, in_specs=vmem(7), out...  1.7 us
    pallas_call x1, Pallas kernels, shards(): pl.pallas_call(unpack_kernel, out_shape=[jax.ShapeDtypeStruct(shape, F32)...  1.63 us
  transfers between devices with their start and end apart: 14, of which 10 were waited for; matrix products, arithmetic and copies ran while one was open for 0% of the time, Pallas kernels for 14%

profile of v7, /device:TPU:0, one launch (start us, length us, event | category | flops | bytes accessed | tf_op | source)
XLA Modules:
  0.0 57.1 jit_solution(18411173576639781349)
XLA Ops:
  0.6 0.7 %convert_element_type.61.ocean_ref = f32[1,512]{1,0:T(1,128)S(1)} convert(s32[1,512]{1,0:T(1,128)} %param.10) | non-fusion elementwise | flops 512 | bytes 4096 | tf_op jit(solution)/shard_map/convert_element_type | solution.py:758
  1.3 0.0 copy-start.3
  1.3 0.9 %copy-done.3 = bf16[1,75,512]{2,1,0:T(8,128)(2,1)S(1)} copy-done((bf16[1,75,512]{2,1,0:T(8,128)(2,1)S(1)}, bf16[1,75,512]{2,1,0:T(8,128)(2,1)}, u32[]{:S(2)}) %copy-start.3) | copy-done | bytes 76824
  2.2 0.0 copy-start.5
  2.2 0.4 shard_map.144
  2.6 0.5 collective-permute-start
  3.1 3.0 %collective-permute-start.1 = (bf16[22,8,128]{2,1,0:T(8,128)(2,1)S(1)}, bf16[22,8,128]{2,1,0:T(8,128)(2,1)S(1)}, u32[]{:S(2)}, u32[]{:S(2)}) collective-permute-start(bf16[22,8,128]{2,1,0:T(8,128)(2,1)S(1)} %get-tuple-element.40), channel_id=1, source_target_pairs={{0,7},{1,0},{2,1},{3,2},{4,3},{5,4},{6,5},{7,6},{8,15},{9,8},{10,9... | collective-permute-start | bytes 135176 | tf_op jit(solution)/shard_map/ppermute | solution.py:677
  6.1 0.0 copy-start.7
  6.1 0.0 copy-start.6
  6.1 0.0 copy-done.5
  6.1 0.7 %copy-done.7 = f32[2,128]{1,0:T(2,128)S(1)} copy-done((f32[2,128]{1,0:T(2,128)S(1)}, f32[2,128]{1,0:T(2,128)}, u32[]{:S(2)}) %copy-start.7) | copy-done | bytes 1048
  6.8 0.0 copy-done.6
  6.8 0.0 copy-start
  6.8 0.0 copy-start.1
  6.9 0.9 %collective-permute-done.west_ref = bf16[22,8,128]{2,1,0:T(8,128)(2,1)S(1)} collective-permute-done((bf16[22,8,128]{2,1,0:T(8,128)(2,1)S(1)}, bf16[22,8,128]{2,1,0:T(8,128)(2,1)S(1)}, u32[]{:S(2)}, u32[]{:S(2)}) %collective-permute-start) | collective-permute-done | bytes 45088 | tf_op jit(solution)/shard_map/ppermute | solution.py:677
  7.8 0.0 collective-permute-done.1.east_ref
  7.8 0.1 shard_map.145
  8.0 0.0 copy-start.4
  8.0 3.3 %collective-permute-start.2 = (bf16[192,128]{1,0:T(8,128)(2,1)S(1)}, bf16[192,128]{1,0:T(8,128)(2,1)S(1)}, u32[]{:S(2)}, u32[]{:S(2)}) collective-permute-start(bf16[192,128]{1,0:T(8,128)(2,1)S(1)} %broadcast_select_fusion.3), channel_id=1, source_target_pairs={{0,8},{1,9},{2,10},{3,11},{4,12},{5,13},{6,14},{7,15},{8,0},{9,1},... | collective-permute-start | bytes 147464 | tf_op jit(solution)/shard_map/ppermute | solution.py:677
  11.3 0.7 %collective-permute-start.3 = (bf16[192,128]{1,0:T(8,128)(2,1)S(1)}, bf16[192,128]{1,0:T(8,128)(2,1)S(1)}, u32[]{:S(2)}, u32[]{:S(2)}) collective-permute-start(bf16[192,128]{1,0:T(8,128)(2,1)S(1)} %get-tuple-element.44), channel_id=1, source_target_pairs={{8,15},{9,14},{10,13},{11,12},{12,11},{13,10},{14,9},{15,8},{24,31... | collective-permute-start | bytes 147464 | tf_op jit(solution)/shard_map/ppermute | solution.py:677
  11.9 0.0 copy-done
  12.0 0.0 copy-done.1
  12.0 0.0 copy-done.4
  12.0 1.7 %shard_map.146 = (bf16[400,128]{1,0:T(8,128)(2,1)S(1)}, f32[400,128]{1,0:T(8,128)S(1)}, f32[400,128]{1,0:T(8,128)S(1)}, bf16[400,128]{1,0:T(8,128)(2,1)S(1)}, bf...) custom-call(bf16[16,32,128]{2,1,0:T(8,128)(2,1)S(1)} %get-tuple-element.38.tile_ref, ...), custom_call_target="tpu_custom_call" | custom-call | flops 4000000000 | bytes 3000000 | tf_op jit(solution)/shard_map/pallas_call | solution.py:797
  13.7 0.0 copy-start.2
  13.7 0.1 collective-permute-done.2
  13.8 0.0 collective-permute-done.3
  13.8 0.8 %copy-done.2 = bf16[1,512,128]{2,1,0:T(8,128)(2,1)S(1)} copy-done((bf16[1,512,128]{2,1,0:T(8,128)(2,1)S(1)}, bf16[1,512,128]{2,1,0:T(8,128)(2,1)}, u32[]{:S(2)}) %copy-start.2) | copy-done | bytes 131096
  14.6 7.3 %shard_map.147 = (bf16[512,128]{1,0:T(8,128)(2,1)}, bf16[2048,128]{1,0:T(8,128)(2,1)S(1)}, f32[8,128]{1,0:T(8,128)S(1)}, bf16[1344,128]{1,0:T(8,128)(2,1)S(1)}, ...) custom-call(s32[1]{0:T(128)} %bitcast.top_ref, ...), custom_call_target="tpu_custom_call" | custom-call | tf_op jit(solution)/shard_map/pallas_call | solution.py:824
  21.9 0.5 collective-permute-start.4
  22.4 0.9 %shard_map.148.gk1 = f32[49,8,128]{2,1,0:T(8,128)S(1)} custom-call(bf16[880,128]{1,0:T(8,128)(2,1)S(1)} %get-tuple-element.61.flat1, bf16[512,128]{1,0:T(8,128)(2,1)S(1)} %get-tuple-element.62.grad1), custom_call_target="tpu_custom_call" | custom-call | flops 2000000000 | bytes 500000 | tf_op jit(solution)/shard_map/pallas_call | solution.py:879
  23.2 0.3 collective-permute-done.4
  23.5 0.1 convert_add_fusion
  23.7 2.5 %collective-permute-start.5 = (bf16[512,128]{1,0:T(8,128)(2,1)S(1)}, bf16[512,128]{1,0:T(8,128)(2,1)S(1)}, u32[]{:S(2)}, u32[]{:S(2)}) collective-permute-start(bf16[512,128]{1,0:T(8,128)(2,1)S(1)} %select_convert_fusion), channel_id=1, source_target_pairs={{0,2},{1,3},{2,0},{3,1},{4,6},{5,7},{6,4},{7,5},{8,10},{9,11},{10,... | collective-permute-start | bytes 393224 | tf_op jit(solution)/shard_map/ppermute | solution.py:677
  26.2 5.4 %shard_map.149 = bf16[192,128]{1,0:T(8,128)(2,1)S(1)} custom-call(s32[1]{0:T(128)} %bitcast.top_ref, f32[51,2,128]{2,1,0:T(2,128)S(1)} %pad_maximum_fusion.4.table_ref.dw_ref, f32[8,128]{1,0:T(8,128)S(1)} %get-tuple-element.56.sums, bf16[1344,128]{1,0:T(8,128)(2,1)S(1)} %get-tuple-element.57.cells, bf16[1344,128]{1,0:T(8,128)(2,1)S(1)} %get-tuple-element.58.flat0, ...), custom_call_target="tpu_custom_call" | custom-call | flops 10000000000 | bytes 4000000 | tf_op jit(solution)/shard_map/pallas_call | solution.py:890
  31.6 0.0 collective-permute-done.5
  31.7 3.7 %collective-permute-start.6 = (bf16[176,128]{1,0:T(8,128)(2,1)S(1)}, bf16[176,128]{1,0:T(8,128)(2,1)S(1)}, u32[]{:S(2)}, u32[]{:S(2)}) collective-permute-start(bf16[176,128]{1,0:T(8,128)(2,1)S(1)} %pad_maximum_fusion.5), channel_id=1, source_target_pairs={{0,12},{1,13},{2,14},{3,15},{4,8},{5,9},{6,10},{7,11},{8,4},{9,5},... | collective-permute-start | bytes 135176 | tf_op jit(solution)/shard_map/ppermute | solution.py:677
  35.4 0.0 collective-permute-start.7
  35.4 0.8 %collective-permute-start.8 = (bf16[176,128]{1,0:T(8,128)(2,1)S(1)}, bf16[176,128]{1,0:T(8,128)(2,1)S(1)}, u32[]{:S(2)}, u32[]{:S(2)}) collective-permute-start(bf16[176,128]{1,0:T(8,128)(2,1)S(1)} %pad_maximum_fusion.7), channel_id=1, source_target_pairs={{0,4},{1,5},{2,6},{3,7},{4,0},{5,1},{6,2},{7,3},{8,12},{9,13},{10,... | collective-permute-start | bytes 135176 | tf_op jit(solution)/shard_map/ppermute | solution.py:677
  36.2 1.5 %collective-permute-done.6 = bf16[176,128]{1,0:T(8,128)(2,1)S(1)} collective-permute-done((bf16[176,128]{1,0:T(8,128)(2,1)S(1)}, bf16[176,128]{1,0:T(8,128)(2,1)S(1)}, u32[]{:S(2)}, u32[]{:S(2)}) %collective-permute-start.6) | collective-permute-done | bytes 45088 | tf_op jit(solution)/shard_map/ppermute | solution.py:677
  37.7 3.0 %collective-permute-done.7 = bf16[176,128]{1,0:T(8,128)(2,1)S(1)} collective-permute-done((bf16[176,128]{1,0:T(8,128)(2,1)S(1)}, bf16[176,128]{1,0:T(8,128)(2,1)S(1)}, u32[]{:S(2)}, u32[]{:S(2)}) %collective-permute-start.7) | collective-permute-done | bytes 45088 | tf_op jit(solution)/shard_map/ppermute | solution.py:677
  40.7 0.0 collective-permute-done.8
  40.7 2.0 %collective-permute-start.11 = (bf16[176,128]{1,0:T(8,128)(2,1)S(1)}, bf16[176,128]{1,0:T(8,128)(2,1)S(1)}, u32[]{:S(2)}, u32[]{:S(2)}) collective-permute-start(bf16[176,128]{1,0:T(8,128)(2,1)S(1)} %get-tuple-element.78), channel_id=1, source_target_pairs={{0,12},{1,13},{2,14},{3,15},{4,8},{5,9},{6,10},{7,11},{8,4},{9,5},... | collective-permute-start | bytes 135176 | tf_op jit(solution)/shard_map/ppermute | solution.py:677
  42.7 0.3 collective-permute-start.9
  43.1 2.1 %collective-permute-start.10 = (bf16[176,128]{1,0:T(8,128)(2,1)S(1)}, bf16[176,128]{1,0:T(8,128)(2,1)S(1)}, u32[]{:S(2)}, u32[]{:S(2)}) collective-permute-start(bf16[176,128]{1,0:T(8,128)(2,1)S(1)} %get-tuple-element.78), channel_id=1, source_target_pairs={{0,8},{1,9},{2,10},{3,11},{4,12},{5,13},{6,14},{7,15},{8,0},{9,1},... | collective-permute-start | bytes 135176 | tf_op jit(solution)/shard_map/ppermute | solution.py:677
  45.2 1.5 %collective-permute-done.11 = bf16[176,128]{1,0:T(8,128)(2,1)S(1)} collective-permute-done((bf16[176,128]{1,0:T(8,128)(2,1)S(1)}, bf16[176,128]{1,0:T(8,128)(2,1)S(1)}, u32[]{:S(2)}, u32[]{:S(2)}) %collective-permute-start.11) | collective-permute-done | bytes 45088 | tf_op jit(solution)/shard_map/ppermute | solution.py:677
  46.7 0.4 collective-permute-done.9
  47.1 0.9 %collective-permute-done.10 = bf16[176,128]{1,0:T(8,128)(2,1)S(1)} collective-permute-done((bf16[176,128]{1,0:T(8,128)(2,1)S(1)}, bf16[176,128]{1,0:T(8,128)(2,1)S(1)}, u32[]{:S(2)}, u32[]{:S(2)}) %collective-permute-start.10) | collective-permute-done | bytes 45088 | tf_op jit(solution)/shard_map/ppermute | solution.py:677
  48.0 0.9 %collective-permute-start.12 = (bf16[4,176,128]{2,1,0:T(8,128)(2,1)S(1)}, bf16[4,176,128]{2,1,0:T(8,128)(2,1)S(1)}, u32[]{:S(2)}, u32[]{:S(2)}) collective-permute-start(bf16[4,176,128]{2,1,0:T(8,128)(2,1)S(1)} %pad_maximum_fusion.3), channel_id=1, source_target_pairs={{0,2},{1,3},{2,0},{3,1},{4,6},{5,7},{6,4},{7,5},{8,10},{9,11},{10,... | collective-permute-start | bytes 540680 | tf_op jit(solution)/shard_map/ppermute | solution.py:677
  49.0 4.6 %collective-permute-done.12 = bf16[4,176,128]{2,1,0:T(8,128)(2,1)S(1)} collective-permute-done((bf16[4,176,128]{2,1,0:T(8,128)(2,1)S(1)}, bf16[4,176,128]{2,1,0:T(8,128)(2,1)S(1)}, u32[]{:S(2)}, u32[]{:S(2)}) %collective-permute-start.12) | collective-permute-done | bytes 180256 | tf_op jit(solution)/shard_map/ppermute | solution.py:677
  53.7 0.1 collective-permute-start.13
  53.8 1.6 %collective-permute-done.13 = bf16[1216,128]{1,0:T(8,128)(2,1)S(1)} collective-permute-done((bf16[1216,128]{1,0:T(8,128)(2,1)S(1)}, bf16[1216,128]{1,0:T(8,128)(2,1)S(1)}, u32[]{:S(2)}, u32[]{:S(2)}) %collective-permute-start.13) | collective-permute-done | bytes 311328 | tf_op jit(solution)/shard_map/ppermute | solution.py:677
  55.4 0.1 pad_maximum_fusion.pieces_ref
  55.5 1.6 %shard_map.150 = (f32[75,128]{1,0:T(8,128)}, f32[49,2,128]{2,1,0:T(2,128)}, f32[2,128]{1,0:T(2,128)}, f32[2,128,512]{2,1,0:T(8,128)}, f32[2,512,128]{2,1,0:T(8,128)}, /*index=5*/f32[2,128]{1,0:T(2,128)}) custom-call(s32[20]{0:T(128)S(1)} %fusion.order_ref, bf16[16,128,128]{2,1,0:T(8,128)(2,1)S(1)} %pad_maximum_fusion.pieces_ref, ...), custom_call_target="tpu_custom_call" | custom-call | tf_op jit(solution)/shard_map/pallas_call | solution.py:912
  (23 shorter events, 0.4 us)
Async XLA Ops:
  1.3 0.9 %copy-start.3 = (bf16[1,75,512]{2,1,0:T(8,128)(2,1)S(1)}, bf16[1,75,512]{2,1,0:T(8,128)(2,1)}, u32[]{:S(2)}) copy-start(bf16[1,75,512]{2,1,0:T(8,128)(2,1)} %param.9) | copy-start | bytes 230404
  2.2 3.9 %copy-start.5 = (f32[2,49,128]{2,0,1:T(2,128)S(1)}, f32[2,49,128]{2,0,1:T(2,128)}, u32[]{:S(2)}) copy-start(f32[2,49,128]{2,0,1:T(2,128)} %param.12) | copy-start | bytes 150532
  2.6 5.2 %collective-permute-start = (bf16[22,8,128]{2,1,0:T(8,128)(2,1)S(1)}, bf16[22,8,128]{2,1,0:T(8,128)(2,1)S(1)}, u32[]{:S(2)}, u32[]{:S(2)}) collective-permute-start(bf16[22,8,128]{2,1,0:T(8,128)(2,1)S(1)} %get-tuple-element.39), channel_id=1, source_target_pairs={{0,1},{1,2},{2,3},{3,4},{4,5},{5,6},{6,7},{7,0},{8,9},{9,10},{10,1... | collective-permute-start | bytes 135176 | tf_op jit(solution)/shard_map/ppermute | solution.py:677
  3.1 4.7 %collective-permute-start.1 = (bf16[22,8,128]{2,1,0:T(8,128)(2,1)S(1)}, bf16[22,8,128]{2,1,0:T(8,128)(2,1)S(1)}, u32[]{:S(2)}, u32[]{:S(2)}) collective-permute-start(bf16[22,8,128]{2,1,0:T(8,128)(2,1)S(1)} %get-tuple-element.40), channel_id=1, source_target_pairs={{0,7},{1,0},{2,1},{3,2},{4,3},{5,4},{6,5},{7,6},{8,15},{9,8},{10,9... | collective-permute-start | bytes 135176 | tf_op jit(solution)/shard_map/ppermute | solution.py:677
  6.1 0.7 %copy-start.7 = (f32[2,128]{1,0:T(2,128)S(1)}, f32[2,128]{1,0:T(2,128)}, u32[]{:S(2)}) copy-start(f32[2,128]{1,0:T(2,128)} %param.13) | copy-start | bytes 3076
  6.1 0.7 %copy-start.6 = (f32[2,128]{1,0:T(2,128)S(1)}, f32[2,128]{1,0:T(2,128)}, u32[]{:S(2)}) copy-start(f32[2,128]{1,0:T(2,128)} %param.16) | copy-start | bytes 3076
  6.8 5.1 %copy-start = (bf16[2,128,512]{2,1,0:T(8,128)(2,1)S(1)}, bf16[2,128,512]{2,1,0:T(8,128)(2,1)}, u32[]{:S(2)}) copy-start(bf16[2,128,512]{2,1,0:T(8,128)(2,1)} %win_ref.3) | copy-start | bytes 786436
  6.8 5.1 %copy-start.1 = (bf16[2,512,128]{2,1,0:T(8,128)(2,1)S(1)}, bf16[2,512,128]{2,1,0:T(8,128)(2,1)}, u32[]{:S(2)}) copy-start(bf16[2,512,128]{2,1,0:T(8,128)(2,1)} %wout_ref.3) | copy-start | bytes 786436
  8.0 4.0 %copy-start.4 = (bf16[75,128]{1,0:T(8,128)(2,1)S(1)}, bf16[75,128]{1,0:T(8,128)(2,1)}, u32[]{:S(2)}) copy-start(bf16[75,128]{1,0:T(8,128)(2,1)} %stem_ref.3) | copy-start | bytes 57604
  8.0 5.8 %collective-permute-start.2 = (bf16[192,128]{1,0:T(8,128)(2,1)S(1)}, bf16[192,128]{1,0:T(8,128)(2,1)S(1)}, u32[]{:S(2)}, u32[]{:S(2)}) collective-permute-start(bf16[192,128]{1,0:T(8,128)(2,1)S(1)} %broadcast_select_fusion.3), channel_id=1, source_target_pairs={{0,8},{1,9},{2,10},{3,11},{4,12},{5,13},{6,14},{7,15},{8,0},{9,1},... | collective-permute-start | bytes 147464 | tf_op jit(solution)/shard_map/ppermute | solution.py:677
  11.3 2.5 %collective-permute-start.3 = (bf16[192,128]{1,0:T(8,128)(2,1)S(1)}, bf16[192,128]{1,0:T(8,128)(2,1)S(1)}, u32[]{:S(2)}, u32[]{:S(2)}) collective-permute-start(bf16[192,128]{1,0:T(8,128)(2,1)S(1)} %get-tuple-element.44), channel_id=1, source_target_pairs={{8,15},{9,14},{10,13},{11,12},{12,11},{13,10},{14,9},{15,8},{24,31... | collective-permute-start | bytes 147464 | tf_op jit(solution)/shard_map/ppermute | solution.py:677
  13.7 0.9 %copy-start.2 = (bf16[1,512,128]{2,1,0:T(8,128)(2,1)S(1)}, bf16[1,512,128]{2,1,0:T(8,128)(2,1)}, u32[]{:S(2)}) copy-start(bf16[1,512,128]{2,1,0:T(8,128)(2,1)} %param.17) | copy-start | bytes 393220
  21.9 1.7 %collective-permute-start.4 = (bf16[1024,128]{1,0:T(8,128)(2,1)S(1)}, bf16[1024,128]{1,0:T(8,128)(2,1)S(1)}, u32[]{:S(2)}, u32[]{:S(2)}) collective-permute-start(bf16[1024,128]{1,0:T(8,128)(2,1)S(1)} %broadcast_select_fusion), channel_id=1, source_target_pairs={{0,1},{1,0},{2,3},{3,2},{4,5},{5,4},{6,7},{7,6},{8,9},{9,8},{10,11... | collective-permute-start | bytes 786440 | tf_op jit(solution)/shard_map/ppermute | solution.py:677
  23.7 7.9 %collective-permute-start.5 = (bf16[512,128]{1,0:T(8,128)(2,1)S(1)}, bf16[512,128]{1,0:T(8,128)(2,1)S(1)}, u32[]{:S(2)}, u32[]{:S(2)}) collective-permute-start(bf16[512,128]{1,0:T(8,128)(2,1)S(1)} %select_convert_fusion), channel_id=1, source_target_pairs={{0,2},{1,3},{2,0},{3,1},{4,6},{5,7},{6,4},{7,5},{8,10},{9,11},{10,... | collective-permute-start | bytes 393224 | tf_op jit(solution)/shard_map/ppermute | solution.py:677
  31.7 6.0 %collective-permute-start.6 = (bf16[176,128]{1,0:T(8,128)(2,1)S(1)}, bf16[176,128]{1,0:T(8,128)(2,1)S(1)}, u32[]{:S(2)}, u32[]{:S(2)}) collective-permute-start(bf16[176,128]{1,0:T(8,128)(2,1)S(1)} %pad_maximum_fusion.5), channel_id=1, source_target_pairs={{0,12},{1,13},{2,14},{3,15},{4,8},{5,9},{6,10},{7,11},{8,4},{9,5},... | collective-permute-start | bytes 135176 | tf_op jit(solution)/shard_map/ppermute | solution.py:677
  35.4 5.3 %collective-permute-start.7 = (bf16[176,128]{1,0:T(8,128)(2,1)S(1)}, bf16[176,128]{1,0:T(8,128)(2,1)S(1)}, u32[]{:S(2)}, u32[]{:S(2)}) collective-permute-start(bf16[176,128]{1,0:T(8,128)(2,1)S(1)} %pad_maximum_fusion.6), channel_id=1, source_target_pairs={{0,8},{1,9},{2,10},{3,11},{4,12},{5,13},{6,14},{7,15},{8,0},{9,1},... | collective-permute-start | bytes 135176 | tf_op jit(solution)/shard_map/ppermute | solution.py:677
  35.4 5.3 %collective-permute-start.8 = (bf16[176,128]{1,0:T(8,128)(2,1)S(1)}, bf16[176,128]{1,0:T(8,128)(2,1)S(1)}, u32[]{:S(2)}, u32[]{:S(2)}) collective-permute-start(bf16[176,128]{1,0:T(8,128)(2,1)S(1)} %pad_maximum_fusion.7), channel_id=1, source_target_pairs={{0,4},{1,5},{2,6},{3,7},{4,0},{5,1},{6,2},{7,3},{8,12},{9,13},{10,... | collective-permute-start | bytes 135176 | tf_op jit(solution)/shard_map/ppermute | solution.py:677
  40.7 5.9 %collective-permute-start.11 = (bf16[176,128]{1,0:T(8,128)(2,1)S(1)}, bf16[176,128]{1,0:T(8,128)(2,1)S(1)}, u32[]{:S(2)}, u32[]{:S(2)}) collective-permute-start(bf16[176,128]{1,0:T(8,128)(2,1)S(1)} %get-tuple-element.78), channel_id=1, source_target_pairs={{0,12},{1,13},{2,14},{3,15},{4,8},{5,9},{6,10},{7,11},{8,4},{9,5},... | collective-permute-start | bytes 135176 | tf_op jit(solution)/shard_map/ppermute | solution.py:677
  42.7 4.4 %collective-permute-start.9 = (bf16[176,128]{1,0:T(8,128)(2,1)S(1)}, bf16[176,128]{1,0:T(8,128)(2,1)S(1)}, u32[]{:S(2)}, u32[]{:S(2)}) collective-permute-start(bf16[176,128]{1,0:T(8,128)(2,1)S(1)} %get-tuple-element.78), channel_id=1, source_target_pairs={{0,4},{1,5},{2,6},{3,7},{4,0},{5,1},{6,2},{7,3},{8,12},{9,13},{10,... | collective-permute-start | bytes 135176 | tf_op jit(solution)/shard_map/ppermute | solution.py:677
  43.1 4.9 %collective-permute-start.10 = (bf16[176,128]{1,0:T(8,128)(2,1)S(1)}, bf16[176,128]{1,0:T(8,128)(2,1)S(1)}, u32[]{:S(2)}, u32[]{:S(2)}) collective-permute-start(bf16[176,128]{1,0:T(8,128)(2,1)S(1)} %get-tuple-element.78), channel_id=1, source_target_pairs={{0,8},{1,9},{2,10},{3,11},{4,12},{5,13},{6,14},{7,15},{8,0},{9,1},... | collective-permute-start | bytes 135176 | tf_op jit(solution)/shard_map/ppermute | solution.py:677
  48.0 5.6 %collective-permute-start.12 = (bf16[4,176,128]{2,1,0:T(8,128)(2,1)S(1)}, bf16[4,176,128]{2,1,0:T(8,128)(2,1)S(1)}, u32[]{:S(2)}, u32[]{:S(2)}) collective-permute-start(bf16[4,176,128]{2,1,0:T(8,128)(2,1)S(1)} %pad_maximum_fusion.3), channel_id=1, source_target_pairs={{0,2},{1,3},{2,0},{3,1},{4,6},{5,7},{6,4},{7,5},{8,10},{9,11},{10,... | collective-permute-start | bytes 540680 | tf_op jit(solution)/shard_map/ppermute | solution.py:677
  53.7 1.7 %collective-permute-start.13 = (bf16[1216,128]{1,0:T(8,128)(2,1)S(1)}, bf16[1216,128]{1,0:T(8,128)(2,1)S(1)}, u32[]{:S(2)}, u32[]{:S(2)}) collective-permute-start(bf16[1216,128]{1,0:T(8,128)(2,1)S(1)} %pad_maximum_fusion.1), channel_id=1, source_target_pairs={{0,1},{1,0},{2,3},{3,2},{4,5},{5,4},{6,7},{7,6},{8,9},{9,8},{10,11... | collective-permute-start | bytes 933896 | tf_op jit(solution)/shard_map/ppermute | solution.py:677
